TPU v7x, 256 devices: a whole 4x4x8 slice. The times are simulated.
256 devices in a mesh: corner: 16 (over y, x_lo, core), tm: 16 (over z, x_hi).
Axes of the slice: x: 4 (x_hi: 2, x_lo: 2; x = x_hi * 2 + x_lo), y: 4, z: 8, core: 2. Of those that a mesh axis runs over, the one named last changes fastest.
Arguments:
- signal: bfloat16 [16, 64, 65536], P('corner', None, 'tm'), may hold values from -6 to 6
- dilated_conv_weight: bfloat16 [2, 256, 128], replicated, may hold values from -0.5 to 0.5
- dilated_conv_bias: float32 [2, 256], replicated, may hold values from -3 to 3
- projection_weight: bfloat16 [2, 128, 128], replicated, may hold values from -0.5 to 0.5
- projection_bias: float32 [2, 128], replicated, may hold values from -3 to 3
- cot_top: bfloat16 [16, 64, 65536], P('corner', None, 'tm'), may hold values from -6 to 6
- cot_skip: bfloat16 [16, 64, 65536], P('corner', None, 'tm'), may hold values from -6 to 6
Outputs:
- x_top: bfloat16 [16, 64, 65536], P('corner', None, 'tm')
- skip_sum: bfloat16 [16, 64, 65536], P('corner', None, 'tm')
- grad_input: bfloat16 [16, 64, 65536], P('corner', None, 'tm')
- grad_conv: float32 [2, 256, 128], replicated
- grad_conv_bias: float32 [2, 256], replicated
- grad_out: float32 [2, 128, 128], replicated
- grad_out_bias: float32 [2, 128], replicated
All inputs are finite; a program needn't handle non-finite values.
Results may differ from a plain program's by a relative error of at most 0.0065.
Values may be sent and summed in bfloat16 or wider, within the bound.
No kernel may reach another device: no remote copies, remote signals or barrier semaphores. Data moves between devices by JAX's collectives and lax.ppermute only.
A program may use at most 64 MiB of HBM per device.

v0:
```python
import math

import jax
import jax.numpy as jnp
from jax import lax
from jax.sharding import PartitionSpec as P


def from_behind(block, axis, distance):
    devices = range(lax.axis_size(axis))
    route = [(i - distance, i) for i in devices if i - distance in devices]
    return lax.ppermute(block, axis, route)


def gated_layer_forward(a_in, tap_in, weight, bias, proj, proj_bias, gsize, rsize):
    stacked = jnp.concatenate([tap_in, a_in], axis=1)
    pre_act = (
        jnp.einsum("oc,bct->bot", weight, stacked, preferred_element_type=jnp.float32)
        + bias[None, :, None]
    )
    gate_out = (jnp.tanh(pre_act[:, :gsize]) * jax.nn.sigmoid(pre_act[:, gsize:])).astype(
        jnp.bfloat16
    )
    mixed = (
        jnp.einsum("og,bgt->bot", proj, gate_out, preferred_element_type=jnp.float32)
        + proj_bias[None, :, None]
    )
    next_act = (a_in.astype(jnp.float32) + mixed[:, :rsize]).astype(jnp.bfloat16)
    return (stacked, pre_act, gate_out, next_act, mixed[:, rsize:])


def layer_backward(go_res, go_skip, stacked, pre_act, gate_out, weight, proj, gsize, rsize):
    upper = jnp.concatenate([go_res, go_skip], axis=1)
    grad_proj = jnp.einsum("bot,bgt->og", upper, gate_out, preferred_element_type=jnp.float32)
    grad_pbias = jnp.sum(upper, axis=(0, 2), dtype=jnp.float32)
    grad_gate = jnp.einsum("og,bot->bgt", proj, upper, preferred_element_type=jnp.float32)
    filt_act = jnp.tanh(pre_act[:, :gsize])
    gate_act = jax.nn.sigmoid(pre_act[:, gsize:])
    grad_pre = jnp.concatenate(
        [
            grad_gate * gate_act * (1.0 - filt_act * filt_act),
            grad_gate * filt_act * gate_act * (1.0 - gate_act),
        ],
        axis=1,
    ).astype(jnp.bfloat16)
    grad_weight = jnp.einsum("bot,bct->oc", grad_pre, stacked, preferred_element_type=jnp.float32)
    grad_bias = jnp.sum(grad_pre, axis=(0, 2), dtype=jnp.float32)
    grad_in = jnp.einsum("oc,bot->bct", weight, grad_pre, preferred_element_type=jnp.float32)
    return (
        grad_in[:, :rsize].astype(jnp.bfloat16),
        grad_in[:, rsize:],
        (grad_weight, grad_bias, grad_proj, grad_pbias),
    )


def on_device(
    signal,
    dilated_conv_weight,
    dilated_conv_bias,
    projection_weight,
    projection_bias,
    cot_top,
    cot_skip,
):
    rsize = signal.shape[1]
    gsize = projection_weight.shape[2]
    tap_near = from_behind(signal, "tm", 1)
    (
        lower_saved_state,
        lower_preactivation,
        lower_gated_output,
        middle_layer_input,
        lower_skip_output,
    ) = gated_layer_forward(
        signal,
        tap_near,
        dilated_conv_weight[0],
        dilated_conv_bias[0],
        projection_weight[0],
        projection_bias[0],
        gsize,
        rsize,
    )
    tap_far = from_behind(middle_layer_input, "tm", 2)
    (
        upper_saved_state,
        upper_preactivation,
        upper_gated_output,
        upper_layer_output,
        upper_skip_output,
    ) = gated_layer_forward(
        middle_layer_input,
        tap_far,
        dilated_conv_weight[1],
        dilated_conv_bias[1],
        projection_weight[1],
        projection_bias[1],
        gsize,
        rsize,
    )
    skip_out = (lower_skip_output + upper_skip_output).astype(jnp.bfloat16)
    delayed_gradient_upper, current_gradient_upper, grads_top = layer_backward(
        cot_top,
        cot_skip,
        upper_saved_state,
        upper_preactivation,
        upper_gated_output,
        dilated_conv_weight[1],
        projection_weight[1],
        gsize,
        rsize,
    )
    later_top = from_behind(delayed_gradient_upper, "tm", -2)
    middle_input_gradient = (
        cot_top.astype(jnp.float32) + current_gradient_upper + later_top.astype(jnp.float32)
    ).astype(jnp.bfloat16)
    delayed_gradient_lower, current_gradient_lower, grads_low = layer_backward(
        middle_input_gradient,
        cot_skip,
        lower_saved_state,
        lower_preactivation,
        lower_gated_output,
        dilated_conv_weight[0],
        projection_weight[0],
        gsize,
        rsize,
    )
    later_low = from_behind(delayed_gradient_lower, "tm", -1)
    lower_input_gradient = (
        middle_input_gradient.astype(jnp.float32)
        + current_gradient_lower
        + later_low.astype(jnp.float32)
    ).astype(jnp.bfloat16)
    summed = lax.psum(
        (
            jnp.stack([grads_low[0], grads_top[0]]),
            jnp.stack([grads_low[1], grads_top[1]]),
            jnp.stack([grads_low[2], grads_top[2]]),
            jnp.stack([grads_low[3], grads_top[3]]),
        ),
        ("corner", "tm"),
    )
    count = signal.shape[0] * lax.axis_size("corner") * signal.shape[2] * lax.axis_size("tm")
    scale = 1.0 / math.sqrt(count)
    return (
        upper_layer_output,
        skip_out,
        lower_input_gradient,
        summed[0] * scale,
        summed[1] * scale,
        summed[2] * scale,
        summed[3] * scale,
    )


def solution(mesh):
    return jax.shard_map(
        on_device,
        mesh=mesh,
        in_specs=(
            P("corner", None, "tm"),
            P(),
            P(),
            P(),
            P(),
            P("corner", None, "tm"),
            P("corner", None, "tm"),
        ),
        out_specs=(
            P("corner", None, "tm"),
            P("corner", None, "tm"),
            P("corner", None, "tm"),
            P(),
            P(),
            P(),
            P(),
        ),
        check_vma=False,
    )
```

profile of v0, /device:TPU:1, one launch (start us, length us, event | category | flops | bytes accessed | tf_op | source)
XLA Modules:
  0.0 411.1 jit_solution(4979422311224916654)
XLA Ops:
  7.2 0.0 all-reduce.4.cloned.1.call-start
  7.2 5.5 %collective-permute-start = (bf16[1,64,4096]{2,1,0:T(8,128)(2,1)}, bf16[1,64,4096]{2,1,0:T(8,128)(2,1)S(1)}, u32[]{:S(2)}, u32[]{:S(2)}) collective-permute-start(bf16[1,64,4096]{2,1,0:T(8,128)(2,1)} %param.7), channel_id=1, source_target_pairs={{0,1},{1,2},{2,3},{3,4},{4,5},{5,6},{6,7},{7,8},{8,9},{9,10},{10,1... | collective-permute-start | bytes 1572872 | tf_op jit(solution)/shard_map/ppermute | solution.py:12
  12.7 0.8 fusion.55
  13.5 0.8 slice_bitcast_fusion
  14.2 1.1 constant_dynamic-update-slice_fusion.1
  15.3 8.3 %collective-permute-done = bf16[1,64,4096]{2,1,0:T(8,128)(2,1)S(1)} collective-permute-done((bf16[1,64,4096]{2,1,0:T(8,128)(2,1)}, bf16[1,64,4096]{2,1,0:T(8,128)(2,1)S(1)}, u32[]{:S(2)}, u32[]{:S(2)}) %collective-permute-start) | collective-permute-done | bytes 524320 | tf_op jit(solution)/shard_map/ppermute | solution.py:12
  23.6 2.0 fusion.1
  25.6 0.8 fusion.18
  26.4 0.0 copy-start.6
  26.4 0.0 copy-start.5
  26.4 0.4 fusion.5
  26.9 0.6 copy-done.6
  27.5 0.1 fusion.26
  27.6 5.3 %collective-permute-start.1 = (bf16[1,64,4096]{2,1,0:T(8,128)(2,1)S(1)}, bf16[1,64,4096]{2,1,0:T(8,128)(2,1)S(1)}, u32[]{:S(2)}, u32[]{:S(2)}) collective-permute-start(bf16[1,64,4096]{2,1,0:T(8,128)(2,1)S(1)} %fusion.26), channel_id=1, source_target_pairs={{0,2},{1,3},{2,4},{3,5},{4,6},{5,7},{6,8},{7,9},{8,10},{9,11},{10,... | collective-permute-start | bytes 1572872 | tf_op jit(solution)/shard_map/ppermute | solution.py:12
  33.0 0.2 convert_reduce_fusion.2
  33.2 9.3 %collective-permute-done.1 = bf16[1,64,4096]{2,1,0:T(8,128)(2,1)S(1)} collective-permute-done((bf16[1,64,4096]{2,1,0:T(8,128)(2,1)S(1)}, bf16[1,64,4096]{2,1,0:T(8,128)(2,1)S(1)}, u32[]{:S(2)}, u32[]{:S(2)}) %collective-permute-start.1) | collective-permute-done | bytes 524320 | tf_op jit(solution)/shard_map/ppermute | solution.py:12
  42.5 0.7 fusion.3
  43.3 1.5 multiply_convert_fusion.3
  44.8 0.5 convolution_bitcast_fusion.6
  45.3 0.1 slice.203
  45.3 1.3 collective-permute-start.2
  46.6 0.4 fusion.7
  47.0 1.2 fusion.24
  48.3 0.4 convert_reduce_fusion
  48.6 0.7 fusion.16
  49.3 0.0 copy-start.4
  49.3 0.4 convolution_bitcast_fusion.8
  49.8 9.4 %collective-permute-done.2 = bf16[1,64,4096]{2,1,0:T(8,128)(2,1)S(1)} collective-permute-done((bf16[1,64,4096]{2,1,0:T(8,128)(2,1)S(1)}, bf16[1,64,4096]{2,1,0:T(8,128)(2,1)S(1)}, u32[]{:S(2)}, u32[]{:S(2)}) %collective-permute-start.2) | collective-permute-done | bytes 524320 | tf_op jit(solution)/shard_map/ppermute | solution.py:12
  59.2 0.2 fusion.23
  59.3 1.3 multiply_convert_fusion.1
  60.7 0.2 convert_reduce_fusion.3
  60.9 0.4 convolution_bitcast_fusion.9
  61.4 0.4 convert_reduce_fusion.1
  61.8 0.2 copy-done.2
  62.0 82.7 %all-reduce = (f32[2,256]{1,0:T(2,128)S(1)}, f32[2,128]{1,0:T(2,128)S(1)}) all-reduce(f32[2,256]{1,0:T(2,128)S(1)} %pad_maximum_fusion.15, f32[2,128]{1,0:T(2,128)S(1)} %pad_maximum_fusion.16), channel_id=1, replica_groups=mesh['corner'=16,'tm'=16] {'corner','tm'}, use_global_device_ids=true, to_apply=%region_3.0 | all-reduce | flops 768 | bytes 6144 | tf_op jit(solution)/shard_map/psum | solution.py:134
  144.7 0.6 broadcast_multiply_fusion.2
  145.3 2.2 convolution_bitcast_fusion.4
  147.5 0.8 slice.202
  148.3 1.3 collective-permute-start.3
  149.6 0.7 pad_maximum_fusion.14
  150.3 0.7 fusion.17
  151.0 0.7 pad_maximum_fusion.13
  151.7 0.0 all-reduce.4.cloned.1.call-update
  151.7 0.6 broadcast_multiply_fusion.3
  152.3 246.7 %all-reduce.4.cloned.1.call-done = (f32[2,256,128]{2,1,0:T(8,128)}, f32[2,128,128]{2,1,0:T(8,128)}) async-done(((f32[2,256,128]{2,1,0:T(8,128)}, f32[2,128,128]{2,1,0:T(8,128)}), (f32[2,256,128]{2,1,0:T(8,128)}, f32[2,128,128]{2,1,0:T(8,128)})) %all-reduce.4.cloned.1.call-update) | async-done | bytes 393232 | tf_op jit(solution)/shard_map/psum | solution.py:134
  399.0 1.6 broadcast_multiply_fusion.1
  400.6 1.7 broadcast_multiply_fusion
  402.2 2.0 fusion.21
  (21 shorter events, 0.1 us)
Async XLA Ops:
  7.2 391.8 %all-reduce.4.cloned.1.call-start = ((), (), s32[]{:S(2)}) async-start(), calls=%async_computation | async-start | bytes 786432 | tf_op jit(solution)/shard_map/psum | solution.py:134
  7.2 16.4 %collective-permute-start = (bf16[1,64,4096]{2,1,0:T(8,128)(2,1)}, bf16[1,64,4096]{2,1,0:T(8,128)(2,1)S(1)}, u32[]{:S(2)}, u32[]{:S(2)}) collective-permute-start(bf16[1,64,4096]{2,1,0:T(8,128)(2,1)} %param.7), channel_id=1, source_target_pairs={{0,1},{1,2},{2,3},{3,4},{4,5},{5,6},{6,7},{7,8},{8,9},{9,10},{10,1... | collective-permute-start | bytes 1572872 | tf_op jit(solution)/shard_map/ppermute | solution.py:12
  23.6 2.0 copy-start.8
  25.6 0.9 copy-start.10
  26.4 1.0 copy-start.6
  26.4 6.5 %copy-start.5 = (bf16[1,64,4096]{2,1,0:T(8,128)(2,1)S(1)}, bf16[1,64,4096]{2,1,0:T(8,128)(2,1)}, u32[]{:S(2)}) copy-start(bf16[1,64,4096]{2,1,0:T(8,128)(2,1)} %param.13) | copy-start | bytes 1572868
  27.5 15.1 %copy-start.7 = (bf16[2,256,128]{2,1,0:T(8,128)(2,1)S(1)}, bf16[2,256,128]{2,1,0:T(8,128)(2,1)}, u32[]{:S(2)}) copy-start(bf16[2,256,128]{2,1,0:T(8,128)(2,1)} %param.8) | copy-start | bytes 393220
  27.6 15.0 %collective-permute-start.1 = (bf16[1,64,4096]{2,1,0:T(8,128)(2,1)S(1)}, bf16[1,64,4096]{2,1,0:T(8,128)(2,1)S(1)}, u32[]{:S(2)}, u32[]{:S(2)}) collective-permute-start(bf16[1,64,4096]{2,1,0:T(8,128)(2,1)S(1)} %fusion.26), channel_id=1, source_target_pairs={{0,2},{1,3},{2,4},{3,5},{4,6},{5,7},{6,8},{7,9},{8,10},{9,11},{10,... | collective-permute-start | bytes 1572872 | tf_op jit(solution)/shard_map/ppermute | solution.py:12
  45.3 13.9 %collective-permute-start.2 = (bf16[1,64,4096]{2,1,0:T(8,128)(2,1)S(1)}, bf16[1,64,4096]{2,1,0:T(8,128)(2,1)S(1)}, u32[]{:S(2)}, u32[]{:S(2)}) collective-permute-start(bf16[1,64,4096]{2,1,0:T(8,128)(2,1)S(1)} %slice.203), channel_id=1, source_target_pairs={{2,0},{3,1},{4,2},{5,3},{6,4},{7,5},{8,6},{9,7},{10,8},{11,9},{12,... | collective-permute-start | bytes 1572872 | tf_op jit(solution)/shard_map/ppermute | solution.py:12
  49.3 9.8 %copy-start.4 = (bf16[1,64,4096]{2,1,0:T(8,128)(2,1)S(1)}, bf16[1,64,4096]{2,1,0:T(8,128)(2,1)}, u32[]{:S(2)}) copy-start(bf16[1,64,4096]{2,1,0:T(8,128)(2,1)} %param.12) | copy-start | bytes 1572868
  60.7 1.1 copy-start
  60.7 1.3 copy-start.2
  145.3 5.0 %copy-start.1 = (bf16[1,128,4096]{2,1,0:T(8,128)(2,1)S(1)}, bf16[1,128,4096]{2,1,0:T(8,128)(2,1)}, u32[]{:S(2)}) copy-start(bf16[1,128,4096]{2,1,0:T(8,128)(2,1)} %copy-done) | copy-start | bytes 3145732
  145.3 5.0 %copy-start.3 = (bf16[1,128,4096]{2,1,0:T(8,128)(2,1)S(1)}, bf16[1,128,4096]{2,1,0:T(8,128)(2,1)}, u32[]{:S(2)}) copy-start(bf16[1,128,4096]{2,1,0:T(8,128)(2,1)} %copy-done.2) | copy-start | bytes 3145732
  145.3 5.0 %copy-start.9 = (bf16[1,64,4096]{2,1,0:T(8,128)(2,1)S(1)}, bf16[1,64,4096]{2,1,0:T(8,128)(2,1)}, u32[]{:S(2)}) copy-start(bf16[1,64,4096]{2,1,0:T(8,128)(2,1)} %copy-done.8) | copy-start | bytes 1572868
  148.3 253.9 %collective-permute-start.3 = (bf16[1,64,4096]{2,1,0:T(8,128)(2,1)}, bf16[1,64,4096]{2,1,0:T(8,128)(2,1)}, u32[]{:S(2)}, u32[]{:S(2)}) collective-permute-start(bf16[1,64,4096]{2,1,0:T(8,128)(2,1)} %slice.202), channel_id=1, source_target_pairs={{1,0},{2,1},{3,2},{4,3},{5,4},{6,5},{7,6},{8,7},{9,8},{10,9},{11,1... | collective-permute-start | bytes 1572872 | tf_op jit(solution)/shard_map/ppermute | solution.py:12
Sparse Core Ops, SparseCore 0:
  151.9 247.0 all-reduce.3
where the time goes:
time: 412 us; the launch traced here: 411 us
  waiting for transfers between devices  274 us (67%)
  blocking collectives  82.7 us (20%)
  between operations  14.3 us (3%)
  starting transfers between devices  13.5 us (3%)
  matrix products  11.3 us (3%)
  other arithmetic  11.3 us (3%)
  local copies, waits for them, and re-layouts  4.41 us (1%)
    psum x1, waiting for transfers between devices, on_device(): lax.psum((jnp.stack([grads_low[0], grads_top[0]]), jnp.stack([grads_low[1...  247 us
    psum x1, blocking collectives, on_device(): lax.psum((jnp.stack([grads_low[0], grads_top[0]]), jnp.stack([grads_low[1...  82.7 us
    ppermute x4, waiting for transfers between devices, from_behind(): return lax.ppermute(block, axis, route)  27 us
    ppermute x4, starting transfers between devices, from_behind(): return lax.ppermute(block, axis, route)  13.4 us
  transfers between devices with their start and end apart: 5, of which 4 were waited for; matrix products, arithmetic and copies ran while one was open for 3% of the time, Pallas kernels for 0%

commit v1 on v0

--- a/solution.py
+++ b/solution.py
@@ -3,13 +3,43 @@
 import jax
 import jax.numpy as jnp
 from jax import lax
-from jax.sharding import PartitionSpec as P
+from jax.sharding import Mesh, PartitionSpec as P
+
+CORNER = ("y", "xl", "core")
+TM = ("z", "xh")
+CHIPS = ("y", "xl", "z", "xh")
 
 
 def from_behind(block, axis, distance):
     devices = range(lax.axis_size(axis))
     route = [(i - distance, i) for i in devices if i - distance in devices]
     return lax.ppermute(block, axis, route)
+
+
+def swap_cores(block):
+    return lax.ppermute(block, "core", [(0, 1), (1, 0)])
+
+
+def pack_layer(grads):
+    weight, bias, proj, proj_bias = grads
+    rows = jnp.concatenate(
+        [weight, proj, bias.reshape(-1, 128), proj_bias.reshape(-1, 128)], axis=0
+    )
+    chips = lax.axis_size(CHIPS)
+    each = -(-rows.shape[0] // (4 * chips)) * 4
+    return jnp.pad(rows, ((0, each * chips - rows.shape[0]), (0, 0)))
+
+
+def unpack_layer(rows):
+    return rows[:256], rows[384:386].reshape(256), rows[256:384], rows[386]
+
+
+def reduce_over_chips(rows):
+    chips = lax.axis_size(CHIPS)
+    parts = rows.reshape(chips, -1, 128)
+    share = jnp.sum(lax.all_to_all(parts, CHIPS, 0, 0, tiled=True), axis=0, keepdims=True)
+    whole = lax.all_to_all(jnp.broadcast_to(share, parts.shape), CHIPS, 0, 0, tiled=True)
+    return whole.reshape(rows.shape)
 
 
 def gated_layer_forward(a_in, tap_in, weight, bias, proj, proj_bias, gsize, rsize):
@@ -64,7 +94,7 @@
 ):
     rsize = signal.shape[1]
     gsize = projection_weight.shape[2]
-    tap_near = from_behind(signal, "tm", 1)
+    tap_near = from_behind(signal, TM, 1)
     (
         lower_saved_state,
         lower_preactivation,
@@ -81,7 +111,7 @@
         gsize,
         rsize,
     )
-    tap_far = from_behind(middle_layer_input, "tm", 2)
+    tap_far = from_behind(middle_layer_input, TM, 2)
     (
         upper_saved_state,
         upper_preactivation,
@@ -110,7 +140,7 @@
         gsize,
         rsize,
     )
-    later_top = from_behind(delayed_gradient_upper, "tm", -2)
+    later_top = from_behind(delayed_gradient_upper, TM, -2)
     middle_input_gradient = (
         cot_top.astype(jnp.float32) + current_gradient_upper + later_top.astype(jnp.float32)
     ).astype(jnp.bfloat16)
@@ -125,55 +155,31 @@
         gsize,
         rsize,
     )
-    later_low = from_behind(delayed_gradient_lower, "tm", -1)
+    later_low = from_behind(delayed_gradient_lower, TM, -1)
     lower_input_gradient = (
         middle_input_gradient.astype(jnp.float32)
         + current_gradient_lower
         + later_low.astype(jnp.float32)
     ).astype(jnp.bfloat16)
-    summed = lax.psum(
-        (
-            jnp.stack([grads_low[0], grads_top[0]]),
-            jnp.stack([grads_low[1], grads_top[1]]),
-            jnp.stack([grads_low[2], grads_top[2]]),
-            jnp.stack([grads_low[3], grads_top[3]]),
-        ),
-        ("corner", "tm"),
-    )
-    count = signal.shape[0] * lax.axis_size("corner") * signal.shape[2] * lax.axis_size("tm")
+    low, top = pack_layer(grads_low), pack_layer(grads_top)
+    mine = lax.axis_index("core") == 0
+    held = jnp.where(mine, low, top) + swap_cores(jnp.where(mine, top, low))
+    held = reduce_over_chips(held)
+    other = swap_cores(held)
+    count = signal.shape[0] * lax.axis_size(CORNER) * signal.shape[2] * lax.axis_size(TM)
     scale = 1.0 / math.sqrt(count)
-    return (
-        upper_layer_output,
-        skip_out,
-        lower_input_gradient,
-        summed[0] * scale,
-        summed[1] * scale,
-        summed[2] * scale,
-        summed[3] * scale,
-    )
+    low, top = jnp.where(mine, held, other), jnp.where(mine, other, held)
+    grads = [jnp.stack(pair) * scale for pair in zip(unpack_layer(low), unpack_layer(top))]
+    return (upper_layer_output, skip_out, lower_input_gradient, *grads)
 
 
 def solution(mesh):
+    fine = Mesh(mesh.devices.reshape(4, 2, 2, 8, 2), ("y", "xl", "core", "z", "xh"))
+    field = P(CORNER, None, TM)
     return jax.shard_map(
         on_device,
-        mesh=mesh,
-        in_specs=(
-            P("corner", None, "tm"),
-            P(),
-            P(),
-            P(),
-            P(),
-            P("corner", None, "tm"),
-            P("corner", None, "tm"),
-        ),
-        out_specs=(
-            P("corner", None, "tm"),
-            P("corner", None, "tm"),
-            P("corner", None, "tm"),
-            P(),
-            P(),
-            P(),
-            P(),
-        ),
+        mesh=fine,
+        in_specs=(field, P(), P(), P(), P(), field, field),
+        out_specs=(field, field, field, P(), P(), P(), P()),
         check_vma=False,
     )

time: 412 us -> 122 us (0.30)
  waiting for transfers between devices: 274 us -> 44.4 us
  blocking collectives: 82.7 us -> 0 us
  starting transfers between devices: 13.5 us -> 45.5 us
  between operations: 14.3 us -> 0.99 us
    psum x1 -> x0, waiting for transfers between devices: 247 us -> none  [on_device(): lax.psum((jnp.stack([grads_low[0], grads_top[0]]), jnp.stack([grads_low[1...]
    psum x1 -> x0, blocking collectives: 82.7 us -> none  [on_device(): lax.psum((jnp.stack([grads_low[0], grads_top[0]]), jnp.stack([grads_low[1...]
    all_to_all x0 -> x2, starting transfers between devices: none -> 25.7 us  [the longest x1 16.2 us: reduce_over_chips(): lax.all_to_all(parts, CHIPS, 0, 0, tiled=True)]
    all_to_all x0 -> x2, waiting for transfers between devices: none -> 14.6 us  [the longest x1 9.27 us: reduce_over_chips(): lax.all_to_all(jnp.broadcast_to(share, parts.shape), CHIPS, 0, 0, tiled=T...]
    ppermute x0 -> x2, starting transfers between devices: none -> 6.4 us  [swap_cores(): return lax.ppermute(block, 'core', [(0, 1), (1, 0)])]
  transfers between devices with their start and end apart: 5 -> 8, of which waited for: 4 -> 6; matrix products, arithmetic and copies ran while one was open for 3% -> 12% of each run, Pallas kernels for 0% -> 0%
where the time goes in v1:
time: 122 us; the launch traced here: 121 us
  starting transfers between devices  45.5 us (37%)
  waiting for transfers between devices  44.4 us (36%)
  matrix products  12.3 us (10%)
  other arithmetic  10.8 us (9%)
  local copies, waits for them, and re-layouts  6.97 us (6%)
    ppermute x4, waiting for transfers between devices, from_behind(): return lax.ppermute(block, axis, route)  28.6 us
    all_to_all x1, starting transfers between devices, reduce_over_chips(): lax.all_to_all(parts, CHIPS, 0, 0, tiled=True)  16.2 us
    ppermute x4, starting transfers between devices, from_behind(): return lax.ppermute(block, axis, route)  13.4 us
    all_to_all x1, starting transfers between devices, reduce_over_chips(): lax.all_to_all(jnp.broadcast_to(share, parts.shape), CHIPS, 0, 0, tiled=T...  9.48 us
    all_to_all x1, waiting for transfers between devices, reduce_over_chips(): lax.all_to_all(jnp.broadcast_to(share, parts.shape), CHIPS, 0, 0, tiled=T...  9.27 us
    ppermute x2, starting transfers between devices, swap_cores(): return lax.ppermute(block, 'core', [(0, 1), (1, 0)])  6.4 us
    all_to_all x1, waiting for transfers between devices, reduce_over_chips(): lax.all_to_all(parts, CHIPS, 0, 0, tiled=True)  5.31 us
    unnamed x27, local copies, waits for them, and re-layouts  3.74 us
  transfers between devices with their start and end apart: 8, of which 6 were waited for; matrix products, arithmetic and copies ran while one was open for 12% of the time, Pallas kernels for 0%

profile of v1, /device:TPU:1, one launch (start us, length us, event | category | flops | bytes accessed | tf_op | source)
XLA Modules:
  0.0 121.0 jit_solution(16010411599410869081)
XLA Ops:
  0.6 5.5 %collective-permute-start = (bf16[1,64,4096]{2,1,0:T(8,128)(2,1)}, bf16[1,64,4096]{2,1,0:T(8,128)(2,1)S(1)}, u32[]{:S(2)}, u32[]{:S(2)}) collective-permute-start(bf16[1,64,4096]{2,1,0:T(8,128)(2,1)} %param.7), channel_id=1, source_target_pairs={{0,1},{1,2},{2,3},{3,4},{4,5},{5,6},{6,7},{7,8},{8,9},{9,10},{10,1... | collective-permute-start | bytes 1572872 | tf_op jit(solution)/shard_map/ppermute | solution.py:16
  6.2 0.8 fusion.55
  6.9 0.8 slice_bitcast_fusion.4
  7.7 1.1 constant_dynamic-update-slice_fusion.1
  8.8 8.3 %collective-permute-done = bf16[1,64,4096]{2,1,0:T(8,128)(2,1)S(1)} collective-permute-done((bf16[1,64,4096]{2,1,0:T(8,128)(2,1)}, bf16[1,64,4096]{2,1,0:T(8,128)(2,1)S(1)}, u32[]{:S(2)}, u32[]{:S(2)}) %collective-permute-start) | collective-permute-done | bytes 524320 | tf_op jit(solution)/shard_map/ppermute | solution.py:16
  17.0 2.0 %fusion.1 = f32[1,256,4096]{2,1,0:T(8,128)S(1)} fusion(f32[256]{0:T(256)S(1)} %bitcast.150, bf16[1,64,4096]{2,1,0:T(8,128)(2,1)} %param.7, bf16[1,64,4096]{2,1,0:T(8,128)(2,1)S(1)} %collective-permute-done, bf16[2,256,128]{2,1,0:T(8,128)(2,1)} %param.8), kind=kOutput, calls=%fused_computation.3 | convolution fusion | flops 271581184 | bytes 5309440 | tf_op jit(solution)/shard_map/oc,bct->bot/dot_general | solution.py:48
  19.0 0.8 fusion.16
  19.9 0.4 fusion.5
  20.3 0.6 copy-done.8
  21.0 5.3 %collective-permute-start.1 = (bf16[1,64,4096]{2,1,0:T(8,128)(2,1)S(1)}, bf16[1,64,4096]{2,1,0:T(8,128)(2,1)S(1)}, u32[]{:S(2)}, u32[]{:S(2)}) collective-permute-start(bf16[1,64,4096]{2,1,0:T(8,128)(2,1)S(1)} %fusion.24), channel_id=1, source_target_pairs={{0,2},{1,3},{2,4},{3,5},{4,6},{5,7},{6,8},{7,9},{8,10},{9,11},{10,... | collective-permute-start | bytes 1572872 | tf_op jit(solution)/shard_map/ppermute | solution.py:16
  26.4 0.2 convert_reduce_fusion.2
  26.6 9.3 %collective-permute-done.1 = bf16[1,64,4096]{2,1,0:T(8,128)(2,1)S(1)} collective-permute-done((bf16[1,64,4096]{2,1,0:T(8,128)(2,1)S(1)}, bf16[1,64,4096]{2,1,0:T(8,128)(2,1)S(1)}, u32[]{:S(2)}, u32[]{:S(2)}) %collective-permute-start.1) | collective-permute-done | bytes 524320 | tf_op jit(solution)/shard_map/ppermute | solution.py:16
  36.0 0.7 fusion.3
  36.7 1.5 %multiply_convert_fusion.3 = (bf16[1,128,4096]{2,1,0:T(8,128)(2,1)S(1)}, bf16[1,128,4096]{2,1,0:T(8,128)(2,1)S(1)}, bf16[128,4096]{1,0:T(8,128)(2,1)S(1)}) fusion(f32[1,256,4096]{2,1,0:T(8,128)S(1)} %fusion.3, bf16[2,128,128]{2,1,0:T(8,128)(2,1)S(1)} %copy-done.12, bf16[1,128,4096]{2,1,0:T(8,128)(2,1)S(1)} %constant_dynamic-update-slice_fusion), kind=kOutput, calls=%fused_computation.35 | convolution fusion | flops 142082048 | bytes 8421376 | tf_op jit(solution)/shard_map/og,bot->bgt/dot_general | solution.py:66
  38.2 0.5 convolution_bitcast_fusion.6
  38.7 1.3 %collective-permute-start.2 = (bf16[1,64,4096]{2,1,0:T(8,128)(2,1)S(1)}, bf16[1,64,4096]{2,1,0:T(8,128)(2,1)S(1)}, u32[]{:S(2)}, u32[]{:S(2)}) collective-permute-start(bf16[1,64,4096]{2,1,0:T(8,128)(2,1)S(1)} %slice.247), channel_id=1, source_target_pairs={{2,0},{3,1},{4,2},{5,3},{6,4},{7,5},{8,6},{9,7},{10,8},{11,9},{12,... | collective-permute-start | bytes 1572872 | tf_op jit(solution)/shard_map/ppermute | solution.py:16
  40.0 0.4 convert_reduce_fusion
  40.4 0.7 fusion.15
  41.1 0.4 fusion.28
  41.6 11.0 %collective-permute-done.2 = bf16[1,64,4096]{2,1,0:T(8,128)(2,1)S(1)} collective-permute-done((bf16[1,64,4096]{2,1,0:T(8,128)(2,1)S(1)}, bf16[1,64,4096]{2,1,0:T(8,128)(2,1)S(1)}, u32[]{:S(2)}, u32[]{:S(2)}) %collective-permute-start.2) | collective-permute-done | bytes 524320 | tf_op jit(solution)/shard_map/ppermute | solution.py:16
  52.6 0.2 fusion.21
  52.8 1.3 %multiply_convert_fusion.1 = (bf16[1,128,4096]{2,1,0:T(8,128)(2,1)S(1)}, bf16[1,128,4096]{2,1,0:T(8,128)(2,1)S(1)}) fusion(f32[1,256,4096]{2,1,0:T(8,128)S(1)} %fusion.1, bf16[2,128,128]{2,1,0:T(8,128)(2,1)S(1)} %copy-done.12, bf16[1,64,4096]{2,1,0:T(8,128)(2,1)S(1)} %copy-done.7, bf16[1,64,4096]{2,1,0:T(8,128)(2,1)S(1)} %fusion.21), kind=kOutput, calls=%fused_computation.33 | convolution fusion | flops 143130624 | bytes 7372800 | tf_op jit(solution)/shard_map/og,bot->bgt/dot_general | solution.py:66
  54.1 0.4 fusion.25
  54.6 0.2 convert_reduce_fusion.3
  54.8 0.4 convert_reduce_fusion.1
  55.2 0.3 copy-done.4
  55.5 0.4 copy-done.11
  55.9 0.7 fusion.14
  56.6 3.2 %collective-permute-start.4 = (f32[512,128]{1,0:T(8,128)S(1)}, f32[512,128]{1,0:T(8,128)S(1)}, u32[]{:S(2)}, u32[]{:S(2)}) collective-permute-start(f32[512,128]{1,0:T(8,128)S(1)} %broadcast_select_fusion.2), channel_id=1, source_target_pairs={{0,16},{16,0},{1,17},{17,1},{2,18},{18,2},{3,19},{19,3},{4,20},{20... | collective-permute-start | bytes 786440 | tf_op jit(solution)/shard_map/ppermute | solution.py:20
  59.8 1.2 collective-permute-done.4
  61.0 0.7 select_add_fusion
  61.7 16.2 %all-to-all-start = ((f32[128,4,128]{2,1,0:T(4,128)}), f32[128,4,128]{2,1,0:T(4,128)S(1)}, u32[]{:S(2)}, u32[]{:S(2)}) async-start(f32[128,4,128]{2,1,0:T(4,128)} %bitcast.140), calls=%async_computation | async-start | bytes 524288 | tf_op jit(solution)/shard_map/all_to_all | solution.py:40
  78.0 3.1 %fusion.7 = f32[1,128,4096]{2,1,0:T(8,128)} fusion(bf16[128,4096]{1,0:T(8,128)(2,1)} %copy-done.1, f32[128]{0:T(128)S(1)} %get-tuple-element.18, bf16[2,128,128]{2,1,0:T(8,128)(2,1)} %param.10), kind=kOutput, calls=%fused_computation.15 | convolution fusion | flops 134742016 | bytes 3179008 | tf_op jit(solution)/shard_map/og,bgt->bot/dot_general | solution.py:55
  81.2 0.5 convolution_bitcast_fusion.4
  81.7 1.3 %copy-done = f32[1,128,4096]{2,1,0:T(8,128)} copy-done((f32[1,128,4096]{2,1,0:T(8,128)}, f32[1,128,4096]{2,1,0:T(8,128)S(1)}, u32[]{:S(2)}) %copy-start) | copy-done | bytes 2097176
  83.0 0.8 slice.246
  83.8 1.3 %collective-permute-start.3 = (bf16[1,64,4096]{2,1,0:T(8,128)(2,1)}, bf16[1,64,4096]{2,1,0:T(8,128)(2,1)}, u32[]{:S(2)}, u32[]{:S(2)}) collective-permute-start(bf16[1,64,4096]{2,1,0:T(8,128)(2,1)} %slice.246), channel_id=1, source_target_pairs={{1,0},{2,1},{3,2},{4,3},{5,4},{6,5},{7,6},{8,7},{9,8},{10,9},{11,1... | collective-permute-start | bytes 1572872 | tf_op jit(solution)/shard_map/ppermute | solution.py:16
  85.1 5.3 %all-to-all-done = f32[128,4,128]{2,1,0:T(4,128)S(1)} async-done(((f32[128,4,128]{2,1,0:T(4,128)}), f32[128,4,128]{2,1,0:T(4,128)S(1)}, u32[]{:S(2)}, u32[]{:S(2)}) %all-to-all-start) | async-done | bytes 262176 | tf_op jit(solution)/shard_map/all_to_all | solution.py:40
  90.6 0.7 broadcast_in_dim.2
  91.3 9.5 %all-to-all-start.1 = ((f32[128,4,128]{2,1,0:T(4,128)}), f32[128,4,128]{2,1,0:T(4,128)S(1)}, u32[]{:S(2)}, u32[]{:S(2)}) async-start(f32[128,4,128]{2,1,0:T(4,128)} %broadcast_in_dim.2), calls=%async_computation.1 | async-start | bytes 524288 | tf_op jit(solution)/shard_map/all_to_all | solution.py:41
  100.8 2.7 %fusion.22 = (bf16[1,64,4096]{2,1,0:T(8,128)(2,1)}, bf16[1,64,4096]{2,1,0:T(8,128)(2,1)}) fusion(f32[1,128,4096]{2,1,0:T(8,128)} %fusion.7, f32[1,128,4096]{2,1,0:T(8,128)S(1)} %fusion.5, bf16[1,64,4096]{2,1,0:T(8,128)(2,1)S(1)} %fusion.24), kind=kLoop, calls=%fused_computation.51 | loop fusion | flops 1310720 | bytes 4718592 | tf_op jit(solution)/shard_map/convert_element_type | solution.py:131
  103.5 9.3 %all-to-all-done.1 = f32[128,4,128]{2,1,0:T(4,128)S(1)} async-done(((f32[128,4,128]{2,1,0:T(4,128)}), f32[128,4,128]{2,1,0:T(4,128)S(1)}, u32[]{:S(2)}, u32[]{:S(2)}) %all-to-all-start.1) | async-done | bytes 262176 | tf_op jit(solution)/shard_map/all_to_all | solution.py:41
  112.8 3.2 %collective-permute-start.5 = (f32[512,128]{1,0:T(8,128)S(1)}, f32[512,128]{1,0:T(8,128)S(1)}, u32[]{:S(2)}, u32[]{:S(2)}) collective-permute-start(f32[512,128]{1,0:T(8,128)S(1)} %bitcast.138), channel_id=1, source_target_pairs={{0,16},{16,0},{1,17},{17,1},{2,18},{18,2},{3,19},{19,3},{4,20},{20... | collective-permute-start | bytes 786440 | tf_op jit(solution)/shard_map/ppermute | solution.py:20
  116.0 2.3 %fusion.19 = bf16[1,64,4096]{2,1,0:T(8,128)(2,1)} fusion(f32[1,128,4096]{2,1,0:T(8,128)} %copy-done, bf16[1,64,4096]{2,1,0:T(8,128)(2,1)} %collective-permute-done.3, bf16[1,64,4096]{2,1,0:T(8,128)(2,1)S(1)} %fusion.21), kind=kLoop, calls=%fused_computation.45 | loop fusion | flops 1310720 | bytes 2621440 | tf_op jit(solution)/shard_map/convert_element_type | solution.py:163
  118.4 0.6 maximum_multiply_fusion.3
  119.0 0.7 maximum_multiply_fusion.1
  119.7 0.6 maximum_multiply_fusion.2
  120.2 0.7 maximum_multiply_fusion
  (36 shorter events, 0.5 us)
Async XLA Ops:
  0.6 16.4 %collective-permute-start = (bf16[1,64,4096]{2,1,0:T(8,128)(2,1)}, bf16[1,64,4096]{2,1,0:T(8,128)(2,1)S(1)}, u32[]{:S(2)}, u32[]{:S(2)}) collective-permute-start(bf16[1,64,4096]{2,1,0:T(8,128)(2,1)} %param.7), channel_id=1, source_target_pairs={{0,1},{1,2},{2,3},{3,4},{4,5},{5,6},{6,7},{7,8},{8,9},{9,10},{10,1... | collective-permute-start | bytes 1572872 | tf_op jit(solution)/shard_map/ppermute | solution.py:16
  17.0 2.0 %copy-start.10 = (bf16[1,64,4096]{2,1,0:T(8,128)(2,1)}, bf16[1,64,4096]{2,1,0:T(8,128)(2,1)S(1)}, u32[]{:S(2)}) copy-start(bf16[1,64,4096]{2,1,0:T(8,128)(2,1)S(1)} %collective-permute-done) | copy-start | bytes 1572868
  19.0 0.9 copy-start.12
  19.8 1.0 copy-start.8
  19.9 6.5 %copy-start.7 = (bf16[1,64,4096]{2,1,0:T(8,128)(2,1)S(1)}, bf16[1,64,4096]{2,1,0:T(8,128)(2,1)}, u32[]{:S(2)}) copy-start(bf16[1,64,4096]{2,1,0:T(8,128)(2,1)} %param.13) | copy-start | bytes 1572868
  20.9 15.1 %copy-start.9 = (bf16[2,256,128]{2,1,0:T(8,128)(2,1)S(1)}, bf16[2,256,128]{2,1,0:T(8,128)(2,1)}, u32[]{:S(2)}) copy-start(bf16[2,256,128]{2,1,0:T(8,128)(2,1)} %param.8) | copy-start | bytes 393220
  21.0 15.0 %collective-permute-start.1 = (bf16[1,64,4096]{2,1,0:T(8,128)(2,1)S(1)}, bf16[1,64,4096]{2,1,0:T(8,128)(2,1)S(1)}, u32[]{:S(2)}, u32[]{:S(2)}) collective-permute-start(bf16[1,64,4096]{2,1,0:T(8,128)(2,1)S(1)} %fusion.24), channel_id=1, source_target_pairs={{0,2},{1,3},{2,4},{3,5},{4,6},{5,7},{6,8},{7,9},{8,10},{9,11},{10,... | collective-permute-start | bytes 1572872 | tf_op jit(solution)/shard_map/ppermute | solution.py:16
  38.2 3.0 %copy-start.1 = (bf16[128,4096]{1,0:T(8,128)(2,1)}, bf16[128,4096]{1,0:T(8,128)(2,1)S(1)}, u32[]{:S(2)}) copy-start(bf16[128,4096]{1,0:T(8,128)(2,1)S(1)} %get-tuple-element.11) | copy-start | bytes 3145732
  38.7 13.9 %collective-permute-start.2 = (bf16[1,64,4096]{2,1,0:T(8,128)(2,1)S(1)}, bf16[1,64,4096]{2,1,0:T(8,128)(2,1)S(1)}, u32[]{:S(2)}, u32[]{:S(2)}) collective-permute-start(bf16[1,64,4096]{2,1,0:T(8,128)(2,1)S(1)} %slice.247), channel_id=1, source_target_pairs={{2,0},{3,1},{4,2},{5,3},{6,4},{7,5},{8,6},{9,7},{10,8},{11,9},{12,... | collective-permute-start | bytes 1572872 | tf_op jit(solution)/shard_map/ppermute | solution.py:16
  41.1 11.5 %copy-start.6 = (bf16[1,64,4096]{2,1,0:T(8,128)(2,1)S(1)}, bf16[1,64,4096]{2,1,0:T(8,128)(2,1)}, u32[]{:S(2)}) copy-start(bf16[1,64,4096]{2,1,0:T(8,128)(2,1)} %param.12) | copy-start | bytes 1572868
  54.1 1.1 copy-start.2
  54.1 1.4 %copy-start.4 = (bf16[1,128,4096]{2,1,0:T(8,128)(2,1)}, bf16[1,128,4096]{2,1,0:T(8,128)(2,1)S(1)}, u32[]{:S(2)}) copy-start(bf16[1,128,4096]{2,1,0:T(8,128)(2,1)S(1)} %get-tuple-element.8) | copy-start | bytes 3145732
  54.6 1.3 %copy-start.11 = (bf16[1,64,4096]{2,1,0:T(8,128)(2,1)S(1)}, bf16[1,64,4096]{2,1,0:T(8,128)(2,1)}, u32[]{:S(2)}) copy-start(bf16[1,64,4096]{2,1,0:T(8,128)(2,1)} %copy-done.10) | copy-start | bytes 1572868
  56.6 4.4 %collective-permute-start.4 = (f32[512,128]{1,0:T(8,128)S(1)}, f32[512,128]{1,0:T(8,128)S(1)}, u32[]{:S(2)}, u32[]{:S(2)}) collective-permute-start(f32[512,128]{1,0:T(8,128)S(1)} %broadcast_select_fusion.2), channel_id=1, source_target_pairs={{0,16},{16,0},{1,17},{17,1},{2,18},{18,2},{3,19},{19,3},{4,20},{20... | collective-permute-start | bytes 786440 | tf_op jit(solution)/shard_map/ppermute | solution.py:20
  61.7 28.7 %all-to-all-start = ((f32[128,4,128]{2,1,0:T(4,128)}), f32[128,4,128]{2,1,0:T(4,128)S(1)}, u32[]{:S(2)}, u32[]{:S(2)}) async-start(f32[128,4,128]{2,1,0:T(4,128)} %bitcast.140), calls=%async_computation | async-start | bytes 524288 | tf_op jit(solution)/shard_map/all_to_all | solution.py:40
  78.0 3.2 %copy-start.3 = (bf16[1,128,4096]{2,1,0:T(8,128)(2,1)S(1)}, bf16[1,128,4096]{2,1,0:T(8,128)(2,1)}, u32[]{:S(2)}) copy-start(bf16[1,128,4096]{2,1,0:T(8,128)(2,1)} %copy-done.2) | copy-start | bytes 3145732
  78.0 3.2 %copy-start.5 = (bf16[1,128,4096]{2,1,0:T(8,128)(2,1)S(1)}, bf16[1,128,4096]{2,1,0:T(8,128)(2,1)}, u32[]{:S(2)}) copy-start(bf16[1,128,4096]{2,1,0:T(8,128)(2,1)} %copy-done.4) | copy-start | bytes 3145732
  81.6 1.3 %copy-start = (f32[1,128,4096]{2,1,0:T(8,128)}, f32[1,128,4096]{2,1,0:T(8,128)S(1)}, u32[]{:S(2)}) copy-start(f32[1,128,4096]{2,1,0:T(8,128)S(1)} %convolution_bitcast_fusion.4) | copy-start | bytes 6291460
  83.8 32.1 %collective-permute-start.3 = (bf16[1,64,4096]{2,1,0:T(8,128)(2,1)}, bf16[1,64,4096]{2,1,0:T(8,128)(2,1)}, u32[]{:S(2)}, u32[]{:S(2)}) collective-permute-start(bf16[1,64,4096]{2,1,0:T(8,128)(2,1)} %slice.246), channel_id=1, source_target_pairs={{1,0},{2,1},{3,2},{4,3},{5,4},{6,5},{7,6},{8,7},{9,8},{10,9},{11,1... | collective-permute-start | bytes 1572872 | tf_op jit(solution)/shard_map/ppermute | solution.py:16
  91.3 21.5 %all-to-all-start.1 = ((f32[128,4,128]{2,1,0:T(4,128)}), f32[128,4,128]{2,1,0:T(4,128)S(1)}, u32[]{:S(2)}, u32[]{:S(2)}) async-start(f32[128,4,128]{2,1,0:T(4,128)} %broadcast_in_dim.2), calls=%async_computation.1 | async-start | bytes 524288 | tf_op jit(solution)/shard_map/all_to_all | solution.py:41
  112.8 5.5 %collective-permute-start.5 = (f32[512,128]{1,0:T(8,128)S(1)}, f32[512,128]{1,0:T(8,128)S(1)}, u32[]{:S(2)}, u32[]{:S(2)}) collective-permute-start(f32[512,128]{1,0:T(8,128)S(1)} %bitcast.138), channel_id=1, source_target_pairs={{0,16},{16,0},{1,17},{17,1},{2,18},{18,2},{3,19},{19,3},{4,20},{20... | collective-permute-start | bytes 786440 | tf_op jit(solution)/shard_map/ppermute | solution.py:20

commit v2 on v1

v2 whole, which is shorter than its diff:
```python
import math

import jax
import jax.numpy as jnp
from jax import lax
from jax.experimental import pallas as pl
from jax.experimental.pallas import tpu as pltpu
from jax.sharding import Mesh, PartitionSpec as P

CORNER = ("y", "xl", "core")
TM = ("z", "xh")
CHIPS = ("y", "xl", "z", "xh")
HALVES = 2
TILE = 512
F32, BF16 = jnp.float32, jnp.bfloat16


def from_behind(block, distance):
    devices = range(lax.axis_size(TM))
    route = [(i - distance, i) for i in devices if i - distance in devices]
    return lax.ppermute(block, TM, route)


def mm(a, b):
    return lax.dot_general(a, b, (((1,), (0,)), ((), ())), preferred_element_type=F32)


def mm_t(a, b):
    return lax.dot_general(a, b, (((1,), (1,)), ((), ())), preferred_element_type=F32)


def gates(weight, stacked, bias):
    pre = mm(weight, stacked) + bias
    half = pre.shape[0] // 2
    return jnp.tanh(pre[:half]), 0.5 * jnp.tanh(0.5 * pre[half:]) + 0.5


def gate_grad(gz, filt, gate):
    both = gz * gate
    return jnp.concatenate(
        [both * (1.0 - filt * filt), both * filt * (1.0 - gate)], axis=0
    ).astype(BF16)


def tiles(n):
    return [slice(i, i + TILE) for i in range(0, n, TILE)]


def shift(s, off):
    return slice(s.start + off, s.stop + off)


def call(body, out, flops, name, *args):
    size = sum(math.prod(a.shape) * a.dtype.itemsize for a in (*args, *out))
    spec = pl.BlockSpec(memory_space=pltpu.VMEM)
    return pl.pallas_call(
        body,
        out_shape=[jax.ShapeDtypeStruct(o.shape, o.dtype) for o in out],
        in_specs=[spec] * len(args),
        out_specs=[spec] * len(out),
        name=name,
        cost_estimate=pl.CostEstimate(
            flops=flops, bytes_accessed=size, transcendentals=0
        ),
        compiler_params=pltpu.CompilerParams(vmem_limit_bytes=12 * 2**20),
    )(*args)


def arr(*shape, dtype=BF16):
    return jax.ShapeDtypeStruct(shape, dtype)


def lower_forward(off, n, signal, tap, w, b, v, vb):
    def body(sig, tap, w, b, v, vb, mid, z_out):
        for s in tiles(n):
            a = sig[0, :, shift(s, off)]
            filt, gate = gates(w[0], jnp.concatenate([tap[:, s], a], axis=0), b[0])
            z = (filt * gate).astype(BF16)
            z_out[:, s] = z
            mid[:, s] = (a.astype(F32) + mm(v[0, :64, :], z) + vb[0, :64, :]).astype(BF16)

    return call(
        body, [arr(64, n), arr(128, n)], 90000 * n, "lower_forward", signal, tap, w, b, v, vb
    )


def upper_critical(off, n, mid, tap, top, skip, w, b, wt, vt):
    def body(mid, tap, top, skip, w, b, wt, vt, z_out, gpre_out, gdel):
        for s in tiles(n):
            filt, gate = gates(w[1], jnp.concatenate([tap[:, s], mid[:, s]], axis=0), b[1])
            z_out[:, s] = (filt * gate).astype(BF16)
            u = jnp.concatenate([top[0, :, shift(s, off)], skip[0, :, shift(s, off)]], axis=0)
            gpre = gate_grad(mm(vt[1], u), filt, gate)
            gpre_out[:, s] = gpre
            gdel[:, s] = mm(wt[1, :64, :], gpre).astype(BF16)

    return call(
        body,
        [arr(128, n), arr(256, n), arr(64, n)],
        130000 * n,
        "upper_critical",
        mid, tap, top, skip, w, b, wt, vt,
    )


def put_sums(out, gpre, u, stacked, z, before=None):
    ones = jnp.ones((16, u.shape[1]), BF16)
    bias, proj_bias = mm_t(ones, gpre), mm_t(ones, u)
    rows = [
        (0, mm_t(gpre, stacked)),
        (256, mm_t(u, z)),
        (384, jnp.concatenate([bias[:1, :128], bias[:1, 128:], proj_bias[:1]], axis=0)),
    ]
    for start, value in rows:
        at = slice(start, start + value.shape[0])
        out[at, :] = value if before is None else before[at, :] + value


def upper_rest(n, mids, taps, gpres, z0s, z1s, top, skip, v, vb):
    h = len(mids)

    def body(*refs):
        mids, taps, gpres, z0s, z1s = (refs[i * h : i * h + h] for i in range(5))
        top, skip, v, vb, x_top, skip_sum, sums, u, st, gp, z1 = refs[5 * h :]
        both = jnp.concatenate([v[0, 64:, :], v[1, 64:, :]], axis=1)
        both_bias = vb[0, 64:, :] + vb[1, 64:, :]
        for i in range(h):
            for s in tiles(n):
                at = shift(s, i * n)
                z = z1s[i][:, s]
                mid = mids[i][:, s]
                x_top[0, :, at] = (mid.astype(F32) + mm(v[1, :64, :], z) + vb[1, :64, :]).astype(BF16)
                zz = jnp.concatenate([z0s[i][:, s], z], axis=0)
                skip_sum[0, :, at] = (mm(both, zz) + both_bias).astype(BF16)
                u[:64, at] = top[0, :, at]
                u[64:, at] = skip[0, :, at]
                st[:64, at] = taps[i][:, s]
                st[64:, at] = mid
                gp[:, at] = gpres[i][:, s]
                z1[:, at] = z
        sums[384:, :] = jnp.zeros((sums.shape[0] - 384, 128), F32)
        put_sums(sums, gp[...], u[...], st[...], z1[...])

    m = h * n
    args = (*mids, *taps, *gpres, *z0s, *z1s, top, skip, v, vb)
    out = [arr(1, 64, m), arr(1, 64, m), arr(512, 128, dtype=F32)]
    size = sum(math.prod(a.shape) * a.dtype.itemsize for a in (*args, *out))
    spec = pl.BlockSpec(memory_space=pltpu.VMEM)
    return pl.pallas_call(
        body,
        out_shape=out,
        in_specs=[spec] * len(args),
        out_specs=[spec] * 3,
        scratch_shapes=[pltpu.VMEM((k, m), BF16) for k in (128, 128, 256, 128)],
        name="upper_rest",
        cost_estimate=pl.CostEstimate(flops=200000 * m, bytes_accessed=size, transcendentals=0),
        compiler_params=pltpu.CompilerParams(vmem_limit_bytes=12 * 2**20),
    )(*args)


def lower_backward(off, n, gdel, gpre1, signal, tap, z0, top, skip, w, b, wt, vt, before):
    def body(gdel, gpre1, sig, tap, z0, top, skip, w, b, wt, vt, *rest):
        before, (mid_grad, gpre_out, sums, u, st) = rest[:-5], rest[-5:]
        for s in tiles(n):
            at = shift(s, off)
            grad = (
                top[0, :, at].astype(F32) + mm(wt[1, 64:, :], gpre1[:, s]) + gdel[:, s].astype(F32)
            ).astype(BF16)
            mid_grad[:, s] = grad
            both = jnp.concatenate([grad, skip[0, :, at]], axis=0)
            u[:, s] = both
            stacked = jnp.concatenate([tap[:, s], sig[0, :, at]], axis=0)
            st[:, s] = stacked
            filt, gate = gates(w[0], stacked, b[0])
            gpre_out[:, s] = gate_grad(mm(vt[0], both), filt, gate)
        sums[384:, :] = jnp.zeros((sums.shape[0] - 384, 128), F32)
        put_sums(sums, gpre_out[...], u[...], st[...], z0[...], *before)

    args = (gdel, gpre1, signal, tap, z0, top, skip, w, b, wt, vt, *before)
    out = [arr(64, n), arr(256, n), arr(512, 128, dtype=F32)]
    size = sum(math.prod(a.shape) * a.dtype.itemsize for a in (*args, *out))
    spec = pl.BlockSpec(memory_space=pltpu.VMEM)
    return pl.pallas_call(
        body,
        out_shape=out,
        in_specs=[spec] * len(args),
        out_specs=[spec] * 3,
        scratch_shapes=[pltpu.VMEM((128, n), BF16)] * 2,
        name="lower_backward",
        cost_estimate=pl.CostEstimate(flops=260000 * n, bytes_accessed=size, transcendentals=0),
        compiler_params=pltpu.CompilerParams(vmem_limit_bytes=12 * 2**20),
    )(*args)


def lower_input(n, mid_grads, gpres, wt):
    h = len(gpres)

    def body(*refs):
        grads, gpres, wt, gdel, rest = refs[:h], refs[h : 2 * h], *refs[2 * h :]
        for i in range(h):
            for s in tiles(n):
                gin = mm(wt[0], gpres[i][:, s])
                gdel[:, shift(s, i * n)] = gin[:64].astype(BF16)
                rest[:, shift(s, i * n)] = grads[i][:, s].astype(F32) + gin[64:]

    m = h * n
    return call(
        body, [arr(64, m), arr(64, m, dtype=F32)], 65000 * m, "lower_input",
        *mid_grads, *gpres, wt,
    )


def swap_cores(block, route=((0, 1), (1, 0))):
    return lax.ppermute(block, "core", route)


def unpack_layer(rows):
    return rows[:256], rows[384:386].reshape(256), rows[256:384], rows[386]


def reduce_over_chips(rows, scale):
    chips = lax.axis_size(CHIPS)
    parts = rows.reshape(chips, -1, 128)
    share = jnp.sum(lax.all_to_all(parts, CHIPS, 0, 0, tiled=True), axis=0, keepdims=True)
    whole = lax.all_to_all(
        jnp.broadcast_to(share * scale, parts.shape), CHIPS, 0, 0, tiled=True
    )
    return whole.reshape(rows.shape)


def on_device(signal, w, b, v, vb, top, skip):
    m = signal.shape[2]
    n = m // HALVES
    offs = range(0, m, n)
    taps = [from_behind(signal[0, :, o : o + n], 1) for o in offs]
    b, vb = b[:, :, None], vb[:, :, None]
    wt, vt = jnp.swapaxes(w, 1, 2), jnp.swapaxes(v, 1, 2)
    mids, z0s, mid_taps = [], [], []
    for o, tap in zip(offs, taps):
        mid, z0 = lower_forward(o, n, signal, tap, w, b, v, vb)
        mids.append(mid)
        z0s.append(z0)
        mid_taps.append(from_behind(mid, 2))
    z1s, gpres1, gdels1 = [], [], []
    for o, mid, tap in zip(offs, mids, mid_taps):
        z1, gpre1, gdel = upper_critical(o, n, mid, tap, top, skip, w, b, wt, vt)
        z1s.append(z1)
        gpres1.append(gpre1)
        gdels1.append(from_behind(gdel, -2))
    x_top, skip_sum, high = upper_rest(n, mids, mid_taps, gpres1, z0s, z1s, top, skip, v, vb)
    high_other = swap_cores(high, [(0, 1)])
    low, mid_grads, gpres0 = [], [], []
    for i, o in enumerate(offs):
        grad, gpre0, *low = lower_backward(
            o, n, gdels1[i], gpres1[i], signal, taps[i], z0s[i], top, skip, w, b, wt, vt, low
        )
        mid_grads.append(grad)
        gpres0.append(gpre0)
    low_other = swap_cores(low[0], [(1, 0)])
    first = lax.axis_index("core") == 0
    count = signal.shape[0] * lax.axis_size(CORNER) * m * lax.axis_size(TM)
    held = reduce_over_chips(
        jnp.where(first, low[0] + low_other, high + high_other), 1.0 / math.sqrt(count)
    )
    gdel0, rest = lower_input(n, mid_grads, gpres0, wt)
    grad_input = (rest + from_behind(gdel0, -1).astype(F32)).astype(BF16)[None]
    other = swap_cores(held)
    low, high = jnp.where(first, held, other), jnp.where(first, other, held)
    grads = [jnp.stack(pair) for pair in zip(unpack_layer(low), unpack_layer(high))]
    return (x_top, skip_sum, grad_input, *grads)


def solution(mesh):
    fine = Mesh(mesh.devices.reshape(4, 2, 2, 8, 2), ("y", "xl", "core", "z", "xh"))
    field = P(CORNER, None, TM)
    return jax.shard_map(
        on_device,
        mesh=fine,
        in_specs=(field, P(), P(), P(), P(), field, field),
        out_specs=(field, field, field, P(), P(), P(), P()),
        check_vma=False,
    )
```

time: 122 us -> 114 us (0.934)
  waiting for transfers between devices: 44.4 us -> 10.6 us
  blocking collectives: 0 us -> 19.6 us
  Pallas kernels: 0 us -> 18.1 us
  matrix products: 12.3 us -> 0 us
  other arithmetic: 10.8 us -> 5.39 us
  starting transfers between devices: 45.5 us -> 50.6 us
  local copies, waits for them, and re-layouts: 6.97 us -> 8.48 us
    ppermute x6 -> x10, waiting for transfers between devices: 29.8 us -> 2.02 us  [the longest x3 1.39 us: swap_cores(): return lax.ppermute(block, 'core', route)]
    all_to_all x0 -> x1, blocking collectives: none -> 19.6 us  [reduce_over_chips(): lax.all_to_all(jnp.broadcast_to(share * scale, parts.shape), CHIPS, 0, 0,...]
    pallas_call x0 -> x8, Pallas kernels: none -> 18.1 us  [the longest x5 9.91 us: call(): pl.pallas_call(body, out_shape=[jax.ShapeDtypeStruct(o.shape, o.dtype) fo...]
    ppermute x6 -> x10, starting transfers between devices: 19.8 us -> 32.9 us  [the longest x7 22.9 us: from_behind(): return lax.ppermute(block, TM, route)]
    dot_general x12 -> x0, matrix products: 12.3 us -> none  [the longest x2 3.57 us: gated_layer_forward(): jnp.einsum('og,bgt->bot', proj, gate_out, preferred_element_type=jnp.floa...]
    all_to_all x1 -> x0, starting transfers between devices: 9.48 us -> none  [reduce_over_chips(): lax.all_to_all(jnp.broadcast_to(share, parts.shape), CHIPS, 0, 0, tiled=T...]
    all_to_all x1 -> x0, waiting for transfers between devices: 9.27 us -> none  [reduce_over_chips(): lax.all_to_all(jnp.broadcast_to(share, parts.shape), CHIPS, 0, 0, tiled=T...]
    convert_element_type x4 -> x0, other arithmetic: 5.28 us -> none  [the longest x1 2.7 us: on_device(): skip_out = (lower_skip_output + upper_skip_output).astype(jnp.bfloat16)]
  transfers between devices with their start and end apart: 8 -> 11, of which waited for: 6 -> 4; matrix products, arithmetic and copies ran while one was open for 12% -> 1% of each run, Pallas kernels for 0% -> 16%
where the time goes in v2:
time: 114 us
  starting transfers between devices  50.6 us (44%)
  blocking collectives  19.6 us (17%)
  Pallas kernels  18.1 us (16%)
  waiting for transfers between devices  10.6 us (9%)
  local copies, waits for them, and re-layouts  8.48 us (7%)
  other arithmetic  5.39 us (5%)
    ppermute x7, starting transfers between devices, from_behind(): return lax.ppermute(block, TM, route)  22.9 us
    all_to_all x1, blocking collectives, reduce_over_chips(): lax.all_to_all(jnp.broadcast_to(share * scale, parts.shape), CHIPS, 0, 0,...  19.6 us
    all_to_all x1, starting transfers between devices, reduce_over_chips(): lax.all_to_all(parts, CHIPS, 0, 0, tiled=True)  17.7 us
    ppermute x3, starting transfers between devices, swap_cores(): return lax.ppermute(block, 'core', route)  9.95 us
    pallas_call x5, Pallas kernels, call(): pl.pallas_call(body, out_shape=[jax.ShapeDtypeStruct(o.shape, o.dtype) fo...  9.91 us
    all_to_all x1, waiting for transfers between devices, reduce_over_chips(): lax.all_to_all(parts, CHIPS, 0, 0, tiled=True)  8.57 us
    unnamed x42, local copies, waits for them, and re-layouts  7 us
    pallas_call x1, Pallas kernels, upper_rest(): pl.pallas_call(body, out_shape=out, in_specs=[spec] * len(args), out_spec...  4.28 us
  transfers between devices with their start and end apart: 11, of which 4 were waited for; matrix products, arithmetic and copies ran while one was open for 1% of the time, Pallas kernels for 16%

profile of v2, /device:TPU:1, one launch (start us, length us, event | category | flops | bytes accessed | tf_op | source)
XLA Modules:
  0.0 113.7 jit_solution(2284187473251477345)
XLA Ops:
  0.6 1.1 slice_bitcast_fusion
  1.8 0.0 copy-start.18
  1.8 5.5 %collective-permute-start = (bf16[64,2048]{1,0:T(8,128)(2,1)S(1)}, bf16[64,2048]{1,0:T(8,128)(2,1)S(1)}, u32[]{:S(2)}, u32[]{:S(2)}) collective-permute-start(bf16[64,2048]{1,0:T(8,128)(2,1)S(1)} %get-tuple-element.52), channel_id=1, source_target_pairs={{0,1},{1,2},{2,3},{3,4},{4,5},{5,6},{6,7},{7,8},{8,9},{9,10},{10,1... | collective-permute-start | bytes 786440 | tf_op jit(solution)/shard_map/ppermute | solution.py:21
  7.3 3.5 %collective-permute-start.1 = (bf16[64,2048]{1,0:T(8,128)(2,1)S(1)}, bf16[64,2048]{1,0:T(8,128)(2,1)S(1)}, u32[]{:S(2)}, u32[]{:S(2)}) collective-permute-start(bf16[64,2048]{1,0:T(8,128)(2,1)S(1)} %get-tuple-element.51), channel_id=1, source_target_pairs={{0,1},{1,2},{2,3},{3,4},{4,5},{5,6},{6,7},{7,8},{8,9},{9,10},{10,1... | collective-permute-start | bytes 786440 | tf_op jit(solution)/shard_map/ppermute | solution.py:21
  10.8 0.0 copy-start.19
  10.8 0.0 copy-start.4
  10.8 0.1 copy.16.b
  11.0 0.0 copy-start.3
  11.0 0.5 copy-done.19
  11.5 0.1 copy.17.vb.refs_13_
  11.6 0.6 collective-permute-done.tap
  12.2 1.9 %lower_forward.2 = (bf16[64,2048]{1,0:T(8,128)(2,1)}, bf16[128,2048]{1,0:T(8,128)(2,1)S(1)}) custom-call(bf16[1,64,4096]{2,1,0:T(8,128)(2,1)S(1)} %copy-done, bf16[64,2048]{1,0:T(8,128)(2,1)S(1)} %collective-permute-done.tap, bf16[2,256,128]{2,1,0:T(8,128)(2,1)S(1)} %copy-done.3, f32[2,256,1]{2,1,0:T(8,128)S(1)} %copy.16.b, ...), custom_call_target="tpu_custom_call" | custom-call | flops 184320000 | bytes 1772544 | tf_op jit(solution)/shard_map/lower_forward/pallas_call | solution.py:56
  14.1 6.1 %collective-permute-start.2 = (bf16[64,2048]{1,0:T(8,128)(2,1)}, bf16[64,2048]{1,0:T(8,128)(2,1)}, u32[]{:S(2)}, u32[]{:S(2)}) collective-permute-start(bf16[64,2048]{1,0:T(8,128)(2,1)} %get-tuple-element.28.mid.refs_0_), channel_id=1, source_target_pairs={{0,2},{1,3},{2,4},{3,5},{4,6},{5,7},{6,8},{7,9},{8,10},{9,11},{10,... | collective-permute-start | bytes 786440 | tf_op jit(solution)/shard_map/ppermute | solution.py:21
  20.2 0.7 copy-done.9
  20.9 0.9 copy-done.10
  21.9 1.8 %lower_forward.3 = (bf16[64,2048]{1,0:T(8,128)(2,1)}, bf16[128,2048]{1,0:T(8,128)(2,1)S(1)}) custom-call(bf16[1,64,4096]{2,1,0:T(8,128)(2,1)S(1)} %copy-done, bf16[64,2048]{1,0:T(8,128)(2,1)S(1)} %copy-done.10, bf16[2,256,128]{2,1,0:T(8,128)(2,1)S(1)} %copy-done.3, f32[2,256,1]{2,1,0:T(8,128)S(1)} %copy.16.b, bf16[2,128,128]{2,1,0:T(8,128)(2,1)S(1)} %copy-done.4, ...), custom_call_target="tpu_custom_call" | custom-call | flops 184320000 | bytes 1772544 | tf_op jit(solution)/shard_map/lower_forward/pallas_call | solution.py:56
  23.7 4.0 %collective-permute-start.3 = (bf16[64,2048]{1,0:T(8,128)(2,1)}, bf16[64,2048]{1,0:T(8,128)(2,1)}, u32[]{:S(2)}, u32[]{:S(2)}) collective-permute-start(bf16[64,2048]{1,0:T(8,128)(2,1)} %get-tuple-element.29.mid.refs_1_), channel_id=1, source_target_pairs={{0,2},{1,3},{2,4},{3,5},{4,6},{5,7},{6,8},{7,9},{8,10},{9,11},{10,... | collective-permute-start | bytes 786440 | tf_op jit(solution)/shard_map/ppermute | solution.py:21
  27.7 0.1 copy.20
  27.8 0.1 copy.21
  28.0 2.5 %upper_critical.2 = (bf16[128,2048]{1,0:T(8,128)(2,1)S(1)}, bf16[256,2048]{1,0:T(8,128)(2,1)S(1)}, bf16[64,2048]{1,0:T(8,128)(2,1)S(1)}) custom-call(bf16[64,2048]{1,0:T(8,128)(2,1)} %get-tuple-element.28.mid.refs_0_, bf16[64,2048]{1,0:T(8,128)(2,1)} %collective-permute-done.2.tap.refs_2_, bf16[1,64,4096]{2,1,0:T(8,128)(2,1)S(1)} %copy-done.1, ...), custom_call_target="tpu_custom_call" | custom-call | flops 266240000 | bytes 3737600 | tf_op jit(solution)/shard_map/upper_critical/pallas_call | solution.py:56
  30.5 1.3 %collective-permute-start.4 = (bf16[64,2048]{1,0:T(8,128)(2,1)S(1)}, bf16[64,2048]{1,0:T(8,128)(2,1)S(1)}, u32[]{:S(2)}, u32[]{:S(2)}) collective-permute-start(bf16[64,2048]{1,0:T(8,128)(2,1)S(1)} %get-tuple-element.38), channel_id=1, source_target_pairs={{2,0},{3,1},{4,2},{5,3},{6,4},{7,5},{8,6},{9,7},{10,8},{11,9},{12,... | collective-permute-start | bytes 786440 | tf_op jit(solution)/shard_map/ppermute | solution.py:21
  31.8 2.5 %upper_critical.3 = (bf16[128,2048]{1,0:T(8,128)(2,1)S(1)}, bf16[256,2048]{1,0:T(8,128)(2,1)S(1)}, bf16[64,2048]{1,0:T(8,128)(2,1)S(1)}) custom-call(bf16[64,2048]{1,0:T(8,128)(2,1)} %get-tuple-element.29.mid.refs_1_, bf16[64,2048]{1,0:T(8,128)(2,1)} %collective-permute-done.3.tap.refs_3_, bf16[1,64,4096]{2,1,0:T(8,128)(2,1)S(1)} %copy-done.1, ...), custom_call_target="tpu_custom_call" | custom-call | flops 266240000 | bytes 3737600 | tf_op jit(solution)/shard_map/upper_critical/pallas_call | solution.py:56
  34.3 1.3 %collective-permute-start.5 = (bf16[64,2048]{1,0:T(8,128)(2,1)S(1)}, bf16[64,2048]{1,0:T(8,128)(2,1)S(1)}, u32[]{:S(2)}, u32[]{:S(2)}) collective-permute-start(bf16[64,2048]{1,0:T(8,128)(2,1)S(1)} %get-tuple-element.40), channel_id=1, source_target_pairs={{2,0},{3,1},{4,2},{5,3},{6,4},{7,5},{8,6},{9,7},{10,8},{11,9},{12,... | collective-permute-start | bytes 786440 | tf_op jit(solution)/shard_map/ppermute | solution.py:21
  35.6 4.3 %upper_rest.1 = (bf16[1,64,4096]{2,1,0:T(8,128)(2,1)}, bf16[1,64,4096]{2,1,0:T(8,128)(2,1)}, f32[512,128]{1,0:T(8,128)}) custom-call(bf16[64,2048]{1,0:T(8,128)(2,1)} %get-tuple-element.28.mid.refs_0_, bf16[64,2048]{1,0:T(8,128)(2,1)} %get-tuple-element.29.mid.refs_1_, bf16[64,2048]{1,0:T(8,128)(2,1)} %collective-permute-done.2.tap.refs_2_, ...), custom_call_target="tpu_custom_call" | custom-call | flops 819200000 | bytes 7668736 | tf_op jit(solution)/shard_map/upper_rest/pallas_call | solution.py:149
  39.9 1.4 %collective-permute-start.8 = (f32[512,128]{1,0:T(8,128)}, f32[512,128]{1,0:T(8,128)}, u32[]{:S(2)}, u32[]{:S(2)}) collective-permute-start(f32[512,128]{1,0:T(8,128)} %get-tuple-element.48), channel_id=1, source_target_pairs={{0,16},{1,17},{2,18},{3,19},{4,20},{5,21},{6,22},{7,23},{8,24},{9,... | collective-permute-start | bytes 786440 | tf_op jit(solution)/shard_map/ppermute | solution.py:214
  41.3 1.9 %lower_backward.2 = (bf16[64,2048]{1,0:T(8,128)(2,1)S(1)}, bf16[256,2048]{1,0:T(8,128)(2,1)S(1)}, f32[512,128]{1,0:T(8,128)S(1)}) custom-call(bf16[64,2048]{1,0:T(8,128)(2,1)S(1)} %collective-permute-done.4.gdel, bf16[256,2048]{1,0:T(8,128)(2,1)S(1)} %get-tuple-element.30.refs_4_.gpre1, bf16[1,64,4096]{2,1,0:T(8,128)(2,1)S(1)} %copy-done, ...), custom_call_target="tpu_custom_call" | custom-call | flops 532480000 | bytes 5572608 | tf_op jit(solution)/shard_map/lower_backward/pallas_call | solution.py:183
  43.2 1.0 copy-done.5
  44.2 0.7 copy-done.14
  44.9 2.0 %lower_backward.3 = (bf16[64,2048]{1,0:T(8,128)(2,1)S(1)}, bf16[256,2048]{1,0:T(8,128)(2,1)S(1)}, f32[512,128]{1,0:T(8,128)S(1)}) custom-call(bf16[64,2048]{1,0:T(8,128)(2,1)S(1)} %collective-permute-done.5.gdel, bf16[256,2048]{1,0:T(8,128)(2,1)S(1)} %get-tuple-element.31.refs_5_.gpre1, bf16[1,64,4096]{2,1,0:T(8,128)(2,1)S(1)} %copy-done, ...), custom_call_target="tpu_custom_call" | custom-call | flops 532480000 | bytes 5834752 | tf_op jit(solution)/shard_map/lower_backward/pallas_call | solution.py:183
  46.9 1.0 copy-done.7
  47.9 0.7 copy-done.16
  48.6 5.3 %collective-permute-start.7 = (f32[512,128]{1,0:T(8,128)S(1)}, f32[512,128]{1,0:T(8,128)S(1)}, u32[]{:S(2)}, u32[]{:S(2)}) collective-permute-start(f32[512,128]{1,0:T(8,128)S(1)} %get-tuple-element.47), channel_id=1, source_target_pairs={{16,0},{17,1},{18,2},{19,3},{20,4},{21,5},{22,6},{23,7},{24,8},{25... | collective-permute-start | bytes 786440 | tf_op jit(solution)/shard_map/ppermute | solution.py:214
  53.9 1.1 collective-permute-done.7
  55.0 1.8 %add_select_fusion = f32[512,128]{1,0:T(8,128)} fusion(f32[512,128]{1,0:T(8,128)} %get-tuple-element.48, f32[512,128]{1,0:T(8,128)} %collective-permute-done.8, f32[512,128]{1,0:T(8,128)S(1)} %get-tuple-element.47, f32[512,128]{1,0:T(8,128)S(1)} %collective-permute-done.7, pred[]{:T(512)S(6)} %eq.3), kind=kLoop, calls=%fused_computation.3 | loop fusion | flops 196608 | bytes 1310721 | tf_op jit(solution)/shard_map/jit(_where)/select_n | solution.py:263
  56.8 17.7 %all-to-all-start = ((f32[128,4,128]{2,1,0:T(4,128)}), f32[128,4,128]{2,1,0:T(4,128)S(1)}, u32[]{:S(2)}, u32[]{:S(2)}) async-start(f32[128,4,128]{2,1,0:T(4,128)} %bitcast.7), calls=%async_computation | async-start | bytes 524288 | tf_op jit(solution)/shard_map/all_to_all | solution.py:224
  74.6 1.2 %copy-done.8 = bf16[256,2048]{1,0:T(8,128)(2,1)S(1)} copy-done((bf16[256,2048]{1,0:T(8,128)(2,1)S(1)}, bf16[256,2048]{1,0:T(8,128)(2,1)}, u32[]{:S(2)}) %copy-start.8) | copy-done | bytes 1048600
  75.8 1.2 %lower_input.1 = (bf16[64,4096]{1,0:T(8,128)(2,1)}, f32[64,4096]{1,0:T(8,128)S(1)}) custom-call(bf16[64,2048]{1,0:T(8,128)(2,1)S(1)} %copy-done.15, bf16[64,2048]{1,0:T(8,128)(2,1)S(1)} %copy-done.17, bf16[256,2048]{1,0:T(8,128)(2,1)S(1)} %copy-done.6, bf16[256,2048]{1,0:T(8,128)(2,1)S(1)} %copy-done.8, bf16[2,128,256]{2,1,0:T(8,128)(2,1)S(1)} %bitcast.26), custom_call_target="tpu_custom_call" | custom-call | flops 266240000 | bytes 4325376 | tf_op jit(solution)/shard_map/lower_input/pallas_call | solution.py:56
  77.0 1.3 %collective-permute-start.6 = (bf16[64,4096]{1,0:T(8,128)(2,1)}, bf16[64,4096]{1,0:T(8,128)(2,1)S(1)}, u32[]{:S(2)}, u32[]{:S(2)}) collective-permute-start(bf16[64,4096]{1,0:T(8,128)(2,1)} %get-tuple-element.46), channel_id=1, source_target_pairs={{1,0},{2,1},{3,2},{4,3},{5,4},{6,5},{7,6},{8,7},{9,8},{10,9},{11,1... | collective-permute-start | bytes 1572872 | tf_op jit(solution)/shard_map/ppermute | solution.py:21
  78.3 8.6 %all-to-all-done = f32[128,4,128]{2,1,0:T(4,128)S(1)} async-done(((f32[128,4,128]{2,1,0:T(4,128)}), f32[128,4,128]{2,1,0:T(4,128)S(1)}, u32[]{:S(2)}, u32[]{:S(2)}) %all-to-all-start) | async-done | bytes 262176 | tf_op jit(solution)/shard_map/all_to_all | solution.py:224
  86.9 0.1 reduce_sum.9
  87.1 19.6 %all_to_all.10 = f32[128,4,128]{2,1,0:T(4,128)S(1)} all-to-all(f32[128,4,128]{2,1,0:T(4,128)S(1)} %broadcast_in_dim.18), channel_id=1, replica_groups=mesh['y'=4,'xl'=2,'core'=2,'z'=8,'xh'=2] {'y','xl','z','xh'}, dimensions={0} | all-to-all | bytes 524288 | tf_op jit(solution)/shard_map/all_to_all | solution.py:225
  106.6 3.2 %collective-permute-start.9 = (f32[512,128]{1,0:T(8,128)S(1)}, f32[512,128]{1,0:T(8,128)S(1)}, u32[]{:S(2)}, u32[]{:S(2)}) collective-permute-start(f32[512,128]{1,0:T(8,128)S(1)} %bitcast.31), channel_id=1, source_target_pairs={{0,16},{16,0},{1,17},{17,1},{2,18},{18,2},{3,19},{19,3},{4,20},{20... | collective-permute-start | bytes 786440 | tf_op jit(solution)/shard_map/ppermute | solution.py:214
  109.9 0.9 fusion
  110.8 0.3 collective-permute-done.9
  111.2 0.7 pad_maximum_fusion
  111.9 0.6 pad_maximum_fusion.2
  112.5 0.7 pad_maximum_fusion.1
  113.1 0.6 pad_maximum_fusion.3
  (44 shorter events, 0.2 us)
Async XLA Ops:
  0.6 11.6 %copy-start = (bf16[1,64,4096]{2,1,0:T(8,128)(2,1)S(1)}, bf16[1,64,4096]{2,1,0:T(8,128)(2,1)}, u32[]{:S(2)}) copy-start(bf16[1,64,4096]{2,1,0:T(8,128)(2,1)} %sig.7) | copy-start | bytes 1572868
  1.8 9.0 %copy-start.18 = (f32[2,256]{1,0:T(2,128)S(1)}, f32[2,256]{1,0:T(2,128)}, u32[]{:S(2)}) copy-start(f32[2,256]{1,0:T(2,128)} %param.9) | copy-start | bytes 6148
  1.8 10.4 %collective-permute-start = (bf16[64,2048]{1,0:T(8,128)(2,1)S(1)}, bf16[64,2048]{1,0:T(8,128)(2,1)S(1)}, u32[]{:S(2)}, u32[]{:S(2)}) collective-permute-start(bf16[64,2048]{1,0:T(8,128)(2,1)S(1)} %get-tuple-element.52), channel_id=1, source_target_pairs={{0,1},{1,2},{2,3},{3,4},{4,5},{5,6},{6,7},{7,8},{8,9},{9,10},{10,1... | collective-permute-start | bytes 786440 | tf_op jit(solution)/shard_map/ppermute | solution.py:21
  7.3 12.9 %collective-permute-start.1 = (bf16[64,2048]{1,0:T(8,128)(2,1)S(1)}, bf16[64,2048]{1,0:T(8,128)(2,1)S(1)}, u32[]{:S(2)}, u32[]{:S(2)}) collective-permute-start(bf16[64,2048]{1,0:T(8,128)(2,1)S(1)} %get-tuple-element.51), channel_id=1, source_target_pairs={{0,1},{1,2},{2,3},{3,4},{4,5},{5,6},{6,7},{7,8},{8,9},{9,10},{10,1... | collective-permute-start | bytes 786440 | tf_op jit(solution)/shard_map/ppermute | solution.py:21
  10.8 0.7 copy-start.19
  10.8 1.4 %copy-start.4 = (bf16[2,128,128]{2,1,0:T(8,128)(2,1)S(1)}, bf16[2,128,128]{2,1,0:T(8,128)(2,1)}, u32[]{:S(2)}) copy-start(bf16[2,128,128]{2,1,0:T(8,128)(2,1)} %refs_12_.1) | copy-start | bytes 196612
  11.0 1.3 %copy-start.3 = (bf16[2,256,128]{2,1,0:T(8,128)(2,1)S(1)}, bf16[2,256,128]{2,1,0:T(8,128)(2,1)}, u32[]{:S(2)}) copy-start(bf16[2,256,128]{2,1,0:T(8,128)(2,1)} %w.11) | copy-start | bytes 393220
  12.2 1.9 %copy-start.12 = (bf16[64,2048]{1,0:T(8,128)(2,1)}, bf16[64,2048]{1,0:T(8,128)(2,1)S(1)}, u32[]{:S(2)}) copy-start(bf16[64,2048]{1,0:T(8,128)(2,1)S(1)} %collective-permute-done.tap) | copy-start | bytes 786436
  14.1 13.8 %collective-permute-start.2 = (bf16[64,2048]{1,0:T(8,128)(2,1)}, bf16[64,2048]{1,0:T(8,128)(2,1)}, u32[]{:S(2)}, u32[]{:S(2)}) collective-permute-start(bf16[64,2048]{1,0:T(8,128)(2,1)} %get-tuple-element.28.mid.refs_0_), channel_id=1, source_target_pairs={{0,2},{1,3},{2,4},{3,5},{4,6},{5,7},{6,8},{7,9},{8,10},{9,11},{10,... | collective-permute-start | bytes 786440 | tf_op jit(solution)/shard_map/ppermute | solution.py:21
  20.2 0.7 copy-start.9
  20.9 0.9 copy-start.10
  21.9 6.1 %copy-start.1 = (bf16[1,64,4096]{2,1,0:T(8,128)(2,1)S(1)}, bf16[1,64,4096]{2,1,0:T(8,128)(2,1)}, u32[]{:S(2)}) copy-start(bf16[1,64,4096]{2,1,0:T(8,128)(2,1)} %top.7) | copy-start | bytes 1572868
  21.9 6.1 %copy-start.2 = (bf16[1,64,4096]{2,1,0:T(8,128)(2,1)S(1)}, bf16[1,64,4096]{2,1,0:T(8,128)(2,1)}, u32[]{:S(2)}) copy-start(bf16[1,64,4096]{2,1,0:T(8,128)(2,1)} %skip.7) | copy-start | bytes 1572868
  23.7 8.0 %collective-permute-start.3 = (bf16[64,2048]{1,0:T(8,128)(2,1)}, bf16[64,2048]{1,0:T(8,128)(2,1)}, u32[]{:S(2)}, u32[]{:S(2)}) collective-permute-start(bf16[64,2048]{1,0:T(8,128)(2,1)} %get-tuple-element.29.mid.refs_1_), channel_id=1, source_target_pairs={{0,2},{1,3},{2,4},{3,5},{4,6},{5,7},{6,8},{7,9},{8,10},{9,11},{10,... | collective-permute-start | bytes 786440 | tf_op jit(solution)/shard_map/ppermute | solution.py:21
  30.5 10.8 %collective-permute-start.4 = (bf16[64,2048]{1,0:T(8,128)(2,1)S(1)}, bf16[64,2048]{1,0:T(8,128)(2,1)S(1)}, u32[]{:S(2)}, u32[]{:S(2)}) collective-permute-start(bf16[64,2048]{1,0:T(8,128)(2,1)S(1)} %get-tuple-element.38), channel_id=1, source_target_pairs={{2,0},{3,1},{4,2},{5,3},{6,4},{7,5},{8,6},{9,7},{10,8},{11,9},{12,... | collective-permute-start | bytes 786440 | tf_op jit(solution)/shard_map/ppermute | solution.py:21
  34.3 10.7 %collective-permute-start.5 = (bf16[64,2048]{1,0:T(8,128)(2,1)S(1)}, bf16[64,2048]{1,0:T(8,128)(2,1)S(1)}, u32[]{:S(2)}, u32[]{:S(2)}) collective-permute-start(bf16[64,2048]{1,0:T(8,128)(2,1)S(1)} %get-tuple-element.40), channel_id=1, source_target_pairs={{2,0},{3,1},{4,2},{5,3},{6,4},{7,5},{8,6},{9,7},{10,8},{11,9},{12,... | collective-permute-start | bytes 786440 | tf_op jit(solution)/shard_map/ppermute | solution.py:21
  35.6 5.7 %copy-start.13 = (bf16[64,2048]{1,0:T(8,128)(2,1)S(1)}, bf16[64,2048]{1,0:T(8,128)(2,1)}, u32[]{:S(2)}) copy-start(bf16[64,2048]{1,0:T(8,128)(2,1)} %copy-done.12) | copy-start | bytes 786436
  39.9 5.1 %copy-start.11 = (bf16[64,2048]{1,0:T(8,128)(2,1)S(1)}, bf16[64,2048]{1,0:T(8,128)(2,1)}, u32[]{:S(2)}) copy-start(bf16[64,2048]{1,0:T(8,128)(2,1)} %copy-done.9) | copy-start | bytes 786436
  39.9 14.0 %collective-permute-start.8 = (f32[512,128]{1,0:T(8,128)}, f32[512,128]{1,0:T(8,128)}, u32[]{:S(2)}, u32[]{:S(2)}) collective-permute-start(f32[512,128]{1,0:T(8,128)} %get-tuple-element.48), channel_id=1, source_target_pairs={{0,16},{1,17},{2,18},{3,19},{4,20},{5,21},{6,22},{7,23},{8,24},{9,... | collective-permute-start | bytes 786440 | tf_op jit(solution)/shard_map/ppermute | solution.py:214
  43.2 1.0 copy-start.5
  44.2 0.7 copy-start.14
  46.9 1.0 copy-start.7
  47.9 0.7 copy-start.16
  48.6 26.0 %copy-start.6 = (bf16[256,2048]{1,0:T(8,128)(2,1)S(1)}, bf16[256,2048]{1,0:T(8,128)(2,1)}, u32[]{:S(2)}) copy-start(bf16[256,2048]{1,0:T(8,128)(2,1)} %copy-done.5) | copy-start | bytes 3145732
  48.6 6.5 %collective-permute-start.7 = (f32[512,128]{1,0:T(8,128)S(1)}, f32[512,128]{1,0:T(8,128)S(1)}, u32[]{:S(2)}, u32[]{:S(2)}) collective-permute-start(f32[512,128]{1,0:T(8,128)S(1)} %get-tuple-element.47), channel_id=1, source_target_pairs={{16,0},{17,1},{18,2},{19,3},{20,4},{21,5},{22,6},{23,7},{24,8},{25... | collective-permute-start | bytes 786440 | tf_op jit(solution)/shard_map/ppermute | solution.py:214
  56.8 17.7 %copy-start.15 = (bf16[64,2048]{1,0:T(8,128)(2,1)S(1)}, bf16[64,2048]{1,0:T(8,128)(2,1)}, u32[]{:S(2)}) copy-start(bf16[64,2048]{1,0:T(8,128)(2,1)} %copy-done.14) | copy-start | bytes 786436
  56.8 17.8 %copy-start.17 = (bf16[64,2048]{1,0:T(8,128)(2,1)S(1)}, bf16[64,2048]{1,0:T(8,128)(2,1)}, u32[]{:S(2)}) copy-start(bf16[64,2048]{1,0:T(8,128)(2,1)} %copy-done.16) | copy-start | bytes 786436
  56.8 30.1 %all-to-all-start = ((f32[128,4,128]{2,1,0:T(4,128)}), f32[128,4,128]{2,1,0:T(4,128)S(1)}, u32[]{:S(2)}, u32[]{:S(2)}) async-start(f32[128,4,128]{2,1,0:T(4,128)} %bitcast.7), calls=%async_computation | async-start | bytes 524288 | tf_op jit(solution)/shard_map/all_to_all | solution.py:224
  74.6 1.2 %copy-start.8 = (bf16[256,2048]{1,0:T(8,128)(2,1)S(1)}, bf16[256,2048]{1,0:T(8,128)(2,1)}, u32[]{:S(2)}) copy-start(bf16[256,2048]{1,0:T(8,128)(2,1)} %copy-done.7) | copy-start | bytes 3145732
  77.0 32.9 %collective-permute-start.6 = (bf16[64,4096]{1,0:T(8,128)(2,1)}, bf16[64,4096]{1,0:T(8,128)(2,1)S(1)}, u32[]{:S(2)}, u32[]{:S(2)}) collective-permute-start(bf16[64,4096]{1,0:T(8,128)(2,1)} %get-tuple-element.46), channel_id=1, source_target_pairs={{1,0},{2,1},{3,2},{4,3},{5,4},{6,5},{7,6},{8,7},{9,8},{10,9},{11,1... | collective-permute-start | bytes 1572872 | tf_op jit(solution)/shard_map/ppermute | solution.py:21
  106.6 4.4 %collective-permute-start.9 = (f32[512,128]{1,0:T(8,128)S(1)}, f32[512,128]{1,0:T(8,128)S(1)}, u32[]{:S(2)}, u32[]{:S(2)}) collective-permute-start(f32[512,128]{1,0:T(8,128)S(1)} %bitcast.31), channel_id=1, source_target_pairs={{0,16},{16,0},{1,17},{17,1},{2,18},{18,2},{3,19},{19,3},{4,20},{20... | collective-permute-start | bytes 786440 | tf_op jit(solution)/shard_map/ppermute | solution.py:214

commit v3 on v2

v3 whole, which is shorter than its diff:
```python
import math

import jax
import jax.numpy as jnp
from jax import lax
from jax.experimental import pallas as pl
from jax.experimental.pallas import tpu as pltpu
from jax.sharding import Mesh, PartitionSpec as P

CORNER = ("y", "xl", "core")
TM = ("z", "xh")
PLANE = ("y", "xl", "xh")
HALVES = 2
TILE = 512
F32, BF16 = jnp.float32, jnp.bfloat16


def from_behind(block, distance):
    devices = range(lax.axis_size(TM))
    route = [(i - distance, i) for i in devices if i - distance in devices]
    return lax.ppermute(block, TM, route)


def mm(a, b):
    return lax.dot_general(a, b, (((1,), (0,)), ((), ())), preferred_element_type=F32)


def mm_t(a, b):
    return lax.dot_general(a, b, (((1,), (1,)), ((), ())), preferred_element_type=F32)


def gates(weight, stacked, bias):
    pre = mm(weight, stacked) + bias
    half = pre.shape[0] // 2
    return jnp.tanh(pre[:half]), 0.5 * jnp.tanh(0.5 * pre[half:]) + 0.5


def gate_grad(gz, filt, gate):
    both = gz * gate
    return jnp.concatenate(
        [both * (1.0 - filt * filt), both * filt * (1.0 - gate)], axis=0
    ).astype(BF16)


def tiles(n):
    return [slice(i, i + TILE) for i in range(0, n, TILE)]


def shift(s, off):
    return slice(s.start + off, s.stop + off)


def call(body, out, flops, name, *args, scratch=()):
    size = sum(math.prod(a.shape) * a.dtype.itemsize for a in (*args, *out))
    spec = pl.BlockSpec(memory_space=pltpu.VMEM)
    return pl.pallas_call(
        body,
        out_shape=out,
        in_specs=[spec] * len(args),
        out_specs=[spec] * len(out),
        scratch_shapes=scratch,
        name=name,
        cost_estimate=pl.CostEstimate(flops=flops, bytes_accessed=size, transcendentals=0),
        compiler_params=pltpu.CompilerParams(vmem_limit_bytes=12 * 2**20),
    )(*args)


def near(*shape, dtype=BF16):
    return jax.ShapeDtypeStruct(shape, dtype)


def prepare(w, b, v, vb):
    def body(w, b, v, vb, b_out, vb_out, wt, vt):
        for rows, out in ((b, b_out), (vb, vb_out)):
            out[...] = jnp.transpose(jnp.tile(rows[...], (4, 1)))
        for layer in range(2):
            wt[layer] = jnp.transpose(w[layer])
            vt[layer] = jnp.transpose(v[layer])

    out = [near(256, 8, dtype=F32), near(128, 8, dtype=F32), near(2, 128, 256), near(2, 128, 128)]
    return call(body, out, 1000, "prepare", w, b, v, vb)


def lower_forward(off, n, signal, tap, w, b, v, vb):
    def body(sig, tap, w, b, v, vb, mid, z_out):
        for s in tiles(n):
            a = sig[0, :, shift(s, off)]
            filt, gate = gates(w[0], jnp.concatenate([tap[:, s], a], axis=0), b[:, 0:1])
            z = (filt * gate).astype(BF16)
            z_out[:, s] = z
            mid[:, s] = (a.astype(F32) + mm(v[0, :64, :], z) + vb[:64, 0:1]).astype(BF16)

    out = [near(64, n), near(128, n)]
    return call(body, out, 90000 * n, "lower_forward", signal, tap, w, b, v, vb)


def upper_critical(off, n, mid, tap, top, skip, w, b, wt, vt):
    def body(mid, tap, top, skip, w, b, wt, vt, z_out, gpre_out, gdel):
        for s in tiles(n):
            filt, gate = gates(w[1], jnp.concatenate([tap[:, s], mid[:, s]], axis=0), b[:, 1:2])
            z_out[:, s] = (filt * gate).astype(BF16)
            u = jnp.concatenate([top[0, :, shift(s, off)], skip[0, :, shift(s, off)]], axis=0)
            gpre = gate_grad(mm(vt[1], u), filt, gate)
            gpre_out[:, s] = gpre
            gdel[:, s] = mm(wt[1, :64, :], gpre).astype(BF16)

    out = [near(128, n), near(256, n), near(64, n)]
    return call(body, out, 130000 * n, "upper_critical", mid, tap, top, skip, w, b, wt, vt)


def put_sums(out, gpre, u, stacked, z, before=None):
    ones = jnp.ones((16, u.shape[1]), BF16)
    bias, proj_bias = mm_t(ones, gpre), mm_t(ones, u)
    rows = [
        (0, mm_t(gpre, stacked)),
        (256, mm_t(u, z)),
        (384, jnp.concatenate([bias[:1, :128], bias[:1, 128:], proj_bias[:1]], axis=0)),
    ]
    for start, value in rows:
        at = slice(start, start + value.shape[0])
        out[at, :] = value if before is None else before[at, :] + value


def upper_sums(n, mids, taps, gpres, z1s, top, skip):
    h = len(mids)

    def body(*refs):
        mids, taps, gpres, z1s = (refs[i * h : i * h + h] for i in range(4))
        top, skip, sums, u, st, gp, z1 = refs[4 * h :]
        u[:64, :], u[64:, :] = top[0], skip[0]
        for i in range(h):
            at = slice(i * n, i * n + n)
            st[:64, at], st[64:, at] = taps[i][...], mids[i][...]
            gp[:, at], z1[:, at] = gpres[i][...], z1s[i][...]
        sums[384:, :] = jnp.zeros((sums.shape[0] - 384, 128), F32)
        put_sums(sums, gp[...], u[...], st[...], z1[...])

    m = h * n
    return call(
        body, [near(512, 128, dtype=F32)], 100000 * m, "upper_sums",
        *mids, *taps, *gpres, *z1s, top, skip,
        scratch=[pltpu.VMEM((k, m), BF16) for k in (128, 128, 256, 128)],
    )[0]


def upper_outputs(n, mids, z0s, z1s, v, vb):
    h = len(mids)

    def body(*refs):
        mids, z0s, z1s = (refs[i * h : i * h + h] for i in range(3))
        v, vb, x_top, skip_sum = refs[3 * h :]
        both = jnp.concatenate([v[0, 64:, :], v[1, 64:, :]], axis=1)
        both_bias = vb[64:, 0:1] + vb[64:, 1:2]
        for i in range(h):
            for s in tiles(n):
                at = shift(s, i * n)
                z = z1s[i][:, s]
                own = mids[i][:, s].astype(F32) + mm(v[1, :64, :], z) + vb[:64, 1:2]
                x_top[0, :, at] = own.astype(BF16)
                zz = jnp.concatenate([z0s[i][:, s], z], axis=0)
                skip_sum[0, :, at] = (mm(both, zz) + both_bias).astype(BF16)

    m = h * n
    out = [jax.ShapeDtypeStruct((1, 64, m), BF16)] * 2
    return call(body, out, 50000 * m, "upper_outputs", *mids, *z0s, *z1s, v, vb)


def lower_backward(off, n, gdel, gpre1, signal, tap, z0, top, skip, w, b, wt, vt, before):
    def body(gdel, gpre1, sig, tap, z0, top, skip, w, b, wt, vt, *rest):
        rest, (u, st, gp) = rest[:-3], rest[-3:]
        gdel_out, part = rest[len(before) : len(before) + 2]
        if before:
            gdel_out[:, :off] = rest[0][...]
        for s in tiles(n):
            at = shift(s, off)
            own = top[0, :, at].astype(F32) + mm(wt[1, 64:, :], gpre1[:, s])
            grad = (own + gdel[:, s].astype(F32)).astype(BF16)
            both = jnp.concatenate([grad, skip[0, :, at]], axis=0)
            u[:, s] = both
            stacked = jnp.concatenate([tap[:, s], sig[0, :, at]], axis=0)
            st[:, s] = stacked
            filt, gate = gates(w[0], stacked, b[:, 0:1])
            gpre = gate_grad(mm(vt[0], both), filt, gate)
            gp[:, s] = gpre
            gin = mm(wt[0], gpre)
            gdel_out[:, shift(s, gdel_out.shape[1] - n)] = gin[:64].astype(BF16)
            part[:, s] = grad.astype(F32) + gin[64:]
        if before:
            _, sums, high, _, _, give, keep = rest
            put_sums(keep, gp[...], u[...], st[...], z0[...], sums)
            keep[387:, :] = jnp.zeros((keep.shape[0] - 387, 128), F32)
            low, high = keep[...], high[...]
            own = jnp.broadcast_to(lax.axis_index("core") == 0, low.shape)
            give[...] = jnp.where(own, high, low)
            keep[...] = jnp.where(own, low, high)
        else:
            put_sums(rest[-1], gp[...], u[...], st[...], z0[...])

    out = [near(64, off + n), near(64, n, dtype=F32)]
    out += [near(512, 128, dtype=F32)] * (2 if before else 1)
    return call(
        body, out, 320000 * n, "lower_backward",
        gdel, gpre1, signal, tap, z0, top, skip, w, b, wt, vt, *before,
        scratch=[pltpu.VMEM((k, n), BF16) for k in (128, 128, 256)],
    )


def place(held, other):
    def body(held, other, conv, conv_bias, proj, proj_bias):
        a, b = held[...], other[...]
        own = jnp.broadcast_to(lax.axis_index("core") == 0, a.shape)
        for layer, rows in enumerate((jnp.where(own, a, b), jnp.where(own, b, a))):
            conv[layer] = rows[:256]
            proj[layer] = rows[256:384]
            conv_bias[layer : layer + 1, :128] = rows[384:385]
            conv_bias[layer : layer + 1, 128:] = rows[385:386]
            proj_bias[layer : layer + 1, :] = rows[386:387]

    out = [jax.ShapeDtypeStruct(d, F32) for d in ((2, 256, 128), (2, 256), (2, 128, 128), (2, 128))]
    return call(body, out, 1000, "place", held, other)


def swap_cores(block):
    return lax.ppermute(block, "core", [(0, 1), (1, 0)])


def add(x, y):
    def body(x, y, out):
        out[...] = x[...] + y[...]

    return call(body, [near(*x.shape, dtype=F32)], 1000, "add", x, y)[0]


def finish(parts, later):
    n = parts[0].shape[1]

    def body(*refs):
        far, out = refs[-2:]
        for i, own in enumerate(refs[:-2]):
            at = slice(i * n, i * n + n)
            out[0, :, at] = (own[...] + far[:, at].astype(F32)).astype(BF16)

    return call(body, [near(1, *later.shape)], 1000, "finish", *parts, later)[0]


def share_out(parts, copies, scale=1.0):
    def body(parts, out):
        total = parts[0]
        for i in range(1, parts.shape[0]):
            total += parts[i]
        total *= scale
        for i in range(copies):
            out[i] = total

    out = [near(copies, *parts.shape[1:], dtype=F32)]
    return call(body, out, 1000, "share_out", parts)[0]


def on_device(signal, w, b, v, vb, top, skip):
    m = signal.shape[2]
    n = m // HALVES
    offs = range(0, m, n)
    taps = [from_behind(signal[0, :, o : o + n], 1) for o in offs]
    b, vb, wt, vt = prepare(w, b, v, vb)
    mids, z0s, mid_taps = [], [], []
    for o, tap in zip(offs, taps):
        mid, z0 = lower_forward(o, n, signal, tap, w, b, v, vb)
        mids.append(mid)
        z0s.append(z0)
        mid_taps.append(from_behind(mid, 2))
    z1s, gpres1, gdels1 = [], [], []
    for o, mid, tap in zip(offs, mids, mid_taps):
        z1, gpre1, gdel = upper_critical(o, n, mid, tap, top, skip, w, b, wt, vt)
        z1s.append(z1)
        gpres1.append(gpre1)
        gdels1.append(from_behind(gdel, -2))
    args = [(o, n, d, g, signal, t, z, top, skip, w, b, wt, vt)
            for o, d, g, t, z in zip(offs, gdels1, gpres1, taps, z0s)]
    gdel_a, part_a, sums = lower_backward(*args[0], [])
    z1s, sums = lax.optimization_barrier((z1s, sums))
    high = upper_sums(n, mids, mid_taps, gpres1, z1s, top, skip)
    gdel0, part_b, give, keep = lower_backward(*args[1], [gdel_a, sums, high])
    count = signal.shape[0] * lax.axis_size(CORNER) * m * lax.axis_size(TM)
    plane, depth = lax.axis_size(PLANE), lax.axis_size("z")
    scale = 1.0 / math.sqrt(count)
    rows = add(keep, swap_cores(give)).reshape(plane, -1, 128)
    rows, gdel0 = lax.optimization_barrier((rows, gdel0))
    later = from_behind(gdel0, -1)
    parts = lax.all_to_all(rows, PLANE, 0, 0, tiled=True)
    x_top, skip_sum = upper_outputs(n, mids, z0s, z1s, v, vb)
    parts, x_top, skip_sum = lax.optimization_barrier((parts, x_top, skip_sum))
    parts = share_out(parts, depth)
    parts = lax.all_to_all(parts, "z", 0, 0, tiled=True)
    parts = share_out(parts, plane, scale)
    held = lax.all_to_all(parts, PLANE, 0, 0, tiled=True).reshape(give.shape)
    grad_input = finish([part_a, part_b], later)
    return (x_top, skip_sum, grad_input, *place(held, swap_cores(held)))


def solution(mesh):
    fine = Mesh(mesh.devices.reshape(4, 2, 2, 8, 2), ("y", "xl", "core", "z", "xh"))
    field = P(CORNER, None, TM)
    return jax.shard_map(
        on_device,
        mesh=fine,
        in_specs=(field, P(), P(), P(), P(), field, field),
        out_specs=(field, field, field, P(), P(), P(), P()),
        check_vma=False,
    )
```

time: 114 us -> 97.1 us (0.85)
  waiting for transfers between devices: 10.6 us -> 21 us
  starting transfers between devices: 50.6 us -> 43.2 us
  blocking collectives: 19.6 us -> 12.4 us
  local copies, waits for them, and re-layouts: 8.48 us -> 1.97 us
  other arithmetic: 5.39 us -> 0 us
    all_to_all x1, blocking collectives: 19.6 us -> 12.4 us  [on_device(): held = lax.all_to_all(parts, PLANE, 0, 0, tiled=True).reshape(give.shape)]
    ppermute x7, waiting for transfers between devices: 0.63 us -> 7.19 us  [from_behind(): return lax.ppermute(block, TM, route)]
    unnamed x42 -> x22, local copies, waits for them, and re-layouts: 7 us -> 0.84 us
    ppermute x3 -> x2, starting transfers between devices: 9.95 us -> 4.77 us  [swap_cores(): return lax.ppermute(block, 'core', [(0, 1), (1, 0)])]
    all_to_all x1 -> x2, waiting for transfers between devices: 8.57 us -> 12.3 us  [the longest x1 6.59 us: on_device(): parts = lax.all_to_all(parts, 'z', 0, 0, tiled=True)]
    another operation x4 -> x0, other arithmetic: 2.54 us -> none  [on_device(): jnp.stack(pair)]
    all_to_all x1 -> x2, starting transfers between devices: 17.7 us -> 15.4 us  [the longest x1 9.79 us: on_device(): parts = lax.all_to_all(parts, 'z', 0, 0, tiled=True)]
    select_n x2 -> x0, other arithmetic: 1.82 us -> none  [the longest x1 1.78 us: on_device(): jnp.where(first, low[0] + low_other, high + high_other)]
  transfers between devices with their start and end apart: 11 -> 11, of which waited for: 4 -> 8; matrix products, arithmetic and copies ran while one was open for 1% -> 0% of each run, Pallas kernels for 16% -> 13%
where the time goes in v3:
time: 97.1 us; the launch traced here: 96.5 us
  starting transfers between devices  43.2 us (44%)
  waiting for transfers between devices  21 us (22%)
  Pallas kernels  17 us (18%)
  blocking collectives  12.4 us (13%)
  local copies, waits for them, and re-layouts  1.97 us (2%)
    ppermute x7, starting transfers between devices, from_behind(): return lax.ppermute(block, TM, route)  23.1 us
    pallas_call x14, Pallas kernels, call(): pl.pallas_call(body, out_shape=out, in_specs=[spec] * len(args), out_spec...  17 us
    all_to_all x1, blocking collectives, on_device(): held = lax.all_to_all(parts, PLANE, 0, 0, tiled=True).reshape(give.shape)  12.4 us
    all_to_all x1, starting transfers between devices, on_device(): parts = lax.all_to_all(parts, 'z', 0, 0, tiled=True)  9.79 us
    ppermute x7, waiting for transfers between devices, from_behind(): return lax.ppermute(block, TM, route)  7.19 us
    all_to_all x1, waiting for transfers between devices, on_device(): parts = lax.all_to_all(parts, 'z', 0, 0, tiled=True)  6.59 us
    all_to_all x1, waiting for transfers between devices, on_device(): parts = lax.all_to_all(rows, PLANE, 0, 0, tiled=True)  5.75 us
    all_to_all x1, starting transfers between devices, on_device(): parts = lax.all_to_all(rows, PLANE, 0, 0, tiled=True)  5.59 us
  transfers between devices with their start and end apart: 11, of which 8 were waited for; matrix products, arithmetic and copies ran while one was open for 0% of the time, Pallas kernels for 13%

profile of v3, /device:TPU:1, one launch (start us, length us, event | category | flops | bytes accessed | tf_op | source)
XLA Modules:
  0.0 96.5 jit_solution(3862689965581720559)
XLA Ops:
  0.7 1.1 %slice_bitcast_fusion = (bf16[64,2048]{1,0:T(8,128)(2,1)S(1)}, bf16[64,2048]{1,0:T(8,128)(2,1)S(1)}) fusion(bf16[1,64,4096]{2,1,0:T(8,128)(2,1)} %sig.7), kind=kLoop, calls=%fused_computation | loop fusion | bytes 1048576 | tf_op jit(solution)/shard_map/squeeze | solution.py:263
  1.8 0.0 copy-start.7
  1.8 0.0 copy-start.8
  1.8 5.5 %collective-permute-start.3 = (bf16[64,2048]{1,0:T(8,128)(2,1)S(1)}, bf16[64,2048]{1,0:T(8,128)(2,1)S(1)}, u32[]{:S(2)}, u32[]{:S(2)}) collective-permute-start(bf16[64,2048]{1,0:T(8,128)(2,1)S(1)} %get-tuple-element.77), channel_id=1, source_target_pairs={{0,1},{1,2},{2,3},{3,4},{4,5},{5,6},{6,7},{7,8},{8,9},{9,10},{10,1... | collective-permute-start | bytes 786440 | tf_op jit(solution)/shard_map/ppermute | solution.py:21
  7.3 3.5 %collective-permute-start = (bf16[64,2048]{1,0:T(8,128)(2,1)S(1)}, bf16[64,2048]{1,0:T(8,128)(2,1)S(1)}, u32[]{:S(2)}, u32[]{:S(2)}) collective-permute-start(bf16[64,2048]{1,0:T(8,128)(2,1)S(1)} %get-tuple-element.78), channel_id=1, source_target_pairs={{0,1},{1,2},{2,3},{3,4},{4,5},{5,6},{6,7},{7,8},{8,9},{9,10},{10,1... | collective-permute-start | bytes 786440 | tf_op jit(solution)/shard_map/ppermute | solution.py:21
  10.8 0.0 copy-done.3
  10.8 0.0 copy-done.4
  10.8 0.0 copy-done.7
  10.9 0.0 copy-done.8
  10.9 0.2 prepare.1
  11.1 1.2 %collective-permute-done.3.tap = bf16[64,2048]{1,0:T(8,128)(2,1)S(1)} collective-permute-done((bf16[64,2048]{1,0:T(8,128)(2,1)S(1)}, bf16[64,2048]{1,0:T(8,128)(2,1)S(1)}, u32[]{:S(2)}, u32[]{:S(2)}) %collective-permute-start.3) | collective-permute-done | bytes 262176 | tf_op jit(solution)/shard_map/ppermute | solution.py:21
  12.3 1.2 %lower_forward.3 = (bf16[64,2048]{1,0:T(8,128)(2,1)S(1)}, bf16[128,2048]{1,0:T(8,128)(2,1)S(1)}) custom-call(bf16[1,64,4096]{2,1,0:T(8,128)(2,1)S(1)} %copy-done, bf16[64,2048]{1,0:T(8,128)(2,1)S(1)} %collective-permute-done.3.tap, bf16[2,256,128]{2,1,0:T(8,128)(2,1)S(1)} %copy-done.3, f32[256,8]{1,0:T(8,128)S(1)} %get-tuple-element.42.b, ...), custom_call_target="tpu_custom_call" | custom-call | flops 184320000 | bytes 1781760 | tf_op jit(solution)/shard_map/lower_forward/pallas_call | solution.py:56
  13.4 0.0 copy-start.2
  13.4 5.5 %collective-permute-start.4 = (bf16[64,2048]{1,0:T(8,128)(2,1)S(1)}, bf16[64,2048]{1,0:T(8,128)(2,1)S(1)}, u32[]{:S(2)}, u32[]{:S(2)}) collective-permute-start(bf16[64,2048]{1,0:T(8,128)(2,1)S(1)} %get-tuple-element.50.mid.refs_0_), channel_id=1, source_target_pairs={{0,2},{1,3},{2,4},{3,5},{4,6},{5,7},{6,8},{7,9},{8,10},{9,11},{10,... | collective-permute-start | bytes 786440 | tf_op jit(solution)/shard_map/ppermute | solution.py:21
  19.0 0.0 collective-permute-done.tap
  19.0 1.1 %lower_forward.2 = (bf16[64,2048]{1,0:T(8,128)(2,1)S(1)}, bf16[128,2048]{1,0:T(8,128)(2,1)S(1)}) custom-call(bf16[1,64,4096]{2,1,0:T(8,128)(2,1)S(1)} %copy-done, bf16[64,2048]{1,0:T(8,128)(2,1)S(1)} %collective-permute-done.tap, bf16[2,256,128]{2,1,0:T(8,128)(2,1)S(1)} %copy-done.3, f32[256,8]{1,0:T(8,128)S(1)} %get-tuple-element.42.b, ...), custom_call_target="tpu_custom_call" | custom-call | flops 184320000 | bytes 1781760 | tf_op jit(solution)/shard_map/lower_forward/pallas_call | solution.py:56
  20.2 4.5 %collective-permute-start.1 = (bf16[64,2048]{1,0:T(8,128)(2,1)S(1)}, bf16[64,2048]{1,0:T(8,128)(2,1)S(1)}, u32[]{:S(2)}, u32[]{:S(2)}) collective-permute-start(bf16[64,2048]{1,0:T(8,128)(2,1)S(1)} %get-tuple-element.44.mid.refs_1_), channel_id=1, source_target_pairs={{0,2},{1,3},{2,4},{3,5},{4,6},{5,7},{6,8},{7,9},{8,10},{9,11},{10,... | collective-permute-start | bytes 786440 | tf_op jit(solution)/shard_map/ppermute | solution.py:21
  24.7 0.0 collective-permute-done.4.tap.refs_2_
  24.7 1.5 %upper_critical.3 = (bf16[128,2048]{1,0:T(8,128)(2,1)S(1)}, bf16[256,2048]{1,0:T(8,128)(2,1)S(1)}, bf16[64,2048]{1,0:T(8,128)(2,1)S(1)}) custom-call(bf16[64,2048]{1,0:T(8,128)(2,1)S(1)} %get-tuple-element.50.mid.refs_0_, bf16[64,2048]{1,0:T(8,128)(2,1)S(1)} %collective-permute-done.4.tap.refs_2_, bf16[1,64,4096]{2,1,0:T(8,128)(2,1)S(1)} %copy-done.1, ...), custom_call_target="tpu_custom_call" | custom-call | flops 266240000 | bytes 3743744 | tf_op jit(solution)/shard_map/upper_critical/pallas_call | solution.py:56
  26.2 1.3 %collective-permute-start.5 = (bf16[64,2048]{1,0:T(8,128)(2,1)S(1)}, bf16[64,2048]{1,0:T(8,128)(2,1)S(1)}, u32[]{:S(2)}, u32[]{:S(2)}) collective-permute-start(bf16[64,2048]{1,0:T(8,128)(2,1)S(1)} %get-tuple-element.51), channel_id=1, source_target_pairs={{2,0},{3,1},{4,2},{5,3},{6,4},{7,5},{8,6},{9,7},{10,8},{11,9},{12,... | collective-permute-start | bytes 786440 | tf_op jit(solution)/shard_map/ppermute | solution.py:21
  27.5 1.1 %collective-permute-done.1.tap.refs_3_ = bf16[64,2048]{1,0:T(8,128)(2,1)S(1)} collective-permute-done((bf16[64,2048]{1,0:T(8,128)(2,1)S(1)}, bf16[64,2048]{1,0:T(8,128)(2,1)S(1)}, u32[]{:S(2)}, u32[]{:S(2)}) %collective-permute-start.1) | collective-permute-done | bytes 262176 | tf_op jit(solution)/shard_map/ppermute | solution.py:21
  28.6 1.5 %upper_critical.2 = (bf16[128,2048]{1,0:T(8,128)(2,1)S(1)}, bf16[256,2048]{1,0:T(8,128)(2,1)S(1)}, bf16[64,2048]{1,0:T(8,128)(2,1)S(1)}) custom-call(bf16[64,2048]{1,0:T(8,128)(2,1)S(1)} %get-tuple-element.44.mid.refs_1_, bf16[64,2048]{1,0:T(8,128)(2,1)S(1)} %collective-permute-done.1.tap.refs_3_, bf16[1,64,4096]{2,1,0:T(8,128)(2,1)S(1)} %copy-done.1, ...), custom_call_target="tpu_custom_call" | custom-call | flops 266240000 | bytes 3743744 | tf_op jit(solution)/shard_map/upper_critical/pallas_call | solution.py:56
  30.0 1.3 %collective-permute-start.2 = (bf16[64,2048]{1,0:T(8,128)(2,1)S(1)}, bf16[64,2048]{1,0:T(8,128)(2,1)S(1)}, u32[]{:S(2)}, u32[]{:S(2)}) collective-permute-start(bf16[64,2048]{1,0:T(8,128)(2,1)S(1)} %get-tuple-element.47), channel_id=1, source_target_pairs={{2,0},{3,1},{4,2},{5,3},{6,4},{7,5},{8,6},{9,7},{10,8},{11,9},{12,... | collective-permute-start | bytes 786440 | tf_op jit(solution)/shard_map/ppermute | solution.py:21
  31.3 3.0 %collective-permute-done.5.gdel = bf16[64,2048]{1,0:T(8,128)(2,1)S(1)} collective-permute-done((bf16[64,2048]{1,0:T(8,128)(2,1)S(1)}, bf16[64,2048]{1,0:T(8,128)(2,1)S(1)}, u32[]{:S(2)}, u32[]{:S(2)}) %collective-permute-start.5) | collective-permute-done | bytes 262176 | tf_op jit(solution)/shard_map/ppermute | solution.py:21
  34.3 2.6 %lower_backward.2 = (bf16[64,2048]{1,0:T(8,128)(2,1)S(1)}, f32[64,2048]{1,0:T(8,128)S(1)}, f32[512,128]{1,0:T(8,128)S(1)}) custom-call(bf16[64,2048]{1,0:T(8,128)(2,1)S(1)} %collective-permute-done.5.gdel, bf16[256,2048]{1,0:T(8,128)(2,1)S(1)} %get-tuple-element.52.gpre1.refs_4_, bf16[1,64,4096]{2,1,0:T(8,128)(2,1)S(1)} %copy-done, ...), custom_call_target="tpu_custom_call" | custom-call | flops 655360000 | bytes 5054464 | tf_op jit(solution)/shard_map/lower_backward/pallas_call | solution.py:56
  36.9 1.8 %upper_sums.1.rest_2_ = f32[512,128]{1,0:T(8,128)S(1)} custom-call(bf16[64,2048]{1,0:T(8,128)(2,1)S(1)} %get-tuple-element.50.mid.refs_0_, bf16[64,2048]{1,0:T(8,128)(2,1)S(1)} %get-tuple-element.44.mid.refs_1_, bf16[64,2048]{1,0:T(8,128)(2,1)S(1)} %collective-permute-done.4.tap.refs_2_, bf16[64,2048]{1,0:T(8,128)(2,1)S(1)} %collective-permute-done.1.tap.refs_3_, ...), custom_call_target="tpu_custom_call" | custom-call | flops 409600000 | bytes 5505024 | tf_op jit(solution)/shard_map/upper_sums/pallas_call | solution.py:56
  38.6 2.0 %collective-permute-done.2.gdel = bf16[64,2048]{1,0:T(8,128)(2,1)S(1)} collective-permute-done((bf16[64,2048]{1,0:T(8,128)(2,1)S(1)}, bf16[64,2048]{1,0:T(8,128)(2,1)S(1)}, u32[]{:S(2)}, u32[]{:S(2)}) %collective-permute-start.2) | collective-permute-done | bytes 262176 | tf_op jit(solution)/shard_map/ppermute | solution.py:21
  40.6 2.6 %lower_backward.3 = (bf16[64,4096]{1,0:T(8,128)(2,1)S(1)}, f32[64,2048]{1,0:T(8,128)S(1)}, f32[512,128]{1,0:T(8,128)S(1)}, f32[512,128]{1,0:T(8,128)S(1)}) custom-call(bf16[64,2048]{1,0:T(8,128)(2,1)S(1)} %collective-permute-done.2.gdel, bf16[256,2048]{1,0:T(8,128)(2,1)S(1)} %get-tuple-element.48.refs_5_.gpre1, bf16[1,64,4096]{2,1,0:T(8,128)(2,1)S(1)} %copy-done, ...), custom_call_target="tpu_custom_call" | custom-call | flops 655360000 | bytes 6365184 | tf_op jit(solution)/shard_map/lower_backward/pallas_call | solution.py:56
  43.2 0.0 copy-start.5
  43.2 0.8 copy-done.5
  44.0 2.0 %collective-permute-start.6 = (f32[512,128]{1,0:T(8,128)S(1)}, f32[512,128]{1,0:T(8,128)S(1)}, u32[]{:S(2)}, u32[]{:S(2)}) collective-permute-start(f32[512,128]{1,0:T(8,128)S(1)} %get-tuple-element.62), channel_id=1, source_target_pairs={{0,16},{16,0},{1,17},{17,1},{2,18},{18,2},{3,19},{19,3},{4,20},{20... | collective-permute-start | bytes 786440 | tf_op jit(solution)/shard_map/ppermute | solution.py:224
  46.0 1.2 %collective-permute-done.6.y = f32[512,128]{1,0:T(8,128)S(1)} collective-permute-done((f32[512,128]{1,0:T(8,128)S(1)}, f32[512,128]{1,0:T(8,128)S(1)}, u32[]{:S(2)}, u32[]{:S(2)}) %collective-permute-start.6) | collective-permute-done | bytes 262176 | tf_op jit(solution)/shard_map/ppermute | solution.py:224
  47.2 0.7 add.1
  47.9 5.6 %all-to-all-start = ((f32[16,32,128]{2,1,0:T(8,128)}), f32[16,32,128]{2,1,0:T(8,128)S(1)}, u32[]{:S(2)}, u32[]{:S(2)}) async-start(f32[16,32,128]{2,1,0:T(8,128)} %bitcast.2), calls=%async_computation | async-start | bytes 524288 | tf_op jit(solution)/shard_map/all_to_all | solution.py:289
  53.5 1.6 %upper_outputs.1 = (bf16[1,64,4096]{2,1,0:T(8,128)(2,1)}, bf16[1,64,4096]{2,1,0:T(8,128)(2,1)}) custom-call(bf16[64,2048]{1,0:T(8,128)(2,1)S(1)} %get-tuple-element.50.mid.refs_0_, bf16[64,2048]{1,0:T(8,128)(2,1)S(1)} %get-tuple-element.44.mid.refs_1_, bf16[128,2048]{1,0:T(8,128)(2,1)S(1)} %get-tuple-element.53.z0.refs_2_, ...), custom_call_target="tpu_custom_call" | custom-call | flops 204800000 | bytes 3739648 | tf_op jit(solution)/shard_map/upper_outputs/pallas_call | solution.py:56
  55.1 5.8 %all-to-all-done.parts = f32[16,32,128]{2,1,0:T(8,128)S(1)} async-done(((f32[16,32,128]{2,1,0:T(8,128)}), f32[16,32,128]{2,1,0:T(8,128)S(1)}, u32[]{:S(2)}, u32[]{:S(2)}) %all-to-all-start) | async-done | bytes 262176 | tf_op jit(solution)/shard_map/all_to_all | solution.py:289
  60.9 0.7 share_out.2
  61.6 9.8 %all-to-all-start.1 = ((f32[8,32,128]{2,1,0:T(8,128)}), f32[8,32,128]{2,1,0:T(8,128)S(1)}, u32[]{:S(2)}, u32[]{:S(2)}) async-start(f32[8,32,128]{2,1,0:T(8,128)} %share_out.2), calls=%async_computation.1 | async-start | bytes 262144 | tf_op jit(solution)/shard_map/all_to_all | solution.py:293
  71.4 0.0 copy-done.10
  71.4 0.0 copy-start.6
  71.4 1.4 %collective-permute-start.7 = (bf16[64,4096]{1,0:T(8,128)(2,1)S(1)}, bf16[64,4096]{1,0:T(8,128)(2,1)S(1)}, u32[]{:S(2)}, u32[]{:S(2)}) collective-permute-start(bf16[64,4096]{1,0:T(8,128)(2,1)S(1)} %copy-done.10), channel_id=1, source_target_pairs={{1,0},{2,1},{3,2},{4,3},{5,4},{6,5},{7,6},{8,7},{9,8},{10,9},{11,1... | collective-permute-start | bytes 1572872 | tf_op jit(solution)/shard_map/ppermute | solution.py:21
  72.8 6.6 %all-to-all-done.1.parts = f32[8,32,128]{2,1,0:T(8,128)S(1)} async-done(((f32[8,32,128]{2,1,0:T(8,128)}), f32[8,32,128]{2,1,0:T(8,128)S(1)}, u32[]{:S(2)}, u32[]{:S(2)}) %all-to-all-start.1) | async-done | bytes 131104 | tf_op jit(solution)/shard_map/all_to_all | solution.py:293
  79.4 12.4 %all_to_all.15 = f32[16,32,128]{2,1,0:T(8,128)S(1)} all-to-all(f32[16,32,128]{2,1,0:T(8,128)S(1)} %share_out.3), channel_id=1, replica_groups=mesh['y'=4,'xl'=2,'core'=2,'z'=8,'xh'=2] {'y','xl','xh'}, dimensions={0} | all-to-all | bytes 524288 | tf_op jit(solution)/shard_map/all_to_all | solution.py:295
  91.8 2.7 %collective-permute-start.8 = (f32[512,128]{1,0:T(8,128)S(1)}, f32[512,128]{1,0:T(8,128)S(1)}, u32[]{:S(2)}, u32[]{:S(2)}) collective-permute-start(f32[512,128]{1,0:T(8,128)S(1)} %bitcast.6), channel_id=1, source_target_pairs={{0,16},{16,0},{1,17},{17,1},{2,18},{18,2},{3,19},{19,3},{4,20},{20... | collective-permute-start | bytes 786440 | tf_op jit(solution)/shard_map/ppermute | solution.py:224
  94.5 0.0 collective-permute-done.7.refs_2_
  94.6 0.9 finish.1
  95.4 0.3 collective-permute-done.8.other
  95.7 0.8 place.1
  (12 shorter events, 0.0 us)
Async XLA Ops:
  0.6 11.6 %copy-start = (bf16[1,64,4096]{2,1,0:T(8,128)(2,1)S(1)}, bf16[1,64,4096]{2,1,0:T(8,128)(2,1)}, u32[]{:S(2)}) copy-start(bf16[1,64,4096]{2,1,0:T(8,128)(2,1)} %sig.7) | copy-start | bytes 1572868
  0.6 10.2 %copy-start.3 = (bf16[2,256,128]{2,1,0:T(8,128)(2,1)S(1)}, bf16[2,256,128]{2,1,0:T(8,128)(2,1)}, u32[]{:S(2)}) copy-start(bf16[2,256,128]{2,1,0:T(8,128)(2,1)} %w.13) | copy-start | bytes 393220
  0.7 10.2 %copy-start.4 = (bf16[2,128,128]{2,1,0:T(8,128)(2,1)S(1)}, bf16[2,128,128]{2,1,0:T(8,128)(2,1)}, u32[]{:S(2)}) copy-start(bf16[2,128,128]{2,1,0:T(8,128)(2,1)} %refs_6_.1) | copy-start | bytes 196612
  1.8 9.0 %copy-start.7 = (f32[2,256]{1,0:T(2,128)S(1)}, f32[2,256]{1,0:T(2,128)}, u32[]{:S(2)}) copy-start(f32[2,256]{1,0:T(2,128)} %b.1) | copy-start | bytes 6148
  1.8 9.0 %copy-start.8 = (f32[2,128]{1,0:T(2,128)S(1)}, f32[2,128]{1,0:T(2,128)}, u32[]{:S(2)}) copy-start(f32[2,128]{1,0:T(2,128)} %vb.1) | copy-start | bytes 3076
  1.8 10.4 %collective-permute-start.3 = (bf16[64,2048]{1,0:T(8,128)(2,1)S(1)}, bf16[64,2048]{1,0:T(8,128)(2,1)S(1)}, u32[]{:S(2)}, u32[]{:S(2)}) collective-permute-start(bf16[64,2048]{1,0:T(8,128)(2,1)S(1)} %get-tuple-element.77), channel_id=1, source_target_pairs={{0,1},{1,2},{2,3},{3,4},{4,5},{5,6},{6,7},{7,8},{8,9},{9,10},{10,1... | collective-permute-start | bytes 786440 | tf_op jit(solution)/shard_map/ppermute | solution.py:21
  7.3 11.7 %collective-permute-start = (bf16[64,2048]{1,0:T(8,128)(2,1)S(1)}, bf16[64,2048]{1,0:T(8,128)(2,1)S(1)}, u32[]{:S(2)}, u32[]{:S(2)}) collective-permute-start(bf16[64,2048]{1,0:T(8,128)(2,1)S(1)} %get-tuple-element.78), channel_id=1, source_target_pairs={{0,1},{1,2},{2,3},{3,4},{4,5},{5,6},{6,7},{7,8},{8,9},{9,10},{10,1... | collective-permute-start | bytes 786440 | tf_op jit(solution)/shard_map/ppermute | solution.py:21
  13.4 11.3 %copy-start.1 = (bf16[1,64,4096]{2,1,0:T(8,128)(2,1)S(1)}, bf16[1,64,4096]{2,1,0:T(8,128)(2,1)}, u32[]{:S(2)}) copy-start(bf16[1,64,4096]{2,1,0:T(8,128)(2,1)} %top.7) | copy-start | bytes 1572868
  13.4 11.3 %copy-start.2 = (bf16[1,64,4096]{2,1,0:T(8,128)(2,1)S(1)}, bf16[1,64,4096]{2,1,0:T(8,128)(2,1)}, u32[]{:S(2)}) copy-start(bf16[1,64,4096]{2,1,0:T(8,128)(2,1)} %skip.7) | copy-start | bytes 1572868
  13.4 11.3 %collective-permute-start.4 = (bf16[64,2048]{1,0:T(8,128)(2,1)S(1)}, bf16[64,2048]{1,0:T(8,128)(2,1)S(1)}, u32[]{:S(2)}, u32[]{:S(2)}) collective-permute-start(bf16[64,2048]{1,0:T(8,128)(2,1)S(1)} %get-tuple-element.50.mid.refs_0_), channel_id=1, source_target_pairs={{0,2},{1,3},{2,4},{3,5},{4,6},{5,7},{6,8},{7,9},{8,10},{9,11},{10,... | collective-permute-start | bytes 786440 | tf_op jit(solution)/shard_map/ppermute | solution.py:21
  20.2 8.4 %collective-permute-start.1 = (bf16[64,2048]{1,0:T(8,128)(2,1)S(1)}, bf16[64,2048]{1,0:T(8,128)(2,1)S(1)}, u32[]{:S(2)}, u32[]{:S(2)}) collective-permute-start(bf16[64,2048]{1,0:T(8,128)(2,1)S(1)} %get-tuple-element.44.mid.refs_1_), channel_id=1, source_target_pairs={{0,2},{1,3},{2,4},{3,5},{4,6},{5,7},{6,8},{7,9},{8,10},{9,11},{10,... | collective-permute-start | bytes 786440 | tf_op jit(solution)/shard_map/ppermute | solution.py:21
  26.2 8.1 %collective-permute-start.5 = (bf16[64,2048]{1,0:T(8,128)(2,1)S(1)}, bf16[64,2048]{1,0:T(8,128)(2,1)S(1)}, u32[]{:S(2)}, u32[]{:S(2)}) collective-permute-start(bf16[64,2048]{1,0:T(8,128)(2,1)S(1)} %get-tuple-element.51), channel_id=1, source_target_pairs={{2,0},{3,1},{4,2},{5,3},{6,4},{7,5},{8,6},{9,7},{10,8},{11,9},{12,... | collective-permute-start | bytes 786440 | tf_op jit(solution)/shard_map/ppermute | solution.py:21
  30.0 10.6 %collective-permute-start.2 = (bf16[64,2048]{1,0:T(8,128)(2,1)S(1)}, bf16[64,2048]{1,0:T(8,128)(2,1)S(1)}, u32[]{:S(2)}, u32[]{:S(2)}) collective-permute-start(bf16[64,2048]{1,0:T(8,128)(2,1)S(1)} %get-tuple-element.47), channel_id=1, source_target_pairs={{2,0},{3,1},{4,2},{5,3},{6,4},{7,5},{8,6},{9,7},{10,8},{11,9},{12,... | collective-permute-start | bytes 786440 | tf_op jit(solution)/shard_map/ppermute | solution.py:21
  43.2 0.8 copy-start.5
  44.0 3.9 %copy-start.9 = (bf16[64,4096]{1,0:T(8,128)(2,1)}, bf16[64,4096]{1,0:T(8,128)(2,1)S(1)}, u32[]{:S(2)}) copy-start(bf16[64,4096]{1,0:T(8,128)(2,1)S(1)} %get-tuple-element.71) | copy-start | bytes 1572868
  44.0 3.2 %collective-permute-start.6 = (f32[512,128]{1,0:T(8,128)S(1)}, f32[512,128]{1,0:T(8,128)S(1)}, u32[]{:S(2)}, u32[]{:S(2)}) collective-permute-start(f32[512,128]{1,0:T(8,128)S(1)} %get-tuple-element.62), channel_id=1, source_target_pairs={{0,16},{16,0},{1,17},{17,1},{2,18},{18,2},{3,19},{19,3},{4,20},{20... | collective-permute-start | bytes 786440 | tf_op jit(solution)/shard_map/ppermute | solution.py:224
  47.9 13.0 %all-to-all-start = ((f32[16,32,128]{2,1,0:T(8,128)}), f32[16,32,128]{2,1,0:T(8,128)S(1)}, u32[]{:S(2)}, u32[]{:S(2)}) async-start(f32[16,32,128]{2,1,0:T(8,128)} %bitcast.2), calls=%async_computation | async-start | bytes 524288 | tf_op jit(solution)/shard_map/all_to_all | solution.py:289
  55.1 16.2 %copy-start.10 = (bf16[64,4096]{1,0:T(8,128)(2,1)S(1)}, bf16[64,4096]{1,0:T(8,128)(2,1)}, u32[]{:S(2)}) copy-start(bf16[64,4096]{1,0:T(8,128)(2,1)} %copy-done.9) | copy-start | bytes 1572868
  61.6 17.8 %all-to-all-start.1 = ((f32[8,32,128]{2,1,0:T(8,128)}), f32[8,32,128]{2,1,0:T(8,128)S(1)}, u32[]{:S(2)}, u32[]{:S(2)}) async-start(f32[8,32,128]{2,1,0:T(8,128)} %share_out.2), calls=%async_computation.1 | async-start | bytes 262144 | tf_op jit(solution)/shard_map/all_to_all | solution.py:293
  71.4 23.2 %copy-start.6 = (f32[64,2048]{1,0:T(8,128)S(1)}, f32[64,2048]{1,0:T(8,128)}, u32[]{:S(2)}) copy-start(f32[64,2048]{1,0:T(8,128)} %copy-done.5) | copy-start | bytes 1572868
  71.4 23.2 %collective-permute-start.7 = (bf16[64,4096]{1,0:T(8,128)(2,1)S(1)}, bf16[64,4096]{1,0:T(8,128)(2,1)S(1)}, u32[]{:S(2)}, u32[]{:S(2)}) collective-permute-start(bf16[64,4096]{1,0:T(8,128)(2,1)S(1)} %copy-done.10), channel_id=1, source_target_pairs={{1,0},{2,1},{3,2},{4,3},{5,4},{6,5},{7,6},{8,7},{9,8},{10,9},{11,1... | collective-permute-start | bytes 1572872 | tf_op jit(solution)/shard_map/ppermute | solution.py:21
  91.8 3.9 %collective-permute-start.8 = (f32[512,128]{1,0:T(8,128)S(1)}, f32[512,128]{1,0:T(8,128)S(1)}, u32[]{:S(2)}, u32[]{:S(2)}) collective-permute-start(f32[512,128]{1,0:T(8,128)S(1)} %bitcast.6), channel_id=1, source_target_pairs={{0,16},{16,0},{1,17},{17,1},{2,18},{18,2},{3,19},{19,3},{4,20},{20... | collective-permute-start | bytes 786440 | tf_op jit(solution)/shard_map/ppermute | solution.py:224

commit v4 on v3

--- a/solution.py
+++ b/solution.py
@@ -11,7 +11,7 @@
 TM = ("z", "xh")
 PLANE = ("y", "xl", "xh")
 HALVES = 2
-TILE = 512
+TILE = 2048
 F32, BF16 = jnp.float32, jnp.bfloat16
 
 
@@ -50,7 +50,7 @@
     return slice(s.start + off, s.stop + off)
 
 
-def call(body, out, flops, name, *args, scratch=()):
+def call(body, out, flops, name, *args):
     size = sum(math.prod(a.shape) * a.dtype.itemsize for a in (*args, *out))
     spec = pl.BlockSpec(memory_space=pltpu.VMEM)
     return pl.pallas_call(
@@ -58,7 +58,6 @@
         out_shape=out,
         in_specs=[spec] * len(args),
         out_specs=[spec] * len(out),
-        scratch_shapes=scratch,
         name=name,
         cost_estimate=pl.CostEstimate(flops=flops, bytes_accessed=size, transcendentals=0),
         compiler_params=pltpu.CompilerParams(vmem_limit_bytes=12 * 2**20),
@@ -108,15 +107,14 @@
     return call(body, out, 130000 * n, "upper_critical", mid, tap, top, skip, w, b, wt, vt)
 
 
-def put_sums(out, gpre, u, stacked, z, before=None):
-    ones = jnp.ones((16, u.shape[1]), BF16)
-    bias, proj_bias = mm_t(ones, gpre), mm_t(ones, u)
-    rows = [
-        (0, mm_t(gpre, stacked)),
-        (256, mm_t(u, z)),
-        (384, jnp.concatenate([bias[:1, :128], bias[:1, 128:], proj_bias[:1]], axis=0)),
-    ]
-    for start, value in rows:
+def put_sums(out, pieces, before=None):
+    conv = sum(mm_t(gpre, stacked) for gpre, _, stacked, _ in pieces)
+    proj = sum(mm_t(u, z) for _, u, _, z in pieces)
+    bias = sum(jnp.sum(p[0].astype(F32), axis=1, keepdims=True) for p in pieces)
+    proj_bias = sum(jnp.sum(p[1].astype(F32), axis=1, keepdims=True) for p in pieces)
+    lane = lax.broadcasted_iota(jnp.int32, (128, 128), 1)
+    biases = jnp.where(lane == 0, bias[:128], jnp.where(lane == 1, bias[128:], proj_bias))
+    for start, value in ((0, conv), (256, proj), (384, jnp.where(lane < 3, biases, 0.0))):
         at = slice(start, start + value.shape[0])
         out[at, :] = value if before is None else before[at, :] + value
 
@@ -126,20 +124,19 @@
 
     def body(*refs):
         mids, taps, gpres, z1s = (refs[i * h : i * h + h] for i in range(4))
-        top, skip, sums, u, st, gp, z1 = refs[4 * h :]
-        u[:64, :], u[64:, :] = top[0], skip[0]
+        top, skip, sums = refs[4 * h :]
+        pieces = []
         for i in range(h):
             at = slice(i * n, i * n + n)
-            st[:64, at], st[64:, at] = taps[i][...], mids[i][...]
-            gp[:, at], z1[:, at] = gpres[i][...], z1s[i][...]
-        sums[384:, :] = jnp.zeros((sums.shape[0] - 384, 128), F32)
-        put_sums(sums, gp[...], u[...], st[...], z1[...])
+            u = jnp.concatenate([top[0, :, at], skip[0, :, at]], axis=0)
+            stacked = jnp.concatenate([taps[i][...], mids[i][...]], axis=0)
+            pieces.append((gpres[i][...], u, stacked, z1s[i][...]))
+        put_sums(sums, pieces)
 
     m = h * n
     return call(
         body, [near(512, 128, dtype=F32)], 100000 * m, "upper_sums",
         *mids, *taps, *gpres, *z1s, top, skip,
-        scratch=[pltpu.VMEM((k, m), BF16) for k in (128, 128, 256, 128)],
     )[0]
 
 
@@ -167,7 +164,7 @@
 
 def lower_backward(off, n, gdel, gpre1, signal, tap, z0, top, skip, w, b, wt, vt, before):
     def body(gdel, gpre1, sig, tap, z0, top, skip, w, b, wt, vt, *rest):
-        rest, (u, st, gp) = rest[:-3], rest[-3:]
+        pieces = []
         gdel_out, part = rest[len(before) : len(before) + 2]
         if before:
             gdel_out[:, :off] = rest[0][...]
@@ -176,32 +173,28 @@
             own = top[0, :, at].astype(F32) + mm(wt[1, 64:, :], gpre1[:, s])
             grad = (own + gdel[:, s].astype(F32)).astype(BF16)
             both = jnp.concatenate([grad, skip[0, :, at]], axis=0)
-            u[:, s] = both
             stacked = jnp.concatenate([tap[:, s], sig[0, :, at]], axis=0)
-            st[:, s] = stacked
             filt, gate = gates(w[0], stacked, b[:, 0:1])
             gpre = gate_grad(mm(vt[0], both), filt, gate)
-            gp[:, s] = gpre
+            pieces.append((gpre, both, stacked, z0[:, s]))
             gin = mm(wt[0], gpre)
             gdel_out[:, shift(s, gdel_out.shape[1] - n)] = gin[:64].astype(BF16)
             part[:, s] = grad.astype(F32) + gin[64:]
         if before:
             _, sums, high, _, _, give, keep = rest
-            put_sums(keep, gp[...], u[...], st[...], z0[...], sums)
-            keep[387:, :] = jnp.zeros((keep.shape[0] - 387, 128), F32)
+            put_sums(keep, pieces, sums)
             low, high = keep[...], high[...]
             own = jnp.broadcast_to(lax.axis_index("core") == 0, low.shape)
             give[...] = jnp.where(own, high, low)
             keep[...] = jnp.where(own, low, high)
         else:
-            put_sums(rest[-1], gp[...], u[...], st[...], z0[...])
+            put_sums(rest[-1], pieces)
 
     out = [near(64, off + n), near(64, n, dtype=F32)]
     out += [near(512, 128, dtype=F32)] * (2 if before else 1)
     return call(
         body, out, 320000 * n, "lower_backward",
         gdel, gpre1, signal, tap, z0, top, skip, w, b, wt, vt, *before,
-        scratch=[pltpu.VMEM((k, n), BF16) for k in (128, 128, 256)],
     )
 
 
@@ -212,9 +205,10 @@
         for layer, rows in enumerate((jnp.where(own, a, b), jnp.where(own, b, a))):
             conv[layer] = rows[:256]
             proj[layer] = rows[256:384]
-            conv_bias[layer : layer + 1, :128] = rows[384:385]
-            conv_bias[layer : layer + 1, 128:] = rows[385:386]
-            proj_bias[layer : layer + 1, :] = rows[386:387]
+            biases = jnp.transpose(rows[384:])
+            conv_bias[layer : layer + 1, :128] = biases[0:1]
+            conv_bias[layer : layer + 1, 128:] = biases[1:2]
+            proj_bias[layer : layer + 1, :] = biases[2:3]
 
     out = [jax.ShapeDtypeStruct(d, F32) for d in ((2, 256, 128), (2, 256), (2, 128, 128), (2, 128))]
     return call(body, out, 1000, "place", held, other)
@@ -274,12 +268,15 @@
         z1s.append(z1)
         gpres1.append(gpre1)
         gdels1.append(from_behind(gdel, -2))
-    args = [(o, n, d, g, signal, t, z, top, skip, w, b, wt, vt)
-            for o, d, g, t, z in zip(offs, gdels1, gpres1, taps, z0s)]
-    gdel_a, part_a, sums = lower_backward(*args[0], [])
+    args = lambda i: [(o, n, d, g, signal, t, z, top, skip, w, b, wt, vt)
+            for o, d, g, t, z in zip(offs, gdels1, gpres1, taps, z0s)][i]
+    gdel_a, part_a, sums = lower_backward(*args(0), [])
     z1s, sums = lax.optimization_barrier((z1s, sums))
     high = upper_sums(n, mids, mid_taps, gpres1, z1s, top, skip)
-    gdel0, part_b, give, keep = lower_backward(*args[1], [gdel_a, sums, high])
+    z1s, high = lax.optimization_barrier((z1s, high))
+    x_top, skip_sum = upper_outputs(n, mids, z0s, z1s, v, vb)
+    gdels1[1], x_top, skip_sum = lax.optimization_barrier((gdels1[1], x_top, skip_sum))
+    gdel0, part_b, give, keep = lower_backward(*args(1), [gdel_a, sums, high])
     count = signal.shape[0] * lax.axis_size(CORNER) * m * lax.axis_size(TM)
     plane, depth = lax.axis_size(PLANE), lax.axis_size("z")
     scale = 1.0 / math.sqrt(count)
@@ -287,8 +284,6 @@
     rows, gdel0 = lax.optimization_barrier((rows, gdel0))
     later = from_behind(gdel0, -1)
     parts = lax.all_to_all(rows, PLANE, 0, 0, tiled=True)
-    x_top, skip_sum = upper_outputs(n, mids, z0s, z1s, v, vb)
-    parts, x_top, skip_sum = lax.optimization_barrier((parts, x_top, skip_sum))
     parts = share_out(parts, depth)
     parts = lax.all_to_all(parts, "z", 0, 0, tiled=True)
     parts = share_out(parts, plane, scale)

time: 97.1 us -> 93.6 us (0.964)
  blocking collectives: 12.4 us -> 25.3 us
  starting transfers between devices: 43.2 us -> 37.9 us
  Pallas kernels: 17 us -> 11.9 us
  waiting for transfers between devices: 21 us -> 16 us
    all_to_all x0 -> x1, blocking collectives: none -> 12.9 us  [on_device(): parts = lax.all_to_all(rows, PLANE, 0, 0, tiled=True)]
    all_to_all x1 -> x0, waiting for transfers between devices: 5.75 us -> none  [on_device(): parts = lax.all_to_all(rows, PLANE, 0, 0, tiled=True)]
    all_to_all x1 -> x0, starting transfers between devices: 5.59 us -> none  [on_device(): parts = lax.all_to_all(rows, PLANE, 0, 0, tiled=True)]
    pallas_call x14, Pallas kernels: 17 us -> 11.9 us  [call(): pl.pallas_call(body, out_shape=out, in_specs=[spec] * len(args), out_spec...]
  transfers between devices with their start and end apart: 11 -> 10, of which waited for: 8 -> 7; matrix products, arithmetic and copies ran while one was open for 0% -> 0% of each run, Pallas kernels for 13% -> 9%
where the time goes in v4:
time: 93.6 us; the launch traced here: 93.2 us
  starting transfers between devices  37.9 us (40%)
  blocking collectives  25.3 us (27%)
  waiting for transfers between devices  16 us (17%)
  Pallas kernels  11.9 us (13%)
  local copies, waits for them, and re-layouts  1.17 us (1%)
    ppermute x7, starting transfers between devices, from_behind(): return lax.ppermute(block, TM, route)  23.4 us
    all_to_all x1, blocking collectives, on_device(): parts = lax.all_to_all(rows, PLANE, 0, 0, tiled=True)  12.9 us
    all_to_all x1, blocking collectives, on_device(): held = lax.all_to_all(parts, PLANE, 0, 0, tiled=True).reshape(give.shape)  12.4 us
    pallas_call x14, Pallas kernels, call(): pl.pallas_call(body, out_shape=out, in_specs=[spec] * len(args), out_spec...  11.9 us
    all_to_all x1, starting transfers between devices, on_device(): parts = lax.all_to_all(parts, 'z', 0, 0, tiled=True)  9.66 us
    ppermute x7, waiting for transfers between devices, from_behind(): return lax.ppermute(block, TM, route)  7.81 us
    all_to_all x1, waiting for transfers between devices, on_device(): parts = lax.all_to_all(parts, 'z', 0, 0, tiled=True)  6.75 us
    ppermute x2, starting transfers between devices, swap_cores(): return lax.ppermute(block, 'core', [(0, 1), (1, 0)])  4.86 us
  transfers between devices with their start and end apart: 10, of which 7 were waited for; matrix products, arithmetic and copies ran while one was open for 0% of the time, Pallas kernels for 9%

profile of v4, /device:TPU:1, one launch (start us, length us, event | category | flops | bytes accessed | tf_op | source)
XLA Modules:
  0.0 93.2 jit_solution(4520898735449013994)
XLA Ops:
  0.6 0.0 copy-start
  0.6 0.0 copy-start.3
  0.7 0.0 copy-start.4
  0.7 1.1 %slice_bitcast_fusion = (bf16[64,2048]{1,0:T(8,128)(2,1)S(1)}, bf16[64,2048]{1,0:T(8,128)(2,1)S(1)}) fusion(bf16[1,64,4096]{2,1,0:T(8,128)(2,1)} %sig.7), kind=kLoop, calls=%fused_computation | loop fusion | bytes 1048576 | tf_op jit(solution)/shard_map/squeeze | solution.py:257
  1.8 0.0 copy-start.5
  1.8 0.0 copy-start.6
  1.8 5.5 %collective-permute-start.3 = (bf16[64,2048]{1,0:T(8,128)(2,1)S(1)}, bf16[64,2048]{1,0:T(8,128)(2,1)S(1)}, u32[]{:S(2)}, u32[]{:S(2)}) collective-permute-start(bf16[64,2048]{1,0:T(8,128)(2,1)S(1)} %get-tuple-element.83), channel_id=1, source_target_pairs={{0,1},{1,2},{2,3},{3,4},{4,5},{5,6},{6,7},{7,8},{8,9},{9,10},{10,1... | collective-permute-start | bytes 786440 | tf_op jit(solution)/shard_map/ppermute | solution.py:21
  7.3 3.5 %collective-permute-start = (bf16[64,2048]{1,0:T(8,128)(2,1)S(1)}, bf16[64,2048]{1,0:T(8,128)(2,1)S(1)}, u32[]{:S(2)}, u32[]{:S(2)}) collective-permute-start(bf16[64,2048]{1,0:T(8,128)(2,1)S(1)} %get-tuple-element.84), channel_id=1, source_target_pairs={{0,1},{1,2},{2,3},{3,4},{4,5},{5,6},{6,7},{7,8},{8,9},{9,10},{10,1... | collective-permute-start | bytes 786440 | tf_op jit(solution)/shard_map/ppermute | solution.py:21
  10.8 0.0 copy-done.3
  10.8 0.0 copy-done.4
  10.8 0.0 copy-done.5
  10.9 0.0 copy-done.6
  10.9 0.2 prepare.1
  11.1 1.2 %collective-permute-done.3.tap = bf16[64,2048]{1,0:T(8,128)(2,1)S(1)} collective-permute-done((bf16[64,2048]{1,0:T(8,128)(2,1)S(1)}, bf16[64,2048]{1,0:T(8,128)(2,1)S(1)}, u32[]{:S(2)}, u32[]{:S(2)}) %collective-permute-start.3) | collective-permute-done | bytes 262176 | tf_op jit(solution)/shard_map/ppermute | solution.py:21
  12.3 0.0 copy-done
  12.3 0.7 lower_forward.3
  13.0 0.0 copy-start.2
  13.0 5.5 %collective-permute-start.4 = (bf16[64,2048]{1,0:T(8,128)(2,1)S(1)}, bf16[64,2048]{1,0:T(8,128)(2,1)S(1)}, u32[]{:S(2)}, u32[]{:S(2)}) collective-permute-start(bf16[64,2048]{1,0:T(8,128)(2,1)S(1)} %get-tuple-element.51.mid.refs_0_), channel_id=1, source_target_pairs={{0,2},{1,3},{2,4},{3,5},{4,6},{5,7},{6,8},{7,9},{8,10},{9,11},{10,... | collective-permute-start | bytes 786440 | tf_op jit(solution)/shard_map/ppermute | solution.py:21
  18.5 0.0 collective-permute-done.tap
  18.5 0.7 lower_forward.2
  19.2 5.0 %collective-permute-start.1 = (bf16[64,2048]{1,0:T(8,128)(2,1)S(1)}, bf16[64,2048]{1,0:T(8,128)(2,1)S(1)}, u32[]{:S(2)}, u32[]{:S(2)}) collective-permute-start(bf16[64,2048]{1,0:T(8,128)(2,1)S(1)} %get-tuple-element.47.mid.refs_1_), channel_id=1, source_target_pairs={{0,2},{1,3},{2,4},{3,5},{4,6},{5,7},{6,8},{7,9},{8,10},{9,11},{10,... | collective-permute-start | bytes 786440 | tf_op jit(solution)/shard_map/ppermute | solution.py:21
  24.2 0.0 collective-permute-done.4.tap.refs_2_
  24.2 0.0 copy-done.1
  24.3 0.0 copy-done.2
  24.3 1.0 %upper_critical.3 = (bf16[128,2048]{1,0:T(8,128)(2,1)S(1)}, bf16[256,2048]{1,0:T(8,128)(2,1)S(1)}, bf16[64,2048]{1,0:T(8,128)(2,1)S(1)}) custom-call(bf16[64,2048]{1,0:T(8,128)(2,1)S(1)} %get-tuple-element.51.mid.refs_0_, bf16[64,2048]{1,0:T(8,128)(2,1)S(1)} %collective-permute-done.4.tap.refs_2_, bf16[1,64,4096]{2,1,0:T(8,128)(2,1)S(1)} %copy-done.1, ...), custom_call_target="tpu_custom_call" | custom-call | flops 266240000 | bytes 3743744 | tf_op jit(solution)/shard_map/upper_critical/pallas_call | solution.py:56
  25.3 1.3 %collective-permute-start.5 = (bf16[64,2048]{1,0:T(8,128)(2,1)S(1)}, bf16[64,2048]{1,0:T(8,128)(2,1)S(1)}, u32[]{:S(2)}, u32[]{:S(2)}) collective-permute-start(bf16[64,2048]{1,0:T(8,128)(2,1)S(1)} %get-tuple-element.56), channel_id=1, source_target_pairs={{2,0},{3,1},{4,2},{5,3},{6,4},{7,5},{8,6},{9,7},{10,8},{11,9},{12,... | collective-permute-start | bytes 786440 | tf_op jit(solution)/shard_map/ppermute | solution.py:21
  26.6 1.9 %collective-permute-done.1.tap.refs_3_ = bf16[64,2048]{1,0:T(8,128)(2,1)S(1)} collective-permute-done((bf16[64,2048]{1,0:T(8,128)(2,1)S(1)}, bf16[64,2048]{1,0:T(8,128)(2,1)S(1)}, u32[]{:S(2)}, u32[]{:S(2)}) %collective-permute-start.1) | collective-permute-done | bytes 262176 | tf_op jit(solution)/shard_map/ppermute | solution.py:21
  28.5 1.0 %upper_critical.2 = (bf16[128,2048]{1,0:T(8,128)(2,1)S(1)}, bf16[256,2048]{1,0:T(8,128)(2,1)S(1)}, bf16[64,2048]{1,0:T(8,128)(2,1)S(1)}) custom-call(bf16[64,2048]{1,0:T(8,128)(2,1)S(1)} %get-tuple-element.47.mid.refs_1_, bf16[64,2048]{1,0:T(8,128)(2,1)S(1)} %collective-permute-done.1.tap.refs_3_, bf16[1,64,4096]{2,1,0:T(8,128)(2,1)S(1)} %copy-done.1, ...), custom_call_target="tpu_custom_call" | custom-call | flops 266240000 | bytes 3743744 | tf_op jit(solution)/shard_map/upper_critical/pallas_call | solution.py:56
  29.5 1.3 %collective-permute-start.2 = (bf16[64,2048]{1,0:T(8,128)(2,1)S(1)}, bf16[64,2048]{1,0:T(8,128)(2,1)S(1)}, u32[]{:S(2)}, u32[]{:S(2)}) collective-permute-start(bf16[64,2048]{1,0:T(8,128)(2,1)S(1)} %get-tuple-element.50), channel_id=1, source_target_pairs={{2,0},{3,1},{4,2},{5,3},{6,4},{7,5},{8,6},{9,7},{10,8},{11,9},{12,... | collective-permute-start | bytes 786440 | tf_op jit(solution)/shard_map/ppermute | solution.py:21
  30.8 2.9 %collective-permute-done.5.gdel = bf16[64,2048]{1,0:T(8,128)(2,1)S(1)} collective-permute-done((bf16[64,2048]{1,0:T(8,128)(2,1)S(1)}, bf16[64,2048]{1,0:T(8,128)(2,1)S(1)}, u32[]{:S(2)}, u32[]{:S(2)}) %collective-permute-start.5) | collective-permute-done | bytes 262176 | tf_op jit(solution)/shard_map/ppermute | solution.py:21
  33.8 1.6 %lower_backward.2 = (bf16[64,2048]{1,0:T(8,128)(2,1)S(1)}, f32[64,2048]{1,0:T(8,128)S(1)}, f32[512,128]{1,0:T(8,128)S(1)}) custom-call(bf16[64,2048]{1,0:T(8,128)(2,1)S(1)} %collective-permute-done.5.gdel, bf16[256,2048]{1,0:T(8,128)(2,1)S(1)} %get-tuple-element.57.gpre1.refs_4_, bf16[1,64,4096]{2,1,0:T(8,128)(2,1)S(1)} %copy-done, ...), custom_call_target="tpu_custom_call" | custom-call | flops 655360000 | bytes 5054464 | tf_op jit(solution)/shard_map/lower_backward/pallas_call | solution.py:56
  35.3 1.1 %upper_sums.1.rest_2_ = f32[512,128]{1,0:T(8,128)S(1)} custom-call(bf16[64,2048]{1,0:T(8,128)(2,1)S(1)} %get-tuple-element.51.mid.refs_0_, bf16[64,2048]{1,0:T(8,128)(2,1)S(1)} %get-tuple-element.47.mid.refs_1_, bf16[64,2048]{1,0:T(8,128)(2,1)S(1)} %collective-permute-done.4.tap.refs_2_, bf16[64,2048]{1,0:T(8,128)(2,1)S(1)} %collective-permute-done.1.tap.refs_3_, ...), custom_call_target="tpu_custom_call" | custom-call | flops 409600000 | bytes 5505024 | tf_op jit(solution)/shard_map/upper_sums/pallas_call | solution.py:56
  36.4 1.5 %upper_outputs.1 = (bf16[1,64,4096]{2,1,0:T(8,128)(2,1)}, bf16[1,64,4096]{2,1,0:T(8,128)(2,1)}) custom-call(bf16[64,2048]{1,0:T(8,128)(2,1)S(1)} %get-tuple-element.51.mid.refs_0_, bf16[64,2048]{1,0:T(8,128)(2,1)S(1)} %get-tuple-element.47.mid.refs_1_, bf16[128,2048]{1,0:T(8,128)(2,1)S(1)} %get-tuple-element.52.z0.refs_2_, ...), custom_call_target="tpu_custom_call" | custom-call | flops 204800000 | bytes 3739648 | tf_op jit(solution)/shard_map/upper_outputs/pallas_call | solution.py:56
  37.9 1.7 %collective-permute-done.2.gdel = bf16[64,2048]{1,0:T(8,128)(2,1)S(1)} collective-permute-done((bf16[64,2048]{1,0:T(8,128)(2,1)S(1)}, bf16[64,2048]{1,0:T(8,128)(2,1)S(1)}, u32[]{:S(2)}, u32[]{:S(2)}) %collective-permute-start.2) | collective-permute-done | bytes 262176 | tf_op jit(solution)/shard_map/ppermute | solution.py:21
  39.6 1.8 %lower_backward.3 = (bf16[64,4096]{1,0:T(8,128)(2,1)S(1)}, f32[64,2048]{1,0:T(8,128)S(1)}, f32[512,128]{1,0:T(8,128)S(1)}, f32[512,128]{1,0:T(8,128)S(1)}) custom-call(bf16[64,2048]{1,0:T(8,128)(2,1)S(1)} %collective-permute-done.2.gdel, bf16[256,2048]{1,0:T(8,128)(2,1)S(1)} %get-tuple-element.61.refs_5_.gpre1, bf16[1,64,4096]{2,1,0:T(8,128)(2,1)S(1)} %copy-done, ...), custom_call_target="tpu_custom_call" | custom-call | flops 655360000 | bytes 6365184 | tf_op jit(solution)/shard_map/lower_backward/pallas_call | solution.py:56
  41.4 2.1 %collective-permute-start.6 = (f32[512,128]{1,0:T(8,128)S(1)}, f32[512,128]{1,0:T(8,128)S(1)}, u32[]{:S(2)}, u32[]{:S(2)}) collective-permute-start(f32[512,128]{1,0:T(8,128)S(1)} %get-tuple-element.75), channel_id=1, source_target_pairs={{0,16},{16,0},{1,17},{17,1},{2,18},{18,2},{3,19},{19,3},{4,20},{20... | collective-permute-start | bytes 786440 | tf_op jit(solution)/shard_map/ppermute | solution.py:218
  43.6 1.2 %collective-permute-done.6.y = f32[512,128]{1,0:T(8,128)S(1)} collective-permute-done((f32[512,128]{1,0:T(8,128)S(1)}, f32[512,128]{1,0:T(8,128)S(1)}, u32[]{:S(2)}, u32[]{:S(2)}) %collective-permute-start.6) | collective-permute-done | bytes 262176 | tf_op jit(solution)/shard_map/ppermute | solution.py:218
  44.8 12.9 %all_to_all.15.parts = f32[16,32,128]{2,1,0:T(8,128)S(1)} all-to-all(f32[16,32,128]{2,1,0:T(8,128)S(1)} %bitcast.6), channel_id=1, replica_groups=mesh['y'=4,'xl'=2,'core'=2,'z'=8,'xh'=2] {'y','xl','xh'}, dimensions={0} | all-to-all | bytes 524288 | tf_op jit(solution)/shard_map/all_to_all | solution.py:286
  57.7 0.7 share_out.2
  58.4 9.7 %all-to-all-start.1 = ((f32[8,32,128]{2,1,0:T(8,128)}), f32[8,32,128]{2,1,0:T(8,128)S(1)}, u32[]{:S(2)}, u32[]{:S(2)}) async-start(f32[8,32,128]{2,1,0:T(8,128)} %share_out.2), calls=%async_computation.1 | async-start | bytes 262144 | tf_op jit(solution)/shard_map/all_to_all | solution.py:288
  68.0 1.3 %collective-permute-start.7 = (bf16[64,4096]{1,0:T(8,128)(2,1)S(1)}, bf16[64,4096]{1,0:T(8,128)(2,1)S(1)}, u32[]{:S(2)}, u32[]{:S(2)}) collective-permute-start(bf16[64,4096]{1,0:T(8,128)(2,1)S(1)} %get-tuple-element.77), channel_id=1, source_target_pairs={{1,0},{2,1},{3,2},{4,3},{5,4},{6,5},{7,6},{8,7},{9,8},{10,9},{11,1... | collective-permute-start | bytes 1572872 | tf_op jit(solution)/shard_map/ppermute | solution.py:21
  69.3 6.7 %all-to-all-done.1.parts = f32[8,32,128]{2,1,0:T(8,128)S(1)} async-done(((f32[8,32,128]{2,1,0:T(8,128)}), f32[8,32,128]{2,1,0:T(8,128)S(1)}, u32[]{:S(2)}, u32[]{:S(2)}) %all-to-all-start.1) | async-done | bytes 131104 | tf_op jit(solution)/shard_map/all_to_all | solution.py:288
  76.1 12.4 %all_to_all.16 = f32[16,32,128]{2,1,0:T(8,128)S(1)} all-to-all(f32[16,32,128]{2,1,0:T(8,128)S(1)} %share_out.3), channel_id=1, replica_groups=mesh['y'=4,'xl'=2,'core'=2,'z'=8,'xh'=2] {'y','xl','xh'}, dimensions={0} | all-to-all | bytes 524288 | tf_op jit(solution)/shard_map/all_to_all | solution.py:290
  88.5 2.7 %collective-permute-start.8 = (f32[512,128]{1,0:T(8,128)S(1)}, f32[512,128]{1,0:T(8,128)S(1)}, u32[]{:S(2)}, u32[]{:S(2)}) collective-permute-start(f32[512,128]{1,0:T(8,128)S(1)} %bitcast.7), channel_id=1, source_target_pairs={{0,16},{16,0},{1,17},{17,1},{2,18},{18,2},{3,19},{19,3},{4,20},{20... | collective-permute-start | bytes 786440 | tf_op jit(solution)/shard_map/ppermute | solution.py:218
  91.2 0.0 collective-permute-done.7.refs_2_
  91.2 0.9 finish.1
  92.1 0.3 collective-permute-done.8.other
  92.4 0.8 place.1
  (3 shorter events, 0.1 us)
Async XLA Ops:
  0.6 11.6 %copy-start = (bf16[1,64,4096]{2,1,0:T(8,128)(2,1)S(1)}, bf16[1,64,4096]{2,1,0:T(8,128)(2,1)}, u32[]{:S(2)}) copy-start(bf16[1,64,4096]{2,1,0:T(8,128)(2,1)} %sig.7) | copy-start | bytes 1572868
  0.6 10.2 %copy-start.3 = (bf16[2,256,128]{2,1,0:T(8,128)(2,1)S(1)}, bf16[2,256,128]{2,1,0:T(8,128)(2,1)}, u32[]{:S(2)}) copy-start(bf16[2,256,128]{2,1,0:T(8,128)(2,1)} %w.13) | copy-start | bytes 393220
  0.7 10.2 %copy-start.4 = (bf16[2,128,128]{2,1,0:T(8,128)(2,1)S(1)}, bf16[2,128,128]{2,1,0:T(8,128)(2,1)}, u32[]{:S(2)}) copy-start(bf16[2,128,128]{2,1,0:T(8,128)(2,1)} %refs_6_.1) | copy-start | bytes 196612
  1.8 9.0 %copy-start.5 = (f32[2,256]{1,0:T(2,128)S(1)}, f32[2,256]{1,0:T(2,128)}, u32[]{:S(2)}) copy-start(f32[2,256]{1,0:T(2,128)} %b.1) | copy-start | bytes 6148
  1.8 9.0 %copy-start.6 = (f32[2,128]{1,0:T(2,128)S(1)}, f32[2,128]{1,0:T(2,128)}, u32[]{:S(2)}) copy-start(f32[2,128]{1,0:T(2,128)} %vb.1) | copy-start | bytes 3076
  1.8 10.4 %collective-permute-start.3 = (bf16[64,2048]{1,0:T(8,128)(2,1)S(1)}, bf16[64,2048]{1,0:T(8,128)(2,1)S(1)}, u32[]{:S(2)}, u32[]{:S(2)}) collective-permute-start(bf16[64,2048]{1,0:T(8,128)(2,1)S(1)} %get-tuple-element.83), channel_id=1, source_target_pairs={{0,1},{1,2},{2,3},{3,4},{4,5},{5,6},{6,7},{7,8},{8,9},{9,10},{10,1... | collective-permute-start | bytes 786440 | tf_op jit(solution)/shard_map/ppermute | solution.py:21
  7.3 11.2 %collective-permute-start = (bf16[64,2048]{1,0:T(8,128)(2,1)S(1)}, bf16[64,2048]{1,0:T(8,128)(2,1)S(1)}, u32[]{:S(2)}, u32[]{:S(2)}) collective-permute-start(bf16[64,2048]{1,0:T(8,128)(2,1)S(1)} %get-tuple-element.84), channel_id=1, source_target_pairs={{0,1},{1,2},{2,3},{3,4},{4,5},{5,6},{6,7},{7,8},{8,9},{9,10},{10,1... | collective-permute-start | bytes 786440 | tf_op jit(solution)/shard_map/ppermute | solution.py:21
  12.9 11.3 %copy-start.1 = (bf16[1,64,4096]{2,1,0:T(8,128)(2,1)S(1)}, bf16[1,64,4096]{2,1,0:T(8,128)(2,1)}, u32[]{:S(2)}) copy-start(bf16[1,64,4096]{2,1,0:T(8,128)(2,1)} %top.7) | copy-start | bytes 1572868
  13.0 11.3 %copy-start.2 = (bf16[1,64,4096]{2,1,0:T(8,128)(2,1)S(1)}, bf16[1,64,4096]{2,1,0:T(8,128)(2,1)}, u32[]{:S(2)}) copy-start(bf16[1,64,4096]{2,1,0:T(8,128)(2,1)} %skip.7) | copy-start | bytes 1572868
  13.0 11.3 %collective-permute-start.4 = (bf16[64,2048]{1,0:T(8,128)(2,1)S(1)}, bf16[64,2048]{1,0:T(8,128)(2,1)S(1)}, u32[]{:S(2)}, u32[]{:S(2)}) collective-permute-start(bf16[64,2048]{1,0:T(8,128)(2,1)S(1)} %get-tuple-element.51.mid.refs_0_), channel_id=1, source_target_pairs={{0,2},{1,3},{2,4},{3,5},{4,6},{5,7},{6,8},{7,9},{8,10},{9,11},{10,... | collective-permute-start | bytes 786440 | tf_op jit(solution)/shard_map/ppermute | solution.py:21
  19.2 9.3 %collective-permute-start.1 = (bf16[64,2048]{1,0:T(8,128)(2,1)S(1)}, bf16[64,2048]{1,0:T(8,128)(2,1)S(1)}, u32[]{:S(2)}, u32[]{:S(2)}) collective-permute-start(bf16[64,2048]{1,0:T(8,128)(2,1)S(1)} %get-tuple-element.47.mid.refs_1_), channel_id=1, source_target_pairs={{0,2},{1,3},{2,4},{3,5},{4,6},{5,7},{6,8},{7,9},{8,10},{9,11},{10,... | collective-permute-start | bytes 786440 | tf_op jit(solution)/shard_map/ppermute | solution.py:21
  25.3 8.5 %collective-permute-start.5 = (bf16[64,2048]{1,0:T(8,128)(2,1)S(1)}, bf16[64,2048]{1,0:T(8,128)(2,1)S(1)}, u32[]{:S(2)}, u32[]{:S(2)}) collective-permute-start(bf16[64,2048]{1,0:T(8,128)(2,1)S(1)} %get-tuple-element.56), channel_id=1, source_target_pairs={{2,0},{3,1},{4,2},{5,3},{6,4},{7,5},{8,6},{9,7},{10,8},{11,9},{12,... | collective-permute-start | bytes 786440 | tf_op jit(solution)/shard_map/ppermute | solution.py:21
  29.5 10.1 %collective-permute-start.2 = (bf16[64,2048]{1,0:T(8,128)(2,1)S(1)}, bf16[64,2048]{1,0:T(8,128)(2,1)S(1)}, u32[]{:S(2)}, u32[]{:S(2)}) collective-permute-start(bf16[64,2048]{1,0:T(8,128)(2,1)S(1)} %get-tuple-element.50), channel_id=1, source_target_pairs={{2,0},{3,1},{4,2},{5,3},{6,4},{7,5},{8,6},{9,7},{10,8},{11,9},{12,... | collective-permute-start | bytes 786440 | tf_op jit(solution)/shard_map/ppermute | solution.py:21
  41.4 3.3 %collective-permute-start.6 = (f32[512,128]{1,0:T(8,128)S(1)}, f32[512,128]{1,0:T(8,128)S(1)}, u32[]{:S(2)}, u32[]{:S(2)}) collective-permute-start(f32[512,128]{1,0:T(8,128)S(1)} %get-tuple-element.75), channel_id=1, source_target_pairs={{0,16},{16,0},{1,17},{17,1},{2,18},{18,2},{3,19},{19,3},{4,20},{20... | collective-permute-start | bytes 786440 | tf_op jit(solution)/shard_map/ppermute | solution.py:218
  58.4 17.7 %all-to-all-start.1 = ((f32[8,32,128]{2,1,0:T(8,128)}), f32[8,32,128]{2,1,0:T(8,128)S(1)}, u32[]{:S(2)}, u32[]{:S(2)}) async-start(f32[8,32,128]{2,1,0:T(8,128)} %share_out.2), calls=%async_computation.1 | async-start | bytes 262144 | tf_op jit(solution)/shard_map/all_to_all | solution.py:288
  68.0 23.2 %collective-permute-start.7 = (bf16[64,4096]{1,0:T(8,128)(2,1)S(1)}, bf16[64,4096]{1,0:T(8,128)(2,1)S(1)}, u32[]{:S(2)}, u32[]{:S(2)}) collective-permute-start(bf16[64,4096]{1,0:T(8,128)(2,1)S(1)} %get-tuple-element.77), channel_id=1, source_target_pairs={{1,0},{2,1},{3,2},{4,3},{5,4},{6,5},{7,6},{8,7},{9,8},{10,9},{11,1... | collective-permute-start | bytes 1572872 | tf_op jit(solution)/shard_map/ppermute | solution.py:21
  88.5 3.9 %collective-permute-start.8 = (f32[512,128]{1,0:T(8,128)S(1)}, f32[512,128]{1,0:T(8,128)S(1)}, u32[]{:S(2)}, u32[]{:S(2)}) collective-permute-start(f32[512,128]{1,0:T(8,128)S(1)} %bitcast.7), channel_id=1, source_target_pairs={{0,16},{16,0},{1,17},{17,1},{2,18},{18,2},{3,19},{19,3},{4,20},{20... | collective-permute-start | bytes 786440 | tf_op jit(solution)/shard_map/ppermute | solution.py:218

commit v5 on v4

--- a/solution.py
+++ b/solution.py
@@ -254,7 +254,8 @@
     m = signal.shape[2]
     n = m // HALVES
     offs = range(0, m, n)
-    taps = [from_behind(signal[0, :, o : o + n], 1) for o in offs]
+    again = lax.optimization_barrier(signal)
+    taps = [from_behind((again if o else signal)[0, :, o : o + n], 1) for o in offs]
     b, vb, wt, vt = prepare(w, b, v, vb)
     mids, z0s, mid_taps = [], [], []
     for o, tap in zip(offs, taps):

time: 93.6 us -> 93.7 us (level)
  no operation moved by 1% of the time
where the time goes in v5:
time: 93.7 us; the launch traced here: 93.2 us
  starting transfers between devices  38.1 us (41%)
  blocking collectives  25.3 us (27%)
  waiting for transfers between devices  16 us (17%)
  Pallas kernels  11.9 us (13%)
  local copies, waits for them, and re-layouts  1.09 us (1%)
    ppermute x7, starting transfers between devices, from_behind(): return lax.ppermute(block, TM, route)  23.6 us
    all_to_all x1, blocking collectives, on_device(): parts = lax.all_to_all(rows, PLANE, 0, 0, tiled=True)  12.9 us
    all_to_all x1, blocking collectives, on_device(): held = lax.all_to_all(parts, PLANE, 0, 0, tiled=True).reshape(give.shape)  12.4 us
    pallas_call x14, Pallas kernels, call(): pl.pallas_call(body, out_shape=out, in_specs=[spec] * len(args), out_spec...  11.9 us
    all_to_all x1, starting transfers between devices, on_device(): parts = lax.all_to_all(parts, 'z', 0, 0, tiled=True)  9.65 us
    ppermute x7, waiting for transfers between devices, from_behind(): return lax.ppermute(block, TM, route)  7.79 us
    all_to_all x1, waiting for transfers between devices, on_device(): parts = lax.all_to_all(parts, 'z', 0, 0, tiled=True)  6.75 us
    ppermute x2, starting transfers between devices, swap_cores(): return lax.ppermute(block, 'core', [(0, 1), (1, 0)])  4.86 us
  transfers between devices with their start and end apart: 10, of which 7 were waited for; matrix products, arithmetic and copies ran while one was open for 0% of the time, Pallas kernels for 9%

profile of v5, /device:TPU:1, one launch (start us, length us, event | category | flops | bytes accessed | tf_op | source)
XLA Modules:
  0.0 93.2 jit_solution(12390176329876709235)
XLA Ops:
  0.6 0.0 copy-start
  0.6 1.0 %slice_bitcast_fusion.1 = bf16[64,2048]{1,0:T(8,128)(2,1)S(1)} fusion(bf16[1,64,4096]{2,1,0:T(8,128)(2,1)} %sig.7), kind=kLoop, calls=%fused_computation.1 | loop fusion | bytes 524288 | tf_op jit(solution)/shard_map/squeeze | solution.py:258
  1.7 0.0 copy-start.3
  1.7 0.0 copy-start.4
  1.7 0.0 copy-start.5
  1.7 0.0 copy-start.6
  1.7 5.6 %collective-permute-start.3 = (bf16[64,2048]{1,0:T(8,128)(2,1)S(1)}, bf16[64,2048]{1,0:T(8,128)(2,1)S(1)}, u32[]{:S(2)}, u32[]{:S(2)}) collective-permute-start(bf16[64,2048]{1,0:T(8,128)(2,1)S(1)} %slice_bitcast_fusion.1), channel_id=1, source_target_pairs={{0,1},{1,2},{2,3},{3,4},{4,5},{5,6},{6,7},{7,8},{8,9},{9,10},{10,1... | collective-permute-start | bytes 786440 | tf_op jit(solution)/shard_map/ppermute | solution.py:21
  7.4 0.0 copy-done
  7.4 3.5 %collective-permute-start = (bf16[64,2048]{1,0:T(8,128)(2,1)S(1)}, bf16[64,2048]{1,0:T(8,128)(2,1)S(1)}, u32[]{:S(2)}, u32[]{:S(2)}) collective-permute-start(bf16[64,2048]{1,0:T(8,128)(2,1)S(1)} %slice_bitcast_fusion), channel_id=1, source_target_pairs={{0,1},{1,2},{2,3},{3,4},{4,5},{5,6},{6,7},{7,8},{8,9},{9,10},{10,1... | collective-permute-start | bytes 786440 | tf_op jit(solution)/shard_map/ppermute | solution.py:21
  10.9 0.0 copy-done.3
  10.9 0.0 copy-done.4
  10.9 0.0 copy-done.5
  10.9 0.0 copy-done.6
  10.9 0.2 prepare.1
  11.1 1.2 %collective-permute-done.3.tap = bf16[64,2048]{1,0:T(8,128)(2,1)S(1)} collective-permute-done((bf16[64,2048]{1,0:T(8,128)(2,1)S(1)}, bf16[64,2048]{1,0:T(8,128)(2,1)S(1)}, u32[]{:S(2)}, u32[]{:S(2)}) %collective-permute-start.3) | collective-permute-done | bytes 262176 | tf_op jit(solution)/shard_map/ppermute | solution.py:21
  12.3 0.7 lower_forward.3
  13.0 0.0 copy-start.2
  13.0 5.5 %collective-permute-start.4 = (bf16[64,2048]{1,0:T(8,128)(2,1)S(1)}, bf16[64,2048]{1,0:T(8,128)(2,1)S(1)}, u32[]{:S(2)}, u32[]{:S(2)}) collective-permute-start(bf16[64,2048]{1,0:T(8,128)(2,1)S(1)} %get-tuple-element.51.mid.refs_0_), channel_id=1, source_target_pairs={{0,2},{1,3},{2,4},{3,5},{4,6},{5,7},{6,8},{7,9},{8,10},{9,11},{10,... | collective-permute-start | bytes 786440 | tf_op jit(solution)/shard_map/ppermute | solution.py:21
  18.5 0.0 collective-permute-done.tap
  18.6 0.7 lower_forward.2
  19.2 5.1 %collective-permute-start.1 = (bf16[64,2048]{1,0:T(8,128)(2,1)S(1)}, bf16[64,2048]{1,0:T(8,128)(2,1)S(1)}, u32[]{:S(2)}, u32[]{:S(2)}) collective-permute-start(bf16[64,2048]{1,0:T(8,128)(2,1)S(1)} %get-tuple-element.47.mid.refs_1_), channel_id=1, source_target_pairs={{0,2},{1,3},{2,4},{3,5},{4,6},{5,7},{6,8},{7,9},{8,10},{9,11},{10,... | collective-permute-start | bytes 786440 | tf_op jit(solution)/shard_map/ppermute | solution.py:21
  24.3 0.0 collective-permute-done.4.tap.refs_2_
  24.3 0.0 copy-done.1
  24.3 0.0 copy-done.2
  24.3 1.0 %upper_critical.3 = (bf16[128,2048]{1,0:T(8,128)(2,1)S(1)}, bf16[256,2048]{1,0:T(8,128)(2,1)S(1)}, bf16[64,2048]{1,0:T(8,128)(2,1)S(1)}) custom-call(bf16[64,2048]{1,0:T(8,128)(2,1)S(1)} %get-tuple-element.51.mid.refs_0_, bf16[64,2048]{1,0:T(8,128)(2,1)S(1)} %collective-permute-done.4.tap.refs_2_, bf16[1,64,4096]{2,1,0:T(8,128)(2,1)S(1)} %copy-done.1, ...), custom_call_target="tpu_custom_call" | custom-call | flops 266240000 | bytes 3743744 | tf_op jit(solution)/shard_map/upper_critical/pallas_call | solution.py:56
  25.4 1.3 %collective-permute-start.5 = (bf16[64,2048]{1,0:T(8,128)(2,1)S(1)}, bf16[64,2048]{1,0:T(8,128)(2,1)S(1)}, u32[]{:S(2)}, u32[]{:S(2)}) collective-permute-start(bf16[64,2048]{1,0:T(8,128)(2,1)S(1)} %get-tuple-element.56), channel_id=1, source_target_pairs={{2,0},{3,1},{4,2},{5,3},{6,4},{7,5},{8,6},{9,7},{10,8},{11,9},{12,... | collective-permute-start | bytes 786440 | tf_op jit(solution)/shard_map/ppermute | solution.py:21
  26.7 2.0 %collective-permute-done.1.tap.refs_3_ = bf16[64,2048]{1,0:T(8,128)(2,1)S(1)} collective-permute-done((bf16[64,2048]{1,0:T(8,128)(2,1)S(1)}, bf16[64,2048]{1,0:T(8,128)(2,1)S(1)}, u32[]{:S(2)}, u32[]{:S(2)}) %collective-permute-start.1) | collective-permute-done | bytes 262176 | tf_op jit(solution)/shard_map/ppermute | solution.py:21
  28.6 1.0 %upper_critical.2 = (bf16[128,2048]{1,0:T(8,128)(2,1)S(1)}, bf16[256,2048]{1,0:T(8,128)(2,1)S(1)}, bf16[64,2048]{1,0:T(8,128)(2,1)S(1)}) custom-call(bf16[64,2048]{1,0:T(8,128)(2,1)S(1)} %get-tuple-element.47.mid.refs_1_, bf16[64,2048]{1,0:T(8,128)(2,1)S(1)} %collective-permute-done.1.tap.refs_3_, bf16[1,64,4096]{2,1,0:T(8,128)(2,1)S(1)} %copy-done.1, ...), custom_call_target="tpu_custom_call" | custom-call | flops 266240000 | bytes 3743744 | tf_op jit(solution)/shard_map/upper_critical/pallas_call | solution.py:56
  29.6 1.3 %collective-permute-start.2 = (bf16[64,2048]{1,0:T(8,128)(2,1)S(1)}, bf16[64,2048]{1,0:T(8,128)(2,1)S(1)}, u32[]{:S(2)}, u32[]{:S(2)}) collective-permute-start(bf16[64,2048]{1,0:T(8,128)(2,1)S(1)} %get-tuple-element.50), channel_id=1, source_target_pairs={{2,0},{3,1},{4,2},{5,3},{6,4},{7,5},{8,6},{9,7},{10,8},{11,9},{12,... | collective-permute-start | bytes 786440 | tf_op jit(solution)/shard_map/ppermute | solution.py:21
  30.9 2.9 %collective-permute-done.5.gdel = bf16[64,2048]{1,0:T(8,128)(2,1)S(1)} collective-permute-done((bf16[64,2048]{1,0:T(8,128)(2,1)S(1)}, bf16[64,2048]{1,0:T(8,128)(2,1)S(1)}, u32[]{:S(2)}, u32[]{:S(2)}) %collective-permute-start.5) | collective-permute-done | bytes 262176 | tf_op jit(solution)/shard_map/ppermute | solution.py:21
  33.9 1.6 %lower_backward.2 = (bf16[64,2048]{1,0:T(8,128)(2,1)S(1)}, f32[64,2048]{1,0:T(8,128)S(1)}, f32[512,128]{1,0:T(8,128)S(1)}) custom-call(bf16[64,2048]{1,0:T(8,128)(2,1)S(1)} %collective-permute-done.5.gdel, bf16[256,2048]{1,0:T(8,128)(2,1)S(1)} %get-tuple-element.57.gpre1.refs_4_, bf16[1,64,4096]{2,1,0:T(8,128)(2,1)S(1)} %copy-done, ...), custom_call_target="tpu_custom_call" | custom-call | flops 655360000 | bytes 5054464 | tf_op jit(solution)/shard_map/lower_backward/pallas_call | solution.py:56
  35.4 1.1 %upper_sums.1.rest_2_ = f32[512,128]{1,0:T(8,128)S(1)} custom-call(bf16[64,2048]{1,0:T(8,128)(2,1)S(1)} %get-tuple-element.51.mid.refs_0_, bf16[64,2048]{1,0:T(8,128)(2,1)S(1)} %get-tuple-element.47.mid.refs_1_, bf16[64,2048]{1,0:T(8,128)(2,1)S(1)} %collective-permute-done.4.tap.refs_2_, bf16[64,2048]{1,0:T(8,128)(2,1)S(1)} %collective-permute-done.1.tap.refs_3_, ...), custom_call_target="tpu_custom_call" | custom-call | flops 409600000 | bytes 5505024 | tf_op jit(solution)/shard_map/upper_sums/pallas_call | solution.py:56
  36.5 1.5 %upper_outputs.1 = (bf16[1,64,4096]{2,1,0:T(8,128)(2,1)}, bf16[1,64,4096]{2,1,0:T(8,128)(2,1)}) custom-call(bf16[64,2048]{1,0:T(8,128)(2,1)S(1)} %get-tuple-element.51.mid.refs_0_, bf16[64,2048]{1,0:T(8,128)(2,1)S(1)} %get-tuple-element.47.mid.refs_1_, bf16[128,2048]{1,0:T(8,128)(2,1)S(1)} %get-tuple-element.52.z0.refs_2_, ...), custom_call_target="tpu_custom_call" | custom-call | flops 204800000 | bytes 3739648 | tf_op jit(solution)/shard_map/upper_outputs/pallas_call | solution.py:56
  38.0 1.7 %collective-permute-done.2.gdel = bf16[64,2048]{1,0:T(8,128)(2,1)S(1)} collective-permute-done((bf16[64,2048]{1,0:T(8,128)(2,1)S(1)}, bf16[64,2048]{1,0:T(8,128)(2,1)S(1)}, u32[]{:S(2)}, u32[]{:S(2)}) %collective-permute-start.2) | collective-permute-done | bytes 262176 | tf_op jit(solution)/shard_map/ppermute | solution.py:21
  39.7 1.8 %lower_backward.3 = (bf16[64,4096]{1,0:T(8,128)(2,1)S(1)}, f32[64,2048]{1,0:T(8,128)S(1)}, f32[512,128]{1,0:T(8,128)S(1)}, f32[512,128]{1,0:T(8,128)S(1)}) custom-call(bf16[64,2048]{1,0:T(8,128)(2,1)S(1)} %collective-permute-done.2.gdel, bf16[256,2048]{1,0:T(8,128)(2,1)S(1)} %get-tuple-element.61.refs_5_.gpre1, bf16[1,64,4096]{2,1,0:T(8,128)(2,1)S(1)} %copy-done, ...), custom_call_target="tpu_custom_call" | custom-call | flops 655360000 | bytes 6365184 | tf_op jit(solution)/shard_map/lower_backward/pallas_call | solution.py:56
  41.5 2.1 %collective-permute-start.6 = (f32[512,128]{1,0:T(8,128)S(1)}, f32[512,128]{1,0:T(8,128)S(1)}, u32[]{:S(2)}, u32[]{:S(2)}) collective-permute-start(f32[512,128]{1,0:T(8,128)S(1)} %get-tuple-element.75), channel_id=1, source_target_pairs={{0,16},{16,0},{1,17},{17,1},{2,18},{18,2},{3,19},{19,3},{4,20},{20... | collective-permute-start | bytes 786440 | tf_op jit(solution)/shard_map/ppermute | solution.py:218
  43.6 1.2 %collective-permute-done.6.y = f32[512,128]{1,0:T(8,128)S(1)} collective-permute-done((f32[512,128]{1,0:T(8,128)S(1)}, f32[512,128]{1,0:T(8,128)S(1)}, u32[]{:S(2)}, u32[]{:S(2)}) %collective-permute-start.6) | collective-permute-done | bytes 262176 | tf_op jit(solution)/shard_map/ppermute | solution.py:218
  44.8 12.9 %all_to_all.15.parts = f32[16,32,128]{2,1,0:T(8,128)S(1)} all-to-all(f32[16,32,128]{2,1,0:T(8,128)S(1)} %bitcast.6), channel_id=1, replica_groups=mesh['y'=4,'xl'=2,'core'=2,'z'=8,'xh'=2] {'y','xl','xh'}, dimensions={0} | all-to-all | bytes 524288 | tf_op jit(solution)/shard_map/all_to_all | solution.py:287
  57.7 0.7 share_out.2
  58.4 9.6 %all-to-all-start.1 = ((f32[8,32,128]{2,1,0:T(8,128)}), f32[8,32,128]{2,1,0:T(8,128)S(1)}, u32[]{:S(2)}, u32[]{:S(2)}) async-start(f32[8,32,128]{2,1,0:T(8,128)} %share_out.2), calls=%async_computation.1 | async-start | bytes 262144 | tf_op jit(solution)/shard_map/all_to_all | solution.py:289
  68.0 1.3 %collective-permute-start.7 = (bf16[64,4096]{1,0:T(8,128)(2,1)S(1)}, bf16[64,4096]{1,0:T(8,128)(2,1)S(1)}, u32[]{:S(2)}, u32[]{:S(2)}) collective-permute-start(bf16[64,4096]{1,0:T(8,128)(2,1)S(1)} %get-tuple-element.77), channel_id=1, source_target_pairs={{1,0},{2,1},{3,2},{4,3},{5,4},{6,5},{7,6},{8,7},{9,8},{10,9},{11,1... | collective-permute-start | bytes 1572872 | tf_op jit(solution)/shard_map/ppermute | solution.py:21
  69.3 6.7 %all-to-all-done.1.parts = f32[8,32,128]{2,1,0:T(8,128)S(1)} async-done(((f32[8,32,128]{2,1,0:T(8,128)}), f32[8,32,128]{2,1,0:T(8,128)S(1)}, u32[]{:S(2)}, u32[]{:S(2)}) %all-to-all-start.1) | async-done | bytes 131104 | tf_op jit(solution)/shard_map/all_to_all | solution.py:289
  76.1 12.4 %all_to_all.16 = f32[16,32,128]{2,1,0:T(8,128)S(1)} all-to-all(f32[16,32,128]{2,1,0:T(8,128)S(1)} %share_out.3), channel_id=1, replica_groups=mesh['y'=4,'xl'=2,'core'=2,'z'=8,'xh'=2] {'y','xl','xh'}, dimensions={0} | all-to-all | bytes 524288 | tf_op jit(solution)/shard_map/all_to_all | solution.py:291
  88.5 2.7 %collective-permute-start.8 = (f32[512,128]{1,0:T(8,128)S(1)}, f32[512,128]{1,0:T(8,128)S(1)}, u32[]{:S(2)}, u32[]{:S(2)}) collective-permute-start(f32[512,128]{1,0:T(8,128)S(1)} %bitcast.7), channel_id=1, source_target_pairs={{0,16},{16,0},{1,17},{17,1},{2,18},{18,2},{3,19},{19,3},{4,20},{20... | collective-permute-start | bytes 786440 | tf_op jit(solution)/shard_map/ppermute | solution.py:218
  91.2 0.0 collective-permute-done.7.refs_2_
  91.2 0.9 finish.1
  92.1 0.3 collective-permute-done.8.other
  92.4 0.8 place.1
  (4 shorter events, 0.1 us)
Async XLA Ops:
  0.6 6.7 %copy-start = (bf16[1,64,4096]{2,1,0:T(8,128)(2,1)S(1)}, bf16[1,64,4096]{2,1,0:T(8,128)(2,1)}, u32[]{:S(2)}) copy-start(bf16[1,64,4096]{2,1,0:T(8,128)(2,1)} %sig.7) | copy-start | bytes 1572868
  1.7 9.2 %copy-start.3 = (bf16[2,256,128]{2,1,0:T(8,128)(2,1)S(1)}, bf16[2,256,128]{2,1,0:T(8,128)(2,1)}, u32[]{:S(2)}) copy-start(bf16[2,256,128]{2,1,0:T(8,128)(2,1)} %w.13) | copy-start | bytes 393220
  1.7 9.2 %copy-start.4 = (bf16[2,128,128]{2,1,0:T(8,128)(2,1)S(1)}, bf16[2,128,128]{2,1,0:T(8,128)(2,1)}, u32[]{:S(2)}) copy-start(bf16[2,128,128]{2,1,0:T(8,128)(2,1)} %refs_6_.1) | copy-start | bytes 196612
  1.7 9.2 %copy-start.5 = (f32[2,256]{1,0:T(2,128)S(1)}, f32[2,256]{1,0:T(2,128)}, u32[]{:S(2)}) copy-start(f32[2,256]{1,0:T(2,128)} %b.1) | copy-start | bytes 6148
  1.7 9.2 %copy-start.6 = (f32[2,128]{1,0:T(2,128)S(1)}, f32[2,128]{1,0:T(2,128)}, u32[]{:S(2)}) copy-start(f32[2,128]{1,0:T(2,128)} %vb.1) | copy-start | bytes 3076
  1.7 10.6 %collective-permute-start.3 = (bf16[64,2048]{1,0:T(8,128)(2,1)S(1)}, bf16[64,2048]{1,0:T(8,128)(2,1)S(1)}, u32[]{:S(2)}, u32[]{:S(2)}) collective-permute-start(bf16[64,2048]{1,0:T(8,128)(2,1)S(1)} %slice_bitcast_fusion.1), channel_id=1, source_target_pairs={{0,1},{1,2},{2,3},{3,4},{4,5},{5,6},{6,7},{7,8},{8,9},{9,10},{10,1... | collective-permute-start | bytes 786440 | tf_op jit(solution)/shard_map/ppermute | solution.py:21
  7.4 11.2 %collective-permute-start = (bf16[64,2048]{1,0:T(8,128)(2,1)S(1)}, bf16[64,2048]{1,0:T(8,128)(2,1)S(1)}, u32[]{:S(2)}, u32[]{:S(2)}) collective-permute-start(bf16[64,2048]{1,0:T(8,128)(2,1)S(1)} %slice_bitcast_fusion), channel_id=1, source_target_pairs={{0,1},{1,2},{2,3},{3,4},{4,5},{5,6},{6,7},{7,8},{8,9},{9,10},{10,1... | collective-permute-start | bytes 786440 | tf_op jit(solution)/shard_map/ppermute | solution.py:21
  13.0 11.3 %copy-start.1 = (bf16[1,64,4096]{2,1,0:T(8,128)(2,1)S(1)}, bf16[1,64,4096]{2,1,0:T(8,128)(2,1)}, u32[]{:S(2)}) copy-start(bf16[1,64,4096]{2,1,0:T(8,128)(2,1)} %top.7) | copy-start | bytes 1572868
  13.0 11.3 %copy-start.2 = (bf16[1,64,4096]{2,1,0:T(8,128)(2,1)S(1)}, bf16[1,64,4096]{2,1,0:T(8,128)(2,1)}, u32[]{:S(2)}) copy-start(bf16[1,64,4096]{2,1,0:T(8,128)(2,1)} %skip.7) | copy-start | bytes 1572868
  13.0 11.3 %collective-permute-start.4 = (bf16[64,2048]{1,0:T(8,128)(2,1)S(1)}, bf16[64,2048]{1,0:T(8,128)(2,1)S(1)}, u32[]{:S(2)}, u32[]{:S(2)}) collective-permute-start(bf16[64,2048]{1,0:T(8,128)(2,1)S(1)} %get-tuple-element.51.mid.refs_0_), channel_id=1, source_target_pairs={{0,2},{1,3},{2,4},{3,5},{4,6},{5,7},{6,8},{7,9},{8,10},{9,11},{10,... | collective-permute-start | bytes 786440 | tf_op jit(solution)/shard_map/ppermute | solution.py:21
  19.2 9.4 %collective-permute-start.1 = (bf16[64,2048]{1,0:T(8,128)(2,1)S(1)}, bf16[64,2048]{1,0:T(8,128)(2,1)S(1)}, u32[]{:S(2)}, u32[]{:S(2)}) collective-permute-start(bf16[64,2048]{1,0:T(8,128)(2,1)S(1)} %get-tuple-element.47.mid.refs_1_), channel_id=1, source_target_pairs={{0,2},{1,3},{2,4},{3,5},{4,6},{5,7},{6,8},{7,9},{8,10},{9,11},{10,... | collective-permute-start | bytes 786440 | tf_op jit(solution)/shard_map/ppermute | solution.py:21
  25.4 8.5 %collective-permute-start.5 = (bf16[64,2048]{1,0:T(8,128)(2,1)S(1)}, bf16[64,2048]{1,0:T(8,128)(2,1)S(1)}, u32[]{:S(2)}, u32[]{:S(2)}) collective-permute-start(bf16[64,2048]{1,0:T(8,128)(2,1)S(1)} %get-tuple-element.56), channel_id=1, source_target_pairs={{2,0},{3,1},{4,2},{5,3},{6,4},{7,5},{8,6},{9,7},{10,8},{11,9},{12,... | collective-permute-start | bytes 786440 | tf_op jit(solution)/shard_map/ppermute | solution.py:21
  29.6 10.1 %collective-permute-start.2 = (bf16[64,2048]{1,0:T(8,128)(2,1)S(1)}, bf16[64,2048]{1,0:T(8,128)(2,1)S(1)}, u32[]{:S(2)}, u32[]{:S(2)}) collective-permute-start(bf16[64,2048]{1,0:T(8,128)(2,1)S(1)} %get-tuple-element.50), channel_id=1, source_target_pairs={{2,0},{3,1},{4,2},{5,3},{6,4},{7,5},{8,6},{9,7},{10,8},{11,9},{12,... | collective-permute-start | bytes 786440 | tf_op jit(solution)/shard_map/ppermute | solution.py:21
  41.5 3.3 %collective-permute-start.6 = (f32[512,128]{1,0:T(8,128)S(1)}, f32[512,128]{1,0:T(8,128)S(1)}, u32[]{:S(2)}, u32[]{:S(2)}) collective-permute-start(f32[512,128]{1,0:T(8,128)S(1)} %get-tuple-element.75), channel_id=1, source_target_pairs={{0,16},{16,0},{1,17},{17,1},{2,18},{18,2},{3,19},{19,3},{4,20},{20... | collective-permute-start | bytes 786440 | tf_op jit(solution)/shard_map/ppermute | solution.py:218
  58.4 17.7 %all-to-all-start.1 = ((f32[8,32,128]{2,1,0:T(8,128)}), f32[8,32,128]{2,1,0:T(8,128)S(1)}, u32[]{:S(2)}, u32[]{:S(2)}) async-start(f32[8,32,128]{2,1,0:T(8,128)} %share_out.2), calls=%async_computation.1 | async-start | bytes 262144 | tf_op jit(solution)/shard_map/all_to_all | solution.py:289
  68.0 23.2 %collective-permute-start.7 = (bf16[64,4096]{1,0:T(8,128)(2,1)S(1)}, bf16[64,4096]{1,0:T(8,128)(2,1)S(1)}, u32[]{:S(2)}, u32[]{:S(2)}) collective-permute-start(bf16[64,4096]{1,0:T(8,128)(2,1)S(1)} %get-tuple-element.77), channel_id=1, source_target_pairs={{1,0},{2,1},{3,2},{4,3},{5,4},{6,5},{7,6},{8,7},{9,8},{10,9},{11,1... | collective-permute-start | bytes 1572872 | tf_op jit(solution)/shard_map/ppermute | solution.py:21
  88.5 3.9 %collective-permute-start.8 = (f32[512,128]{1,0:T(8,128)S(1)}, f32[512,128]{1,0:T(8,128)S(1)}, u32[]{:S(2)}, u32[]{:S(2)}) collective-permute-start(f32[512,128]{1,0:T(8,128)S(1)} %bitcast.7), channel_id=1, source_target_pairs={{0,16},{16,0},{1,17},{17,1},{2,18},{18,2},{3,19},{19,3},{4,20},{20... | collective-permute-start | bytes 786440 | tf_op jit(solution)/shard_map/ppermute | solution.py:218

commit v6 on v4

--- a/solution.py
+++ b/solution.py
@@ -200,7 +200,7 @@
 
 def place(held, other):
     def body(held, other, conv, conv_bias, proj, proj_bias):
-        a, b = held[...], other[...]
+        a, b = held[...].astype(F32), other[...].astype(F32)
         own = jnp.broadcast_to(lax.axis_index("core") == 0, a.shape)
         for layer, rows in enumerate((jnp.where(own, a, b), jnp.where(own, b, a))):
             conv[layer] = rows[:256]
@@ -237,16 +237,16 @@
     return call(body, [near(1, *later.shape)], 1000, "finish", *parts, later)[0]
 
 
-def share_out(parts, copies, scale=1.0):
+def share_out(parts, copies, scale=1.0, dtype=F32):
     def body(parts, out):
         total = parts[0]
         for i in range(1, parts.shape[0]):
             total += parts[i]
         total *= scale
         for i in range(copies):
-            out[i] = total
-
-    out = [near(copies, *parts.shape[1:], dtype=F32)]
+            out[i] = total.astype(dtype)
+
+    out = [near(copies, *parts.shape[1:], dtype=dtype)]
     return call(body, out, 1000, "share_out", parts)[0]
 
 
@@ -286,7 +286,7 @@
     parts = lax.all_to_all(rows, PLANE, 0, 0, tiled=True)
     parts = share_out(parts, depth)
     parts = lax.all_to_all(parts, "z", 0, 0, tiled=True)
-    parts = share_out(parts, plane, scale)
+    parts = share_out(parts, plane, scale, BF16)
     held = lax.all_to_all(parts, PLANE, 0, 0, tiled=True).reshape(give.shape)
     grad_input = finish([part_a, part_b], later)
     return (x_top, skip_sum, grad_input, *place(held, swap_cores(held)))

time: 93.6 us -> 93.2 us (level)
  blocking collectives: 25.3 us -> 27.7 us
  starting transfers between devices: 37.9 us -> 35.8 us
    all_to_all x1, blocking collectives: 12.9 us -> 17.4 us  [on_device(): parts = lax.all_to_all(parts, 'z', 0, 0, tiled=True)]
    all_to_all x1, starting transfers between devices: 9.66 us -> 5.75 us  [on_device(): parts = lax.all_to_all(rows, PLANE, 0, 0, tiled=True)]
    all_to_all x1, blocking collectives: 12.4 us -> 10.3 us  [on_device(): held = lax.all_to_all(parts, PLANE, 0, 0, tiled=True).reshape(give.shape)]
    ppermute x2, starting transfers between devices: 4.86 us -> 6.59 us  [swap_cores(): return lax.ppermute(block, 'core', [(0, 1), (1, 0)])]
where the time goes in v6:
time: 93.2 us; the launch traced here: 92.6 us
  starting transfers between devices  35.8 us (38%)
  blocking collectives  27.7 us (30%)
  waiting for transfers between devices  15.1 us (16%)
  Pallas kernels  11.9 us (13%)
  local copies, waits for them, and re-layouts  1.17 us (1%)
    ppermute x7, starting transfers between devices, from_behind(): return lax.ppermute(block, TM, route)  23.4 us
    all_to_all x1, blocking collectives, on_device(): parts = lax.all_to_all(parts, 'z', 0, 0, tiled=True)  17.4 us
    pallas_call x14, Pallas kernels, call(): pl.pallas_call(body, out_shape=out, in_specs=[spec] * len(args), out_spec...  11.9 us
    all_to_all x1, blocking collectives, on_device(): held = lax.all_to_all(parts, PLANE, 0, 0, tiled=True).reshape(give.shape)  10.3 us
    ppermute x7, waiting for transfers between devices, from_behind(): return lax.ppermute(block, TM, route)  7.81 us
    ppermute x2, starting transfers between devices, swap_cores(): return lax.ppermute(block, 'core', [(0, 1), (1, 0)])  6.59 us
    all_to_all x1, waiting for transfers between devices, on_device(): parts = lax.all_to_all(rows, PLANE, 0, 0, tiled=True)  6.07 us
    all_to_all x1, starting transfers between devices, on_device(): parts = lax.all_to_all(rows, PLANE, 0, 0, tiled=True)  5.75 us
  transfers between devices with their start and end apart: 10, of which 7 were waited for; matrix products, arithmetic and copies ran while one was open for 0% of the time, Pallas kernels for 9%

profile of v6, /device:TPU:1, one launch (start us, length us, event | category | flops | bytes accessed | tf_op | source)
XLA Modules:
  0.0 92.6 jit_solution(8933888086990888825)
XLA Ops:
  0.6 0.0 copy-start
  0.6 0.0 copy-start.3
  0.7 0.0 copy-start.4
  0.7 1.1 %slice_bitcast_fusion = (bf16[64,2048]{1,0:T(8,128)(2,1)S(1)}, bf16[64,2048]{1,0:T(8,128)(2,1)S(1)}) fusion(bf16[1,64,4096]{2,1,0:T(8,128)(2,1)} %sig.7), kind=kLoop, calls=%fused_computation | loop fusion | bytes 1048576 | tf_op jit(solution)/shard_map/squeeze | solution.py:257
  1.8 0.0 copy-start.5
  1.8 0.0 copy-start.6
  1.8 5.5 %collective-permute-start.3 = (bf16[64,2048]{1,0:T(8,128)(2,1)S(1)}, bf16[64,2048]{1,0:T(8,128)(2,1)S(1)}, u32[]{:S(2)}, u32[]{:S(2)}) collective-permute-start(bf16[64,2048]{1,0:T(8,128)(2,1)S(1)} %get-tuple-element.83), channel_id=1, source_target_pairs={{0,1},{1,2},{2,3},{3,4},{4,5},{5,6},{6,7},{7,8},{8,9},{9,10},{10,1... | collective-permute-start | bytes 786440 | tf_op jit(solution)/shard_map/ppermute | solution.py:21
  7.3 3.5 %collective-permute-start = (bf16[64,2048]{1,0:T(8,128)(2,1)S(1)}, bf16[64,2048]{1,0:T(8,128)(2,1)S(1)}, u32[]{:S(2)}, u32[]{:S(2)}) collective-permute-start(bf16[64,2048]{1,0:T(8,128)(2,1)S(1)} %get-tuple-element.84), channel_id=1, source_target_pairs={{0,1},{1,2},{2,3},{3,4},{4,5},{5,6},{6,7},{7,8},{8,9},{9,10},{10,1... | collective-permute-start | bytes 786440 | tf_op jit(solution)/shard_map/ppermute | solution.py:21
  10.8 0.0 copy-done.3
  10.8 0.0 copy-done.4
  10.8 0.0 copy-done.5
  10.9 0.0 copy-done.6
  10.9 0.2 prepare.1
  11.1 1.2 %collective-permute-done.3.tap = bf16[64,2048]{1,0:T(8,128)(2,1)S(1)} collective-permute-done((bf16[64,2048]{1,0:T(8,128)(2,1)S(1)}, bf16[64,2048]{1,0:T(8,128)(2,1)S(1)}, u32[]{:S(2)}, u32[]{:S(2)}) %collective-permute-start.3) | collective-permute-done | bytes 262176 | tf_op jit(solution)/shard_map/ppermute | solution.py:21
  12.3 0.0 copy-done
  12.3 0.7 lower_forward.3
  13.0 0.0 copy-start.2
  13.0 5.5 %collective-permute-start.4 = (bf16[64,2048]{1,0:T(8,128)(2,1)S(1)}, bf16[64,2048]{1,0:T(8,128)(2,1)S(1)}, u32[]{:S(2)}, u32[]{:S(2)}) collective-permute-start(bf16[64,2048]{1,0:T(8,128)(2,1)S(1)} %get-tuple-element.51.mid.refs_0_), channel_id=1, source_target_pairs={{0,2},{1,3},{2,4},{3,5},{4,6},{5,7},{6,8},{7,9},{8,10},{9,11},{10,... | collective-permute-start | bytes 786440 | tf_op jit(solution)/shard_map/ppermute | solution.py:21
  18.5 0.0 collective-permute-done.tap
  18.5 0.7 lower_forward.2
  19.2 5.0 %collective-permute-start.1 = (bf16[64,2048]{1,0:T(8,128)(2,1)S(1)}, bf16[64,2048]{1,0:T(8,128)(2,1)S(1)}, u32[]{:S(2)}, u32[]{:S(2)}) collective-permute-start(bf16[64,2048]{1,0:T(8,128)(2,1)S(1)} %get-tuple-element.47.mid.refs_1_), channel_id=1, source_target_pairs={{0,2},{1,3},{2,4},{3,5},{4,6},{5,7},{6,8},{7,9},{8,10},{9,11},{10,... | collective-permute-start | bytes 786440 | tf_op jit(solution)/shard_map/ppermute | solution.py:21
  24.2 0.0 collective-permute-done.4.tap.refs_2_
  24.2 0.0 copy-done.1
  24.3 0.0 copy-done.2
  24.3 1.0 %upper_critical.3 = (bf16[128,2048]{1,0:T(8,128)(2,1)S(1)}, bf16[256,2048]{1,0:T(8,128)(2,1)S(1)}, bf16[64,2048]{1,0:T(8,128)(2,1)S(1)}) custom-call(bf16[64,2048]{1,0:T(8,128)(2,1)S(1)} %get-tuple-element.51.mid.refs_0_, bf16[64,2048]{1,0:T(8,128)(2,1)S(1)} %collective-permute-done.4.tap.refs_2_, bf16[1,64,4096]{2,1,0:T(8,128)(2,1)S(1)} %copy-done.1, ...), custom_call_target="tpu_custom_call" | custom-call | flops 266240000 | bytes 3743744 | tf_op jit(solution)/shard_map/upper_critical/pallas_call | solution.py:56
  25.3 1.3 %collective-permute-start.5 = (bf16[64,2048]{1,0:T(8,128)(2,1)S(1)}, bf16[64,2048]{1,0:T(8,128)(2,1)S(1)}, u32[]{:S(2)}, u32[]{:S(2)}) collective-permute-start(bf16[64,2048]{1,0:T(8,128)(2,1)S(1)} %get-tuple-element.56), channel_id=1, source_target_pairs={{2,0},{3,1},{4,2},{5,3},{6,4},{7,5},{8,6},{9,7},{10,8},{11,9},{12,... | collective-permute-start | bytes 786440 | tf_op jit(solution)/shard_map/ppermute | solution.py:21
  26.6 1.9 %collective-permute-done.1.tap.refs_3_ = bf16[64,2048]{1,0:T(8,128)(2,1)S(1)} collective-permute-done((bf16[64,2048]{1,0:T(8,128)(2,1)S(1)}, bf16[64,2048]{1,0:T(8,128)(2,1)S(1)}, u32[]{:S(2)}, u32[]{:S(2)}) %collective-permute-start.1) | collective-permute-done | bytes 262176 | tf_op jit(solution)/shard_map/ppermute | solution.py:21
  28.5 1.0 %upper_critical.2 = (bf16[128,2048]{1,0:T(8,128)(2,1)S(1)}, bf16[256,2048]{1,0:T(8,128)(2,1)S(1)}, bf16[64,2048]{1,0:T(8,128)(2,1)S(1)}) custom-call(bf16[64,2048]{1,0:T(8,128)(2,1)S(1)} %get-tuple-element.47.mid.refs_1_, bf16[64,2048]{1,0:T(8,128)(2,1)S(1)} %collective-permute-done.1.tap.refs_3_, bf16[1,64,4096]{2,1,0:T(8,128)(2,1)S(1)} %copy-done.1, ...), custom_call_target="tpu_custom_call" | custom-call | flops 266240000 | bytes 3743744 | tf_op jit(solution)/shard_map/upper_critical/pallas_call | solution.py:56
  29.5 1.3 %collective-permute-start.2 = (bf16[64,2048]{1,0:T(8,128)(2,1)S(1)}, bf16[64,2048]{1,0:T(8,128)(2,1)S(1)}, u32[]{:S(2)}, u32[]{:S(2)}) collective-permute-start(bf16[64,2048]{1,0:T(8,128)(2,1)S(1)} %get-tuple-element.50), channel_id=1, source_target_pairs={{2,0},{3,1},{4,2},{5,3},{6,4},{7,5},{8,6},{9,7},{10,8},{11,9},{12,... | collective-permute-start | bytes 786440 | tf_op jit(solution)/shard_map/ppermute | solution.py:21
  30.8 2.9 %collective-permute-done.5.gdel = bf16[64,2048]{1,0:T(8,128)(2,1)S(1)} collective-permute-done((bf16[64,2048]{1,0:T(8,128)(2,1)S(1)}, bf16[64,2048]{1,0:T(8,128)(2,1)S(1)}, u32[]{:S(2)}, u32[]{:S(2)}) %collective-permute-start.5) | collective-permute-done | bytes 262176 | tf_op jit(solution)/shard_map/ppermute | solution.py:21
  33.8 1.6 %lower_backward.2 = (bf16[64,2048]{1,0:T(8,128)(2,1)S(1)}, f32[64,2048]{1,0:T(8,128)S(1)}, f32[512,128]{1,0:T(8,128)S(1)}) custom-call(bf16[64,2048]{1,0:T(8,128)(2,1)S(1)} %collective-permute-done.5.gdel, bf16[256,2048]{1,0:T(8,128)(2,1)S(1)} %get-tuple-element.57.gpre1.refs_4_, bf16[1,64,4096]{2,1,0:T(8,128)(2,1)S(1)} %copy-done, ...), custom_call_target="tpu_custom_call" | custom-call | flops 655360000 | bytes 5054464 | tf_op jit(solution)/shard_map/lower_backward/pallas_call | solution.py:56
  35.3 1.1 %upper_sums.1.rest_2_ = f32[512,128]{1,0:T(8,128)S(1)} custom-call(bf16[64,2048]{1,0:T(8,128)(2,1)S(1)} %get-tuple-element.51.mid.refs_0_, bf16[64,2048]{1,0:T(8,128)(2,1)S(1)} %get-tuple-element.47.mid.refs_1_, bf16[64,2048]{1,0:T(8,128)(2,1)S(1)} %collective-permute-done.4.tap.refs_2_, bf16[64,2048]{1,0:T(8,128)(2,1)S(1)} %collective-permute-done.1.tap.refs_3_, ...), custom_call_target="tpu_custom_call" | custom-call | flops 409600000 | bytes 5505024 | tf_op jit(solution)/shard_map/upper_sums/pallas_call | solution.py:56
  36.4 1.5 %upper_outputs.1 = (bf16[1,64,4096]{2,1,0:T(8,128)(2,1)}, bf16[1,64,4096]{2,1,0:T(8,128)(2,1)}) custom-call(bf16[64,2048]{1,0:T(8,128)(2,1)S(1)} %get-tuple-element.51.mid.refs_0_, bf16[64,2048]{1,0:T(8,128)(2,1)S(1)} %get-tuple-element.47.mid.refs_1_, bf16[128,2048]{1,0:T(8,128)(2,1)S(1)} %get-tuple-element.52.z0.refs_2_, ...), custom_call_target="tpu_custom_call" | custom-call | flops 204800000 | bytes 3739648 | tf_op jit(solution)/shard_map/upper_outputs/pallas_call | solution.py:56
  37.9 1.7 %collective-permute-done.2.gdel = bf16[64,2048]{1,0:T(8,128)(2,1)S(1)} collective-permute-done((bf16[64,2048]{1,0:T(8,128)(2,1)S(1)}, bf16[64,2048]{1,0:T(8,128)(2,1)S(1)}, u32[]{:S(2)}, u32[]{:S(2)}) %collective-permute-start.2) | collective-permute-done | bytes 262176 | tf_op jit(solution)/shard_map/ppermute | solution.py:21
  39.6 1.8 %lower_backward.3 = (bf16[64,4096]{1,0:T(8,128)(2,1)S(1)}, f32[64,2048]{1,0:T(8,128)S(1)}, f32[512,128]{1,0:T(8,128)S(1)}, f32[512,128]{1,0:T(8,128)S(1)}) custom-call(bf16[64,2048]{1,0:T(8,128)(2,1)S(1)} %collective-permute-done.2.gdel, bf16[256,2048]{1,0:T(8,128)(2,1)S(1)} %get-tuple-element.61.refs_5_.gpre1, bf16[1,64,4096]{2,1,0:T(8,128)(2,1)S(1)} %copy-done, ...), custom_call_target="tpu_custom_call" | custom-call | flops 655360000 | bytes 6365184 | tf_op jit(solution)/shard_map/lower_backward/pallas_call | solution.py:56
  41.4 2.1 %collective-permute-start.6 = (f32[512,128]{1,0:T(8,128)S(1)}, f32[512,128]{1,0:T(8,128)S(1)}, u32[]{:S(2)}, u32[]{:S(2)}) collective-permute-start(f32[512,128]{1,0:T(8,128)S(1)} %get-tuple-element.75), channel_id=1, source_target_pairs={{0,16},{16,0},{1,17},{17,1},{2,18},{18,2},{3,19},{19,3},{4,20},{20... | collective-permute-start | bytes 786440 | tf_op jit(solution)/shard_map/ppermute | solution.py:218
  43.6 1.2 %collective-permute-done.6.y = f32[512,128]{1,0:T(8,128)S(1)} collective-permute-done((f32[512,128]{1,0:T(8,128)S(1)}, f32[512,128]{1,0:T(8,128)S(1)}, u32[]{:S(2)}, u32[]{:S(2)}) %collective-permute-start.6) | collective-permute-done | bytes 262176 | tf_op jit(solution)/shard_map/ppermute | solution.py:218
  44.7 0.7 add.1
  45.5 5.7 %all-to-all-start = ((f32[16,32,128]{2,1,0:T(8,128)}), f32[16,32,128]{2,1,0:T(8,128)S(1)}, u32[]{:S(2)}, u32[]{:S(2)}) async-start(f32[16,32,128]{2,1,0:T(8,128)} %bitcast.2), calls=%async_computation | async-start | bytes 524288 | tf_op jit(solution)/shard_map/all_to_all | solution.py:286
  51.2 1.3 %collective-permute-start.7 = (bf16[64,4096]{1,0:T(8,128)(2,1)S(1)}, bf16[64,4096]{1,0:T(8,128)(2,1)S(1)}, u32[]{:S(2)}, u32[]{:S(2)}) collective-permute-start(bf16[64,4096]{1,0:T(8,128)(2,1)S(1)} %get-tuple-element.77), channel_id=1, source_target_pairs={{1,0},{2,1},{3,2},{4,3},{5,4},{6,5},{7,6},{8,7},{9,8},{10,9},{11,1... | collective-permute-start | bytes 1572872 | tf_op jit(solution)/shard_map/ppermute | solution.py:21
  52.5 6.1 %all-to-all-done.parts = f32[16,32,128]{2,1,0:T(8,128)S(1)} async-done(((f32[16,32,128]{2,1,0:T(8,128)}), f32[16,32,128]{2,1,0:T(8,128)S(1)}, u32[]{:S(2)}, u32[]{:S(2)}) %all-to-all-start) | async-done | bytes 262176 | tf_op jit(solution)/shard_map/all_to_all | solution.py:286
  58.6 17.4 %all_to_all.15.parts = f32[8,32,128]{2,1,0:T(8,128)S(1)} all-to-all(f32[8,32,128]{2,1,0:T(8,128)S(1)} %share_out.2), channel_id=1, replica_groups=mesh['y'=4,'xl'=2,'core'=2,'z'=8,'xh'=2] {'z'}, dimensions={0} | all-to-all | bytes 262144 | tf_op jit(solution)/shard_map/all_to_all | solution.py:288
  76.0 10.3 %all_to_all.16 = bf16[16,32,128]{2,1,0:T(8,128)(2,1)S(1)} all-to-all(bf16[16,32,128]{2,1,0:T(8,128)(2,1)S(1)} %share_out.3), channel_id=1, replica_groups=mesh['y'=4,'xl'=2,'core'=2,'z'=8,'xh'=2] {'y','xl','xh'}, dimensions={0} | all-to-all | bytes 262144 | tf_op jit(solution)/shard_map/all_to_all | solution.py:290
  86.4 4.5 %collective-permute-start.8 = (bf16[512,128]{1,0:T(8,128)(2,1)S(1)}, bf16[512,128]{1,0:T(8,128)(2,1)S(1)}, u32[]{:S(2)}, u32[]{:S(2)}) collective-permute-start(bf16[512,128]{1,0:T(8,128)(2,1)S(1)} %bitcast.6), channel_id=1, source_target_pairs={{0,16},{16,0},{1,17},{17,1},{2,18},{18,2},{3,19},{19,3},{4,20},{20... | collective-permute-start | bytes 393224 | tf_op jit(solution)/shard_map/ppermute | solution.py:218
  90.8 0.0 collective-permute-done.7.refs_2_
  90.8 0.9 finish.1
  91.7 0.1 collective-permute-done.8.other
  91.8 0.8 place.1
  (3 shorter events, 0.0 us)
Async XLA Ops:
  0.6 11.6 %copy-start = (bf16[1,64,4096]{2,1,0:T(8,128)(2,1)S(1)}, bf16[1,64,4096]{2,1,0:T(8,128)(2,1)}, u32[]{:S(2)}) copy-start(bf16[1,64,4096]{2,1,0:T(8,128)(2,1)} %sig.7) | copy-start | bytes 1572868
  0.6 10.2 %copy-start.3 = (bf16[2,256,128]{2,1,0:T(8,128)(2,1)S(1)}, bf16[2,256,128]{2,1,0:T(8,128)(2,1)}, u32[]{:S(2)}) copy-start(bf16[2,256,128]{2,1,0:T(8,128)(2,1)} %w.13) | copy-start | bytes 393220
  0.7 10.2 %copy-start.4 = (bf16[2,128,128]{2,1,0:T(8,128)(2,1)S(1)}, bf16[2,128,128]{2,1,0:T(8,128)(2,1)}, u32[]{:S(2)}) copy-start(bf16[2,128,128]{2,1,0:T(8,128)(2,1)} %refs_6_.1) | copy-start | bytes 196612
  1.8 9.0 %copy-start.5 = (f32[2,256]{1,0:T(2,128)S(1)}, f32[2,256]{1,0:T(2,128)}, u32[]{:S(2)}) copy-start(f32[2,256]{1,0:T(2,128)} %b.1) | copy-start | bytes 6148
  1.8 9.0 %copy-start.6 = (f32[2,128]{1,0:T(2,128)S(1)}, f32[2,128]{1,0:T(2,128)}, u32[]{:S(2)}) copy-start(f32[2,128]{1,0:T(2,128)} %vb.1) | copy-start | bytes 3076
  1.8 10.4 %collective-permute-start.3 = (bf16[64,2048]{1,0:T(8,128)(2,1)S(1)}, bf16[64,2048]{1,0:T(8,128)(2,1)S(1)}, u32[]{:S(2)}, u32[]{:S(2)}) collective-permute-start(bf16[64,2048]{1,0:T(8,128)(2,1)S(1)} %get-tuple-element.83), channel_id=1, source_target_pairs={{0,1},{1,2},{2,3},{3,4},{4,5},{5,6},{6,7},{7,8},{8,9},{9,10},{10,1... | collective-permute-start | bytes 786440 | tf_op jit(solution)/shard_map/ppermute | solution.py:21
  7.3 11.2 %collective-permute-start = (bf16[64,2048]{1,0:T(8,128)(2,1)S(1)}, bf16[64,2048]{1,0:T(8,128)(2,1)S(1)}, u32[]{:S(2)}, u32[]{:S(2)}) collective-permute-start(bf16[64,2048]{1,0:T(8,128)(2,1)S(1)} %get-tuple-element.84), channel_id=1, source_target_pairs={{0,1},{1,2},{2,3},{3,4},{4,5},{5,6},{6,7},{7,8},{8,9},{9,10},{10,1... | collective-permute-start | bytes 786440 | tf_op jit(solution)/shard_map/ppermute | solution.py:21
  12.9 11.3 %copy-start.1 = (bf16[1,64,4096]{2,1,0:T(8,128)(2,1)S(1)}, bf16[1,64,4096]{2,1,0:T(8,128)(2,1)}, u32[]{:S(2)}) copy-start(bf16[1,64,4096]{2,1,0:T(8,128)(2,1)} %top.7) | copy-start | bytes 1572868
  13.0 11.3 %copy-start.2 = (bf16[1,64,4096]{2,1,0:T(8,128)(2,1)S(1)}, bf16[1,64,4096]{2,1,0:T(8,128)(2,1)}, u32[]{:S(2)}) copy-start(bf16[1,64,4096]{2,1,0:T(8,128)(2,1)} %skip.7) | copy-start | bytes 1572868
  13.0 11.3 %collective-permute-start.4 = (bf16[64,2048]{1,0:T(8,128)(2,1)S(1)}, bf16[64,2048]{1,0:T(8,128)(2,1)S(1)}, u32[]{:S(2)}, u32[]{:S(2)}) collective-permute-start(bf16[64,2048]{1,0:T(8,128)(2,1)S(1)} %get-tuple-element.51.mid.refs_0_), channel_id=1, source_target_pairs={{0,2},{1,3},{2,4},{3,5},{4,6},{5,7},{6,8},{7,9},{8,10},{9,11},{10,... | collective-permute-start | bytes 786440 | tf_op jit(solution)/shard_map/ppermute | solution.py:21
  19.2 9.3 %collective-permute-start.1 = (bf16[64,2048]{1,0:T(8,128)(2,1)S(1)}, bf16[64,2048]{1,0:T(8,128)(2,1)S(1)}, u32[]{:S(2)}, u32[]{:S(2)}) collective-permute-start(bf16[64,2048]{1,0:T(8,128)(2,1)S(1)} %get-tuple-element.47.mid.refs_1_), channel_id=1, source_target_pairs={{0,2},{1,3},{2,4},{3,5},{4,6},{5,7},{6,8},{7,9},{8,10},{9,11},{10,... | collective-permute-start | bytes 786440 | tf_op jit(solution)/shard_map/ppermute | solution.py:21
  25.3 8.5 %collective-permute-start.5 = (bf16[64,2048]{1,0:T(8,128)(2,1)S(1)}, bf16[64,2048]{1,0:T(8,128)(2,1)S(1)}, u32[]{:S(2)}, u32[]{:S(2)}) collective-permute-start(bf16[64,2048]{1,0:T(8,128)(2,1)S(1)} %get-tuple-element.56), channel_id=1, source_target_pairs={{2,0},{3,1},{4,2},{5,3},{6,4},{7,5},{8,6},{9,7},{10,8},{11,9},{12,... | collective-permute-start | bytes 786440 | tf_op jit(solution)/shard_map/ppermute | solution.py:21
  29.5 10.1 %collective-permute-start.2 = (bf16[64,2048]{1,0:T(8,128)(2,1)S(1)}, bf16[64,2048]{1,0:T(8,128)(2,1)S(1)}, u32[]{:S(2)}, u32[]{:S(2)}) collective-permute-start(bf16[64,2048]{1,0:T(8,128)(2,1)S(1)} %get-tuple-element.50), channel_id=1, source_target_pairs={{2,0},{3,1},{4,2},{5,3},{6,4},{7,5},{8,6},{9,7},{10,8},{11,9},{12,... | collective-permute-start | bytes 786440 | tf_op jit(solution)/shard_map/ppermute | solution.py:21
  41.4 3.3 %collective-permute-start.6 = (f32[512,128]{1,0:T(8,128)S(1)}, f32[512,128]{1,0:T(8,128)S(1)}, u32[]{:S(2)}, u32[]{:S(2)}) collective-permute-start(f32[512,128]{1,0:T(8,128)S(1)} %get-tuple-element.75), channel_id=1, source_target_pairs={{0,16},{16,0},{1,17},{17,1},{2,18},{18,2},{3,19},{19,3},{4,20},{20... | collective-permute-start | bytes 786440 | tf_op jit(solution)/shard_map/ppermute | solution.py:218
  45.5 13.1 %all-to-all-start = ((f32[16,32,128]{2,1,0:T(8,128)}), f32[16,32,128]{2,1,0:T(8,128)S(1)}, u32[]{:S(2)}, u32[]{:S(2)}) async-start(f32[16,32,128]{2,1,0:T(8,128)} %bitcast.2), calls=%async_computation | async-start | bytes 524288 | tf_op jit(solution)/shard_map/all_to_all | solution.py:286
  51.2 39.6 %collective-permute-start.7 = (bf16[64,4096]{1,0:T(8,128)(2,1)S(1)}, bf16[64,4096]{1,0:T(8,128)(2,1)S(1)}, u32[]{:S(2)}, u32[]{:S(2)}) collective-permute-start(bf16[64,4096]{1,0:T(8,128)(2,1)S(1)} %get-tuple-element.77), channel_id=1, source_target_pairs={{1,0},{2,1},{3,2},{4,3},{5,4},{6,5},{7,6},{8,7},{9,8},{10,9},{11,1... | collective-permute-start | bytes 1572872 | tf_op jit(solution)/shard_map/ppermute | solution.py:21
  86.4 5.4 %collective-permute-start.8 = (bf16[512,128]{1,0:T(8,128)(2,1)S(1)}, bf16[512,128]{1,0:T(8,128)(2,1)S(1)}, u32[]{:S(2)}, u32[]{:S(2)}) collective-permute-start(bf16[512,128]{1,0:T(8,128)(2,1)S(1)} %bitcast.6), channel_id=1, source_target_pairs={{0,16},{16,0},{1,17},{17,1},{2,18},{18,2},{3,19},{19,3},{4,20},{20... | collective-permute-start | bytes 393224 | tf_op jit(solution)/shard_map/ppermute | solution.py:218
